TPU v7x, 128 devices: a whole 4x4x4 slice. The times are simulated.
128 devices in a mesh: dp: 16 (over x_hi, y, core), ind: 8 (over x_lo, z).
Axes of the slice: x: 4 (x_hi: 2, x_lo: 2; x = x_hi * 2 + x_lo), y: 4, z: 4, core: 2. Of those that a mesh axis runs over, the one named last changes fastest.
Arguments:
- x_points: float32 [3, 32768], P(None, 'dp'), may hold values from 0 to 1
- z_points: float32 [3, 16384], P(None, 'ind'), may hold values from 0 to 1
- length_scales: float32 [3], replicated, may hold values from 0.35 to 0.7
- dpsi_grad: float32 [16384, 16384], P('dp', 'ind'), may hold values from -0.625 to 0.625
- block_rows: int32 [16, 8, 3], P('dp', 'ind'), may hold values from 0 to 7, as said below
- block_cols: int32 [16, 8, 3], P('dp', 'ind'), may hold values from 0 to 7, as said below
- block_count: int32 [16, 8], P('dp', 'ind'), may hold values from 1 to 3, as said below
Outputs:
- dk_blocks: float32 [16, 8, 3, 256, 256], P('dp', 'ind')
- z_grad: float32 [3, 16384], P(None, 'ind')
- scale_grad: float32 [3], replicated
Inputs may be any that keep to these rules, and one draw needn't show every extreme that they name: `block_rows`: within a tile the live slots lie in distinct row blocks, and the live slots of all tiles of one row group lie in at most 3 distinct row blocks; entries of unused slots carry no meaning. `block_cols`: entries of unused slots carry no meaning. `block_count`: some tile holds exactly 3 listed blocks in every draw.
All inputs are finite; a program needn't handle non-finite values.
Results may differ from a plain program's by a relative error of at most 0.0003.
Values sent between devices are 32-bit elements; how exact they have to be, the bound alone decides.
No kernel may reach another device: no remote copies, remote signals or barrier semaphores. Data moves between devices by JAX's collectives and lax.ppermute only.
A program may use at most 128 MiB of HBM per device.

v0:
```python
import jax
import jax.numpy as jnp
from jax import lax
from jax.sharding import PartitionSpec as P

M = 16384
BS = 256


def wendland(x_rows, z_cols, length_scales):
    dist_sq = jnp.zeros((x_rows.shape[1], z_cols.shape[1]), x_rows.dtype)
    for dim_q in range(x_rows.shape[0]):
        offset = (x_rows[dim_q][:, None] - z_cols[dim_q][None, :]) / length_scales[dim_q]
        dist_sq = dist_sq + offset * offset
    radius = jnp.sqrt(dist_sq)
    remain = jnp.maximum(1.0 - radius, 0.0)
    remain_cube = remain * remain * remain
    return (remain_cube * remain * (4.0 * radius + 1.0), -10.0 * remain_cube)


def on_device(x_points, z_points, length_scales, dpsi_grad, block_rows, block_cols, block_count):
    highest = lax.Precision.HIGHEST
    groups_dp = lax.axis_size("dp")
    groups_ind = lax.axis_size("ind")
    dp_index = lax.axis_index("dp")
    ind_index = lax.axis_index("ind")
    owner_ratio = groups_dp // groups_ind
    col_blocks = M // (BS * groups_ind)
    own_blocks = M // (BS * groups_dp)
    dim_count = x_points.shape[0]
    slot_count = block_rows.shape[2]
    row_count = x_points.shape[1] // BS
    slot_ids = jnp.arange(slot_count, dtype=jnp.int32)
    batched_kernel = jax.vmap(wendland, in_axes=(0, 0, None))
    all_rows, all_cols, all_count = (
        lax.all_gather(block_rows, ("dp", "ind"), axis=0, tiled=True),
        lax.all_gather(block_cols, ("dp", "ind"), axis=0, tiled=True),
        lax.all_gather(block_count, ("dp", "ind"), axis=0, tiled=True),
    )
    all_rows = all_rows.reshape(groups_dp, groups_ind, slot_count)
    all_cols = all_cols.reshape(groups_dp, groups_ind, slot_count)
    all_count = all_count.reshape(groups_dp, groups_ind)
    live_all = slot_ids[None, None, :] < all_count[:, :, None]
    z_all = lax.all_gather(z_points, "ind", axis=1, tiled=True)
    z_blocks = z_all.reshape(dim_count, M // BS, BS)
    own_rows = block_rows[0, 0]
    own_cols = block_cols[0, 0]
    own_live = (slot_ids < block_count[0, 0]).astype(jnp.float32)
    x_own = jnp.transpose(x_points.reshape(dim_count, row_count, BS)[:, own_rows, :], (1, 0, 2))
    my_group = dp_index // owner_ratio
    my_part = dp_index % owner_ratio
    dest_rows = all_rows[:, ind_index, :]
    dest_cols = all_cols[:, ind_index, :]
    source_rows = all_rows[:, my_group, :]
    source_cols = all_cols[:, my_group, :]
    source_live = live_all[:, my_group, :]
    matched = source_live[:, None, :] & (source_rows[:, None, :] == dest_rows[:, :, None])
    found_col = jnp.sum(jnp.where(matched, source_cols[:, None, :], 0), axis=2)
    keep_weight = (jnp.any(matched, axis=2) & (found_col // own_blocks == my_part)).astype(
        jnp.float32
    )
    row_start = (found_col - my_part * own_blocks) * BS
    col_start = dest_cols * BS

    def pick_tile(row_at, col_at, weight):
        return lax.dynamic_slice(dpsi_grad, (row_at, col_at), (BS, BS)) * weight

    outgoing = jax.vmap(pick_tile)(
        row_start.reshape(-1), col_start.reshape(-1), keep_weight.reshape(-1)
    )
    outgoing = outgoing.reshape(groups_dp, slot_count, BS, BS)
    received = lax.all_to_all(outgoing, "dp", split_axis=0, concat_axis=0, tiled=True)
    grouped = jnp.sum(received.reshape(groups_ind, owner_ratio, slot_count, BS, BS), axis=1)
    row_tiles = all_rows[dp_index]
    col_tiles = all_cols[dp_index]
    live_tiles = live_all[dp_index]
    near_match = live_tiles[None, :, :] & (row_tiles[None, :, :] == own_rows[:, None, None])
    near_weight = jnp.any(near_match, axis=2).astype(jnp.float32)
    near_local = jnp.sum(jnp.where(near_match, col_tiles[None, :, :], 0), axis=2)
    near_blocks = jnp.arange(groups_ind, dtype=jnp.int32)[None, :] * col_blocks + near_local
    z_near = jnp.transpose(z_blocks[:, near_blocks, :], (1, 0, 2, 3)).reshape(
        slot_count, dim_count, groups_ind * BS
    )
    kernel, _ = batched_kernel(x_own, z_near, length_scales)
    masked = kernel * jnp.repeat(near_weight, BS, axis=1)[:, None, :]
    dk_local = jnp.einsum(
        "spgk,gskc->spc", masked.reshape(slot_count, BS, groups_ind, BS), grouped, precision=highest
    )
    dk_local = dk_local * own_live[:, None, None]
    z_own = jnp.transpose(z_points.reshape(dim_count, col_blocks, BS)[:, own_cols, :], (1, 0, 2))
    _, slopes = batched_kernel(x_own, z_own, length_scales)
    grad_k = dk_local * slopes
    col_sum = jnp.sum(grad_k, axis=1)
    x_weighted = jnp.einsum("sqn,snm->sqm", x_own, grad_k, precision=highest)
    inverse_square = -2.0 / (length_scales * length_scales)
    z_parts = inverse_square[None, :, None] * (x_weighted - z_own * col_sum[:, None, :])
    scale_terms = []
    for dim_q in range(dim_count):
        offset = x_own[:, dim_q, :, None] - z_own[:, dim_q, None, :]
        scale_terms.append(jnp.sum(grad_k * offset * offset, axis=(1, 2)))
    cube_scale = length_scales * length_scales * length_scales
    scale_parts = (-2.0 / cube_scale)[None, :] * jnp.stack(scale_terms, axis=1)
    onehot = (own_cols[:, None] == jnp.arange(col_blocks, dtype=jnp.int32)[None, :]).astype(
        jnp.float32
    )
    z_local = jnp.einsum("tc,tqb->qcb", onehot, z_parts, precision=highest).reshape(
        dim_count, col_blocks * BS
    )
    scale_local = jnp.sum(scale_parts, axis=0)
    z_grad = lax.psum(z_local, "dp")
    scale_grad = lax.psum(scale_local, ("dp", "ind"))
    return (dk_local.reshape(1, 1, slot_count, BS, BS), z_grad, scale_grad)


def solution(mesh):
    return jax.shard_map(
        on_device,
        mesh=mesh,
        in_specs=(
            P(None, "dp"),
            P(None, "ind"),
            P(),
            P("dp", "ind"),
            P("dp", "ind", None),
            P("dp", "ind", None),
            P("dp", "ind"),
        ),
        out_specs=(P("dp", "ind", None, None, None), P(None, "ind"), P()),
        check_vma=False,
    )
```

profile of v0, /device:TPU:0, one launch (start us, length us, event | category | flops | bytes accessed | tf_op | source)
XLA Modules:
  0.0 1267.7 jit_solution(14289409882634302694)
XLA Ops:
  1.4 68.2 %all-reduce = s32[128]{0:T(128)S(1)} all-reduce(s32[128]{0:T(128)S(1)} %bitcast_dynamic-update-slice_fusion.1), channel_id=1, replica_groups=mesh['dp'=16,'ind'=8] {'dp','ind'}, use_global_device_ids=true, to_apply=%add | all-reduce | flops 128 | bytes 1024
  69.8 312.4 %all_gather.14 = s32[128,1,3]{2,1,0:T(1,128)S(1)} all-gather(s32[1,1,3]{2,1,0:T(1,128)} %param.11), channel_id=1, replica_groups=mesh['dp'=16,'ind'=8] {'dp','ind'}, dimensions={0}, use_global_device_ids=true | all-gather | bytes 1548 | tf_op jit(solution)/shard_map/all_gather | solution.py:36
  382.3 310.6 %all_gather.15 = s32[128,1,3]{2,1,0:T(1,128)S(1)} all-gather(s32[1,1,3]{2,1,0:T(1,128)} %param.12), channel_id=1, replica_groups=mesh['dp'=16,'ind'=8] {'dp','ind'}, dimensions={0}, use_global_device_ids=true | all-gather | bytes 1548 | tf_op jit(solution)/shard_map/all_gather | solution.py:37
  693.5 184.9 %while.1 = (s32[]{:T(128)}, f32[1024,2048]{1,0:T(8,128)}, s32[48,2]{0,1:T(2,128)S(1)}, f32[48,256,256]{2,1,0:T(8,128)}, s32[]{:T(128)}) while((s32[]{:T(128)}, f32[1024,2048]{1,0:T(8,128)}, s32[48,2]{0,1:T(2,128)S(1)}, f32[48,256,256]{2,1,0:T(8,128)}, s32[]{:T(128)}) %tuple.44), condition=%wide.while_cond, body=%wide.while_body.sunk | while | flops 2 | bytes 525421 | solution.py:66
  694.2 3.2 bitcast_dynamic-update-slice_fusion.3
  698.0 3.2 bitcast_dynamic-update-slice_fusion.3
  701.9 3.2 bitcast_dynamic-update-slice_fusion.3
  705.8 3.2 bitcast_dynamic-update-slice_fusion.3
  717.3 3.2 bitcast_dynamic-update-slice_fusion.3
  721.1 3.2 bitcast_dynamic-update-slice_fusion.3
  725.0 3.2 bitcast_dynamic-update-slice_fusion.3
  728.9 3.2 bitcast_dynamic-update-slice_fusion.3
  732.7 3.2 bitcast_dynamic-update-slice_fusion.3
  736.6 3.2 bitcast_dynamic-update-slice_fusion.3
  740.5 3.2 bitcast_dynamic-update-slice_fusion.3
  744.3 3.2 bitcast_dynamic-update-slice_fusion.3
  755.8 3.2 bitcast_dynamic-update-slice_fusion.3
  759.6 3.2 bitcast_dynamic-update-slice_fusion.3
  763.5 3.2 bitcast_dynamic-update-slice_fusion.3
  767.4 3.2 bitcast_dynamic-update-slice_fusion.3
  771.2 3.2 bitcast_dynamic-update-slice_fusion.3
  775.1 3.2 bitcast_dynamic-update-slice_fusion.3
  779.0 3.2 bitcast_dynamic-update-slice_fusion.3
  782.8 3.2 bitcast_dynamic-update-slice_fusion.3
  786.7 3.2 bitcast_dynamic-update-slice_fusion.3
  790.6 3.2 bitcast_dynamic-update-slice_fusion.3
  794.4 3.2 bitcast_dynamic-update-slice_fusion.3
  798.3 3.2 bitcast_dynamic-update-slice_fusion.3
  802.2 3.2 bitcast_dynamic-update-slice_fusion.3
  806.0 3.2 bitcast_dynamic-update-slice_fusion.3
  809.9 3.2 bitcast_dynamic-update-slice_fusion.3
  825.2 3.2 bitcast_dynamic-update-slice_fusion.3
  829.0 3.2 bitcast_dynamic-update-slice_fusion.3
  832.9 3.2 bitcast_dynamic-update-slice_fusion.3
  836.8 3.2 bitcast_dynamic-update-slice_fusion.3
  848.3 3.2 bitcast_dynamic-update-slice_fusion.3
  852.1 3.2 bitcast_dynamic-update-slice_fusion.3
  856.0 3.2 bitcast_dynamic-update-slice_fusion.3
  859.9 3.2 bitcast_dynamic-update-slice_fusion.3
  863.7 3.2 bitcast_dynamic-update-slice_fusion.3
  871.4 3.2 bitcast_dynamic-update-slice_fusion.3
  878.4 11.3 broadcast_multiply_fusion
  889.8 5.1 all-to-all-start
  895.6 207.9 %all_gather.12 = f32[3,16384]{1,0:T(4,128)S(1)} all-gather(f32[3,2048]{1,0:T(4,128)S(1)} %copy-done.1), channel_id=1, replica_groups=mesh['dp'=16,'ind'=8] {'ind'}, dimensions={1}, use_global_device_ids=true | all-gather | bytes 221184 | tf_op jit(solution)/shard_map/all_gather | solution.py:44
  1106.2 6.6 bitcast_reduce_fusion
  1112.8 14.7 %fusion.55 = (f32[3]{0:T(128)S(1)}, f32[3]{0:T(128)S(1)}, f32[3]{0:T(128)S(1)}, f32[3,256]{1,0:T(4,128)S(1)}, f32[3,256,256]{2,1,0:T(8,128)}, /*index=5*/f32[3,256,256]{2,1,0:T(8,128)}) fusion(f32[3,256]{1,0:T(4,128)S(1)} %get-tuple-element.53, f32[3,256]{1,0:T(4,128)S(1)} %get-tuple-element.54, f32[3,256]{1,0:T(4,128)S(1)} %get-tuple-element.47, ...), kind=kOutput, calls=%fused_computation.66 | convolution fusion | flops 4868799488 | bytes 7959708 | tf_op jit(solution)/shard_map/spgk,gskc->spc/dot_general | solution.py:86
  1127.6 69.2 %psum.15 = f32[3]{0:T(128)} all-reduce(f32[3]{0:T(128)S(1)} %fusion.63), channel_id=1, replica_groups=mesh['dp'=16,'ind'=8] {'dp','ind'}, use_global_device_ids=true, to_apply=%region_11.12 | all-reduce | flops 3 | bytes 24 | tf_op jit(solution)/shard_map/psum | solution.py:111
  1198.7 69.0 %psum.14 = f32[3,2048]{1,0:T(4,128)} all-reduce(f32[3,2048]{1,0:T(4,128)S(1)} %bitcast.111), channel_id=1, replica_groups=mesh['dp'=16,'ind'=8] {'dp'}, use_global_device_ids=true, to_apply=%region_6.7 | all-reduce | flops 6144 | bytes 49152 | tf_op jit(solution)/shard_map/psum | solution.py:110
  (178 shorter events, 72.9 us)
Async XLA Ops:
  0.6 1103.7 %copy-start = (f32[3,2048]{1,0:T(4,128)S(1)}, f32[3,2048]{1,0:T(4,128)}, u32[]{:S(2)}) copy-start(f32[3,2048]{1,0:T(4,128)} %param.7) | copy-start | bytes 73732
  889.8 5.5 copy-start.2
  889.8 5.8 copy-start.1
  889.8 215.1 %copy-start.4 = (s32[1,1,3]{2,1,0:T(1,128)S(1)}, s32[1,1,3]{2,1,0:T(1,128)}, u32[]{:S(2)}) copy-start(s32[1,1,3]{2,1,0:T(1,128)} %param.12) | copy-start | bytes 40
  889.8 215.7 %copy-start.3 = (f32[3]{0:T(128)S(1)}, f32[3]{0:T(128)}, u32[]{:S(2)}) copy-start(f32[3]{0:T(128)} %param.9) | copy-start | bytes 40
  889.8 216.4 %all-to-all-start = ((f32[16,3,256,256]{3,2,1,0:T(8,128)}), f32[16,3,256,256]{3,2,1,0:T(8,128)}, u32[]{:S(2)}, u32[]{:S(2)}) async-start(f32[16,3,256,256]{3,2,1,0:T(8,128)} %broadcast_multiply_fusion), calls=%async_computation | async-start | bytes 25165824 | tf_op jit(solution)/shard_map/all_to_all | solution.py:72
where the time goes:
time: 1270 us
  blocking collectives  1040 us (82%)
  local copies, waits for them, and re-layouts  189 us (15%)
  other arithmetic  18.5 us (1%)
  matrix products  16.6 us (1%)
    all_gather x1, blocking collectives, on_device(): lax.all_gather(block_rows, ('dp', 'ind'), axis=0, tiled=True)  312 us
    all_gather x1, blocking collectives, on_device(): lax.all_gather(block_cols, ('dp', 'ind'), axis=0, tiled=True)  311 us
    all_gather x1, blocking collectives, on_device(): z_all = lax.all_gather(z_points, 'ind', axis=1, tiled=True)  208 us
    gather x144, local copies, waits for them, and re-layouts  185 us
    psum x1, blocking collectives, on_device(): scale_grad = lax.psum(scale_local, ('dp', 'ind'))  69.2 us
    psum x1, blocking collectives, on_device(): z_grad = lax.psum(z_local, 'dp')  69 us
    unnamed x1, blocking collectives  68.2 us
  transfers between devices with their start and end apart: 1, of which 0 were waited for; matrix products, arithmetic and copies ran while one was open for 0% of the time, Pallas kernels for 0%

commit v1 on v0

v1 whole, which is shorter than its diff:
```python
import itertools

import jax
import jax.numpy as jnp
from jax import lax
from jax.experimental import pallas as pl
from jax.experimental.pallas import tpu as pltpu
from jax.sharding import Mesh, PartitionSpec as P

BS = 256
SLOTS = 3
AXES = ("xh", "y", "c", "xl", "z")
SIZES = (2, 4, 2, 2, 4)
DP = ("xh", "y", "c")
IND = ("xl", "z")


def pairs(target):
    def flat(place):
        index = 0
        for size, coord in zip(SIZES, place):
            index = index * size + coord
        return index

    places = itertools.product(*(range(size) for size in SIZES))
    return [(flat(place), flat(target(*place))) for place in places]


def shift_y(step):
    return pairs(lambda xh, y, c, xl, z: (xh, (y + step) % 4, c, xl, z))


SWAP_CORE = pairs(lambda xh, y, c, xl, z: (xh, y, 1 - c, xl, z))
SWAP_XH = pairs(lambda xh, y, c, xl, z: (1 - xh, y, c, xl, z))
Y_UP = shift_y(1)
Y_DOWN = shift_y(3)


def transpose_place(xh, y, c, xl, z):
    row = (xh * 4 + y) * 2 + c
    col = xl * 4 + z
    owner, new_col = 2 * col + row % 2, row // 2
    return (owner // 8, owner // 2 % 4, owner % 2, new_col // 4, new_col % 4)


TRANSPOSE = pairs(transpose_place)


def permute(value, perm):
    return lax.ppermute(value, AXES, perm)


def payload_kernel(rows_ref, cols_ref, count_ref, x_ref, out_ref, pack_ref):
    lane = lax.broadcasted_iota(jnp.int32, (1, BS), 1)
    pack_ref[...] = jnp.zeros_like(pack_ref)
    for slot in range(SLOTS):
        live = jnp.where(count_ref[0] > slot, 1, 0)
        row = rows_ref[slot] * live
        col = cols_ref[slot] * live
        start = pl.multiple_of(row * BS, BS)
        pack_ref[4 * slot : 4 * slot + 3, :] = x_ref[:, pl.ds(start, BS)]
        info = jnp.where(lane == 0, row, jnp.where(lane == 1, col, jnp.where(lane == 2, live, 0)))
        pack_ref[4 * slot + 3 : 4 * slot + 4, :] = info.astype(jnp.float32)
    packed = pack_ref[...]
    for dest in range(out_ref.shape[0]):
        out_ref[dest] = packed


def slot_of(place, step, own_ref, near_ref, pos_ref):
    own_x = place // SLOTS
    slot = place % SLOTS
    xh = jnp.where(own_x == 1, pos_ref[0], 1 - pos_ref[0])
    group = xh * 8 + lax.rem(pos_ref[1] + step, 4) * 2 + pos_ref[2]
    base = group * 9
    row = own_ref[base + 3 * slot]
    col = own_ref[base + 3 * slot + 1]
    live = own_ref[base + 3 * slot + 2]
    near = 0
    found = 0
    for other in range(SLOTS):
        match = jnp.where(near_ref[base + 3 * other] == row, near_ref[base + 3 * other + 2], 0)
        near = near + match * near_ref[base + 3 * other + 1]
        found = found + match
    return group, slot, col, near, (live * found) > 0


def column_of(pay_ref, group, slot):
    rolled = pltpu.roll(pay_ref[group], lax.rem(16 - 4 * slot, 16), 0)
    padded = jnp.concatenate([rolled[0:8], jnp.zeros((120, BS), jnp.float32)], axis=0)
    return jnp.transpose(padded)


def split(value):
    high = value.astype(jnp.bfloat16)
    return high, (value - high.astype(jnp.float32)).astype(jnp.bfloat16)


def product_kernel(steps, own_ref, near_ref, pos_ref, scale_ref, pay_ref, z_ref, mine_ref, mate_ref,
                   out_ref, tiles, results, in_sems, out_sems):
    count = 2 * SLOTS

    def copy_in(source, row, col, place):
        window = source.at[pl.ds(row * BS, BS), pl.ds(col * BS, BS)]
        return pltpu.make_async_copy(window, tiles.at[place], in_sems.at[place])

    for number, step in enumerate(steps):
        for local in range(count):
            place = number * count + local
            _, _, col, near, active = slot_of(local, step, own_ref, near_ref, pos_ref)
            mine = (near // 4) == pos_ref[2]
            row = lax.rem(near, 4)

            @pl.when(jnp.logical_and(active, mine))
            def _():
                copy_in(mine_ref, row, col, place).start()

            @pl.when(jnp.logical_and(active, jnp.logical_not(mine)))
            def _():
                copy_in(mate_ref, row, col, place).start()

    for number, step in enumerate(steps):

        def body(local, carry):
            place = number * count + local
            group, slot, col, near, active = slot_of(local, step, own_ref, near_ref, pos_ref)

            @pl.when(active)
            def _():
                x_cols = column_of(pay_ref, group, slot)
                z_rows = z_ref[:, pl.ds(pl.multiple_of(near * BS, BS), BS)]
                dist = jnp.zeros((BS, BS), jnp.float32)
                for q in range(3):
                    offset = (x_cols[:, q : q + 1] - z_rows[q : q + 1, :]) * (1.0 / scale_ref[q])
                    dist = dist + offset * offset
                radius = jnp.sqrt(dist)
                remain = jnp.maximum(1.0 - radius, 0.0)
                square = remain * remain
                kernel = square * square * (4.0 * radius + 1.0)
                copy_in(mine_ref, 0, 0, place).wait()
                k_high, k_low = split(kernel)
                d_high, d_low = split(tiles[place])
                total = jnp.dot(k_high, d_low, preferred_element_type=jnp.float32)
                total = total + jnp.dot(k_low, d_high, preferred_element_type=jnp.float32)
                results[place] = total + jnp.dot(k_high, d_high, preferred_element_type=jnp.float32)

            @pl.when(jnp.logical_not(active))
            def _():
                results[place] = jnp.zeros((BS, BS), jnp.float32)

            pltpu.make_async_copy(results.at[place], out_ref.at[place], out_sems.at[place]).start()
            return carry

        lax.fori_loop(0, count, body, 0)

    for place in range(count * len(steps)):
        pltpu.make_async_copy(results.at[place], out_ref.at[place], out_sems.at[place]).wait()


def products(steps, tables, scales, payload, z_near, mine, mate):
    number = 2 * SLOTS * len(steps)
    smem = pl.BlockSpec(memory_space=pltpu.SMEM)
    vmem = pl.BlockSpec(memory_space=pltpu.VMEM)
    hbm = pl.BlockSpec(memory_space=pl.ANY)

    def kernel(*refs):
        product_kernel(steps, *refs)

    return pl.pallas_call(
        kernel,
        out_shape=jax.ShapeDtypeStruct((number, BS, BS), jnp.float32),
        in_specs=[smem, smem, smem, smem, vmem, vmem, hbm, hbm],
        out_specs=hbm,
        scratch_shapes=[
            pltpu.VMEM((number, BS, BS), jnp.float32),
            pltpu.VMEM((number, BS, BS), jnp.float32),
            pltpu.SemaphoreType.DMA((number,)),
            pltpu.SemaphoreType.DMA((number,)),
        ],
        name="products",
    )(*tables, scales, payload, z_near, mine, mate)


def gradient_kernel(plan, own_ref, near_ref, pos_ref, scale_ref, pay_ref, z_ref, *refs):
    parts, out_ref = refs[:-1], refs[-1]
    out_ref[...] = jnp.zeros_like(out_ref)
    count = 2 * SLOTS
    for part, steps in zip(parts, plan):
        for number, step in enumerate(steps):

            def body(local, carry):
                group, slot, col, near, active = slot_of(local, step, own_ref, near_ref, pos_ref)

                @pl.when(active)
                def _():
                    x_cols = column_of(pay_ref, group, slot)
                    start = pl.multiple_of(col * BS, BS)
                    z_rows = z_ref[:, pl.ds(start, BS)]
                    dist = jnp.zeros((BS, BS), jnp.float32)
                    offsets = []
                    for q in range(3):
                        offset = (x_cols[:, q : q + 1] - z_rows[q : q + 1, :]) * (1.0 / scale_ref[q])
                        offsets.append(offset)
                        dist = dist + offset * offset
                    remain = jnp.maximum(1.0 - jnp.sqrt(dist), 0.0)
                    grad = part[number * count + local] * (remain * remain * remain)
                    z_sums, scale_sums = [], []
                    for q in range(3):
                        weighted = grad * offsets[q]
                        factor = 20.0 / scale_ref[q]
                        z_sums.append(factor * jnp.sum(weighted, axis=0, keepdims=True))
                        scale_sums.append(factor * jnp.sum(weighted * offsets[q], axis=0, keepdims=True))
                    for q in range(3):
                        out_ref[q : q + 1, pl.ds(start, BS)] += z_sums[q]
                        out_ref[3:4, q * BS : (q + 1) * BS] += scale_sums[q]

                return carry

            lax.fori_loop(0, count, body, 0)


def gradients(plan, tables, scales, payload, z_own, parts):
    smem = pl.BlockSpec(memory_space=pltpu.SMEM)
    vmem = pl.BlockSpec(memory_space=pltpu.VMEM)

    def kernel(*refs):
        gradient_kernel(plan, *refs)

    return pl.pallas_call(
        kernel,
        out_shape=jax.ShapeDtypeStruct((4, z_own.shape[1]), jnp.float32),
        in_specs=[smem, smem, smem, smem, vmem, vmem] + [vmem] * len(parts),
        out_specs=vmem,
        name="gradients",
    )(*tables, scales, payload, z_own, *parts)


def on_device(x_points, z_points, length_scales, dpsi_grad, block_rows, block_cols, block_count):
    smem = pl.BlockSpec(memory_space=pltpu.SMEM)
    vmem = pl.BlockSpec(memory_space=pltpu.VMEM)
    xh, y, core = (lax.axis_index(name).astype(jnp.int32) for name in DP)
    mate = permute(dpsi_grad, SWAP_CORE)
    z_near = permute(z_points, TRANSPOSE)
    outgoing = pl.pallas_call(
        payload_kernel,
        out_shape=jax.ShapeDtypeStruct((16, 16, BS), jnp.float32),
        in_specs=[smem, smem, smem, vmem],
        out_specs=vmem,
        scratch_shapes=[pltpu.VMEM((16, BS), jnp.float32)],
        name="payload",
    )(block_rows.reshape(-1), block_cols.reshape(-1), block_count.reshape(-1), x_points)
    payload = lax.all_to_all(outgoing, DP, 0, 0, tiled=True)
    own_table = jnp.stack([payload[:, 4 * s + 3, :3] for s in range(SLOTS)], axis=1).reshape(16, 9)
    own_table = own_table.astype(jnp.int32)
    near_table = permute(own_table, TRANSPOSE)
    tables = (own_table.reshape(-1), near_table.reshape(-1), jnp.stack([xh, y, core]))

    plan = ((2,), (1, 3), (0,))
    args = (tables, length_scales, payload, z_near, dpsi_grad, mate)
    far = products(plan[0], *args)
    sides = products(plan[1], *args)
    here = products(plan[2], *args)

    half = BS // 2
    s3 = SLOTS
    far_o, far_w = far[:s3], far[s3:]
    up_o, up_w, down_o, down_w = (sides[k * s3 : (k + 1) * s3] for k in range(4))
    got_up_o = permute(far_o[:, :half], Y_UP)
    got_down_o = permute(far_o[:, half:], Y_DOWN)
    got_up_w = permute(far_w[:, :half], Y_UP)
    got_down_w = permute(far_w[:, half:], Y_DOWN)
    up_o = up_o.at[:, :half].add(got_up_o)
    down_o = down_o.at[:, half:].add(got_down_o)
    up_w = up_w.at[:, :half].add(got_up_w)
    down_w = down_w.at[:, half:].add(got_down_w)
    sum_o = here[:s3] + permute(up_o, Y_UP) + permute(down_o, Y_DOWN)
    got_x = permute(sum_o, SWAP_XH)
    sum_w = here[s3:] + permute(up_w, Y_UP) + permute(down_w, Y_DOWN)
    live = jnp.arange(s3, dtype=jnp.int32) < block_count[0, 0]
    dk_local = jnp.where(live[:, None, None], sum_w + got_x, 0.0)

    local = gradients(plan, tables, length_scales, payload, z_points, (far, sides, here))
    width = local.shape[1] // 16
    scale_part = jnp.sum(local[3, : 3 * BS].reshape(3, BS), axis=1)
    chunks = local[:3].reshape(3, 16, width).transpose(1, 0, 2)
    scale_row = jnp.broadcast_to(jnp.pad(scale_part, (0, width - 3))[None, None, :], (16, 1, width))
    chunks = jnp.concatenate([chunks, scale_row], axis=1)
    summed = jnp.sum(lax.all_to_all(chunks, DP, 0, 0, tiled=True), axis=0)
    spread = lax.all_to_all(jnp.broadcast_to(summed[None], (16, 4, width)), DP, 0, 0, tiled=True)
    z_grad = spread[:, :3].transpose(1, 0, 2).reshape(3, 16 * width)
    by_col = lax.all_to_all(jnp.broadcast_to(summed[3:4], (8, width)), IND, 0, 0, tiled=True)
    scale_grad = jnp.sum(by_col[:, :3], axis=0)
    return dk_local.reshape(1, 1, s3, BS, BS), z_grad, scale_grad


def solution(mesh):
    fine = Mesh(mesh.devices.reshape(SIZES), AXES)
    return jax.shard_map(
        on_device,
        mesh=fine,
        in_specs=(
            P(None, DP),
            P(None, IND),
            P(),
            P(DP, IND),
            P(DP, IND, None),
            P(DP, IND, None),
            P(DP, IND),
        ),
        out_specs=(P(DP, IND, None, None, None), P(None, IND), P()),
        check_vma=False,
    )
```

time: 1270 us -> 140 us (0.11)
  blocking collectives: 1040 us -> 10.2 us
  local copies, waits for them, and re-layouts: 189 us -> 11.4 us
  starting transfers between devices: 5.12 us -> 40.7 us
  Pallas kernels: 0 us -> 34 us
  waiting for transfers between devices: 0.01 us -> 31.7 us
  matrix products: 16.6 us -> 0 us
    all_gather x3 -> x0, blocking collectives: 831 us -> none  [the longest x1 312 us: on_device(): lax.all_gather(block_rows, ('dp', 'ind'), axis=0, tiled=True)]
    gather x147 -> x0, local copies, waits for them, and re-layouts: 187 us -> none
    psum x2 -> x0, blocking collectives: 138 us -> none  [the longest x1 69.2 us: on_device(): scale_grad = lax.psum(scale_local, ('dp', 'ind'))]
    unnamed x1 -> x0, blocking collectives: 68.2 us -> none
    pallas_call x0 -> x5, Pallas kernels: none -> 34 us  [the longest x3 19.6 us: products(): pl.pallas_call(kernel, out_shape=jax.ShapeDtypeStruct((number, BS, BS), j...]
    all_to_all x1 -> x3, waiting for transfers between devices: 0.01 us -> 30.5 us  [the longest x1 15.3 us: on_device(): lax.all_to_all(jnp.broadcast_to(summed[3:4], (8, width)), IND, 0, 0, tile...]
    ppermute x0 -> x12, starting transfers between devices: none -> 20.2 us  [permute(): return lax.ppermute(value, AXES, perm)]
    dot_general x3 -> x0, matrix products: 16.6 us -> none  [the longest x1 14.7 us: on_device(): jnp.einsum('spgk,gskc->spc', masked.reshape(slot_count, BS, groups_ind, B...]
  transfers between devices with their start and end apart: 1 -> 15, of which waited for: 0 -> 5; matrix products, arithmetic and copies ran while one was open for 0% -> 9% of each run, Pallas kernels for 0% -> 21%
where the time goes in v1:
time: 140 us; the launch traced here: 138 us
  starting transfers between devices  40.7 us (29%)
  Pallas kernels  34 us (24%)
  waiting for transfers between devices  31.7 us (23%)
  local copies, waits for them, and re-layouts  11.4 us (8%)
  blocking collectives  10.2 us (7%)
  other arithmetic  8.36 us (6%)
  between operations  1.41 us (1%)
    ppermute x12, starting transfers between devices, permute(): return lax.ppermute(value, AXES, perm)  20.2 us
    pallas_call x3, Pallas kernels, products(): pl.pallas_call(kernel, out_shape=jax.ShapeDtypeStruct((number, BS, BS), j...  19.6 us
    all_to_all x1, waiting for transfers between devices, on_device(): lax.all_to_all(jnp.broadcast_to(summed[3:4], (8, width)), IND, 0, 0, tile...  15.3 us
    pallas_call x1, Pallas kernels, gradients(): pl.pallas_call(kernel, out_shape=jax.ShapeDtypeStruct((4, z_own.shape[1])...  12.9 us
    all_to_all x1, blocking collectives, on_device(): summed = jnp.sum(lax.all_to_all(chunks, DP, 0, 0, tiled=True), axis=0)  10.2 us
    all_to_all x1, starting transfers between devices, on_device(): lax.all_to_all(jnp.broadcast_to(summed[3:4], (8, width)), IND, 0, 0, tile...  8.33 us
    all_to_all x1, waiting for transfers between devices, on_device(): payload = lax.all_to_all(outgoing, DP, 0, 0, tiled=True)  8.1 us
    all_to_all x1, starting transfers between devices, on_device(): payload = lax.all_to_all(outgoing, DP, 0, 0, tiled=True)  7.25 us
  transfers between devices with their start and end apart: 15, of which 5 were waited for; matrix products, arithmetic and copies ran while one was open for 9% of the time, Pallas kernels for 21%

profile of v1, /device:TPU:0, one launch (start us, length us, event | category | flops | bytes accessed | tf_op | source)
XLA Modules:
  0.0 137.7 jit_solution(9095454920227228137)
XLA Ops:
  0.6 0.1 collective-permute-start.2
  1.4 1.5 %payload.1 = f32[16,16,256]{2,1,0:T(8,128)} custom-call(s32[3]{0:T(128)} %bitcast.25, s32[3]{0:T(128)} %bitcast.26, s32[1]{0:T(128)} %bitcast.23.count_ref, f32[3,2048]{1,0:T(4,128)} %x_ref.1), custom_call_target="tpu_custom_call" | custom-call | tf_op jit(solution)/shard_map/payload/pallas_call | solution.py:243
  2.9 7.3 %all-to-all-start = ((f32[16,16,256]{2,1,0:T(8,128)}), f32[16,16,256]{2,1,0:T(8,128)S(1)}, u32[]{:S(2)}, u32[]{:S(2)}) async-start(f32[16,16,256]{2,1,0:T(8,128)} %payload.1), calls=%async_computation | async-start | bytes 524288 | tf_op jit(solution)/shard_map/all_to_all | solution.py:251
  10.1 1.4 %collective-permute-start.1 = (f32[3,2048]{1,0:T(4,128)}, f32[3,2048]{1,0:T(4,128)S(1)}, u32[]{:S(2)}, u32[]{:S(2)}) collective-permute-start(f32[3,2048]{1,0:T(4,128)} %refs_5_.1), channel_id=1, source_target_pairs={{0,0},{1,16},{2,32},{3,48},{4,64},{5,80},{6,96},{7,112},{8,8},{9,2... | collective-permute-start | bytes 73736 | tf_op jit(solution)/shard_map/ppermute | solution.py:50
  11.6 8.1 %all-to-all-done.refs_4_ = f32[16,16,256]{2,1,0:T(8,128)S(1)} async-done(((f32[16,16,256]{2,1,0:T(8,128)}), f32[16,16,256]{2,1,0:T(8,128)S(1)}, u32[]{:S(2)}, u32[]{:S(2)}) %all-to-all-start) | async-done | bytes 262176 | tf_op jit(solution)/shard_map/all_to_all | solution.py:251
  19.7 0.1 copy.25
  19.8 0.1 copy.27
  19.8 0.1 copy.26
  20.0 0.7 collective-permute-start
  20.6 0.7 pad_add_fusion.refs_2_
  21.3 0.1 copy.28
  21.4 0.7 convert_element_type.13.refs_0_
  22.1 0.0 collective-permute-done
  22.1 0.1 copy.29
  22.2 0.7 reshape.165.refs_1_
  22.9 0.6 copy-done.4
  23.5 5.4 %products.5.refs_6_ = f32[6,256,256]{2,1,0:T(8,128)} custom-call(s32[144]{0:T(256)} %convert_element_type.13.refs_0_, s32[144]{0:T(256)} %reshape.165.refs_1_, s32[3]{0:T(128)} %pad_add_fusion.refs_2_, f32[3]{0:T(128)} %refs_3_.7, f32[16,16,256]{2,1,0:T(8,128)} %copy-done.2, f32[3,2048]{1,0:T(4,128)} %copy-done.4, f32[1024,2048]{1,0:T(8,128)} %refs_6_.5, ...), custom_call_target="tpu_custom_call" | custom-call | tf_op jit(solution)/shard_map/products/pallas_call | solution.py:168
  28.9 2.4 %fusion.10 = (f32[3,128,256]{2,1,0:T(8,128)}, f32[3,128,256]{2,1,0:T(8,128)}, f32[3,128,256]{2,1,0:T(8,128)}, f32[3,128,256]{2,1,0:T(8,128)S(1)}) fusion(f32[6,256,256]{2,1,0:T(8,128)} %products.5.refs_6_), kind=kLoop, calls=%fused_computation.25 | loop fusion | bytes 3145728 | tf_op jit(solution)/shard_map/slice | solution.py:269
  31.3 1.8 %collective-permute-start.3 = (f32[3,128,256]{2,1,0:T(8,128)}, f32[3,128,256]{2,1,0:T(8,128)S(1)}, u32[]{:S(2)}, u32[]{:S(2)}) collective-permute-start(f32[3,128,256]{2,1,0:T(8,128)} %get-tuple-element.59), channel_id=1, source_target_pairs={{0,16},{1,17},{2,18},{3,19},{4,20},{5,21},{6,22},{7,23},{8,24},{9,... | collective-permute-start | bytes 1179656 | tf_op jit(solution)/shard_map/ppermute | solution.py:50
  33.1 7.0 %collective-permute-start.9 = (f32[3,128,256]{2,1,0:T(8,128)}, f32[3,128,256]{2,1,0:T(8,128)S(1)}, u32[]{:S(2)}, u32[]{:S(2)}) collective-permute-start(f32[3,128,256]{2,1,0:T(8,128)} %get-tuple-element.60), channel_id=1, source_target_pairs={{0,48},{1,49},{2,50},{3,51},{4,52},{5,53},{6,54},{7,55},{8,56},{9,... | collective-permute-start | bytes 1179656 | tf_op jit(solution)/shard_map/ppermute | solution.py:50
  40.1 0.1 collective-permute-start.7
  40.2 3.1 %collective-permute-start.5 = (f32[3,128,256]{2,1,0:T(8,128)S(1)}, f32[3,128,256]{2,1,0:T(8,128)}, u32[]{:S(2)}, u32[]{:S(2)}) collective-permute-start(f32[3,128,256]{2,1,0:T(8,128)S(1)} %get-tuple-element.62), channel_id=1, source_target_pairs={{0,48},{1,49},{2,50},{3,51},{4,52},{5,53},{6,54},{7,55},{8,56},{9,... | collective-permute-start | bytes 1179656 | tf_op jit(solution)/shard_map/ppermute | solution.py:50
  43.4 8.0 %products.4.refs_7_ = f32[12,256,256]{2,1,0:T(8,128)} custom-call(s32[144]{0:T(256)} %convert_element_type.13.refs_0_, s32[144]{0:T(256)} %reshape.165.refs_1_, s32[3]{0:T(128)} %pad_add_fusion.refs_2_, f32[3]{0:T(128)} %refs_3_.7, f32[16,16,256]{2,1,0:T(8,128)} %copy-done.2, f32[3,2048]{1,0:T(4,128)} %copy-done.4, f32[1024,2048]{1,0:T(8,128)} %refs_6_.5, ...), custom_call_target="tpu_custom_call" | custom-call | tf_op jit(solution)/shard_map/products/pallas_call | solution.py:168
  51.4 3.2 %fusion.9 = (f32[3,256,256]{2,1,0:T(8,128)S(1)}, f32[3,256,256]{2,1,0:T(8,128)S(1)}, f32[3,256,256]{2,1,0:T(8,128)}, f32[3,256,256]{2,1,0:T(8,128)S(1)}) fusion(f32[12,256,256]{2,1,0:T(8,128)} %products.4.refs_7_), kind=kLoop, calls=%fused_computation.24 | loop fusion | bytes 6291456 | tf_op jit(solution)/shard_map/slice | solution.py:266
  54.6 0.1 collective-permute-done.7
  54.7 1.1 collective-permute-done.5
  55.8 2.1 %fusion.8 = (f32[3,256,256]{2,1,0:T(8,128)S(1)}, f32[3,256,256]{2,1,0:T(8,128)S(1)}, f32[3,256,256]{2,1,0:T(8,128)}, f32[3,256,256]{2,1,0:T(8,128)S(1)}) fusion(f32[3,256,256]{2,1,0:T(8,128)S(1)} %get-tuple-element.55, f32[3,128,256]{2,1,0:T(8,128)S(1)} %collective-permute-done.3, f32[12,256,256]{2,1,0:T(8,128)S(1)} %copy-done, ...), kind=kLoop, calls=%fused_computation.14 | loop fusion | flops 393216 | bytes 4718592 | tf_op jit(solution)/shard_map/scatter-add | solution.py:273
  57.9 1.9 %collective-permute-start.10 = (f32[3,256,256]{2,1,0:T(8,128)S(1)}, f32[3,256,256]{2,1,0:T(8,128)}, u32[]{:S(2)}, u32[]{:S(2)}) collective-permute-start(f32[3,256,256]{2,1,0:T(8,128)S(1)} %get-tuple-element.52), channel_id=1, source_target_pairs={{0,48},{1,49},{2,50},{3,51},{4,52},{5,53},{6,54},{7,55},{8,56},{9,... | collective-permute-start | bytes 2359304 | tf_op jit(solution)/shard_map/ppermute | solution.py:50
  59.8 0.1 collective-permute-start.8
  59.9 6.1 %products.3.refs_8_ = f32[6,256,256]{2,1,0:T(8,128)} custom-call(s32[144]{0:T(256)} %convert_element_type.13.refs_0_, s32[144]{0:T(256)} %reshape.165.refs_1_, s32[3]{0:T(128)} %pad_add_fusion.refs_2_, f32[3]{0:T(128)} %refs_3_.7, f32[16,16,256]{2,1,0:T(8,128)} %copy-done.2, f32[3,2048]{1,0:T(4,128)} %copy-done.4, f32[1024,2048]{1,0:T(8,128)} %refs_6_.5, ...), custom_call_target="tpu_custom_call" | custom-call | tf_op jit(solution)/shard_map/products/pallas_call | solution.py:168
  66.1 12.9 %gradients.1 = f32[4,2048]{1,0:T(4,128)} custom-call(s32[144]{0:T(256)} %convert_element_type.13.refs_0_, s32[144]{0:T(256)} %reshape.165.refs_1_, s32[3]{0:T(128)} %pad_add_fusion.refs_2_, f32[3]{0:T(128)} %refs_3_.7, f32[16,16,256]{2,1,0:T(8,128)} %copy-done.2, f32[3,2048]{1,0:T(4,128)} %refs_5_.1, f32[6,256,256]{2,1,0:T(8,128)} %products.5.refs_6_, ...), custom_call_target="tpu_custom_call" | custom-call | tf_op jit(solution)/shard_map/gradients/pallas_call | solution.py:228
  79.0 0.7 slice_reduce_fusion.1
  79.7 0.1 reduce_sum.27
  79.9 0.8 slice_bitcast_fusion.1
  80.7 10.2 %all_to_all.24 = f32[16,4,128]{2,1,0:T(4,128)S(1)} all-to-all(f32[16,4,128]{2,1,0:T(4,128)S(1)} %pad_maximum_fusion), channel_id=1, replica_groups=mesh['xh'=2,'y'=4,'c'=2,'xl'=2,'z'=4] {'xh','y','c'}, dimensions={0} | all-to-all | bytes 65536 | tf_op jit(solution)/shard_map/all_to_all | solution.py:287
  90.8 0.6 collective-permute-start.4
  91.5 2.7 %collective-permute-start.6 = (f32[3,256,256]{2,1,0:T(8,128)}, f32[3,256,256]{2,1,0:T(8,128)}, u32[]{:S(2)}, u32[]{:S(2)}) collective-permute-start(f32[3,256,256]{2,1,0:T(8,128)} %copy-done.3), channel_id=1, source_target_pairs={{0,48},{1,49},{2,50},{3,51},{4,52},{5,53},{6,54},{7,55},{8,56},{9,... | collective-permute-start | bytes 2359304 | tf_op jit(solution)/shard_map/ppermute | solution.py:50
  94.2 2.4 %fusion = f32[3,256,256]{2,1,0:T(8,128)} fusion(f32[3,256,256]{2,1,0:T(8,128)} %collective-permute-done.10, f32[3,256,256]{2,1,0:T(8,128)} %collective-permute-done.8, f32[6,256,256]{2,1,0:T(8,128)S(1)} %copy-done.1), kind=kLoop, calls=%fused_computation.1 | loop fusion | flops 393216 | bytes 3145728 | tf_op jit(solution)/shard_map/add | solution.py:275
  96.6 0.6 collective-permute-start.11
  97.2 0.6 broadcast_in_dim.34
  97.8 8.3 %all-to-all-start.3 = ((f32[8,1,128]{2,1,0:T(1,128)}), f32[8,1,128]{2,1,0:T(1,128)S(1)}, u32[]{:S(2)}, u32[]{:S(2)}) async-start(f32[8,1,128]{2,1,0:T(1,128)} %broadcast_in_dim.34), calls=%async_computation.3 | async-start | bytes 8192 | tf_op jit(solution)/shard_map/all_to_all | solution.py:290
  106.1 15.3 %all-to-all-done.3 = f32[8,1,128]{2,1,0:T(1,128)S(1)} async-done(((f32[8,1,128]{2,1,0:T(1,128)}), f32[8,1,128]{2,1,0:T(1,128)S(1)}, u32[]{:S(2)}, u32[]{:S(2)}) %all-to-all-start.3) | async-done | bytes 4128 | tf_op jit(solution)/shard_map/all_to_all | solution.py:290
  121.4 0.6 broadcast_in_dim.33
  122.1 4.9 %all-to-all-start.2 = ((f32[16,4,128]{2,1,0:T(4,128)}), f32[16,4,128]{2,1,0:T(4,128)S(1)}, u32[]{:S(2)}, u32[]{:S(2)}) async-start(f32[16,4,128]{2,1,0:T(4,128)} %broadcast_in_dim.33), calls=%async_computation.2 | async-start | bytes 65536 | tf_op jit(solution)/shard_map/all_to_all | solution.py:288
  127.0 0.5 slice_reduce_fusion
  127.5 7.1 %all-to-all-done.2 = f32[16,4,128]{2,1,0:T(4,128)S(1)} async-done(((f32[16,4,128]{2,1,0:T(4,128)}), f32[16,4,128]{2,1,0:T(4,128)S(1)}, u32[]{:S(2)}, u32[]{:S(2)}) %all-to-all-start.2) | async-done | bytes 32800 | tf_op jit(solution)/shard_map/all_to_all | solution.py:288
  134.6 0.6 slice_bitcast_fusion
  135.2 2.5 %fusion.4 = f32[1,1,3,256,256]{4,3,2,1,0:T(8,128)} fusion(f32[3,256,256]{2,1,0:T(8,128)S(1)} %collective-permute-done.11, f32[3,256,256]{2,1,0:T(8,128)} %collective-permute-done.6, f32[3,256,256]{2,1,0:T(8,128)} %collective-permute-done.4, f32[6,256,256]{2,1,0:T(8,128)S(1)} %copy-done.1, pred[3]{0:T(512)(128)(4,1)S(1)} %iota_compare_fusion), kind=kLoop, calls=%fused_computation.6 | loop fusion | flops 786432 | bytes 3932163 | tf_op jit(solution)/shard_map/reshape | solution.py:292
  (28 shorter events, 0.2 us)
Async XLA Ops:
  0.6 22.2 %collective-permute-start.2 = (f32[1024,2048]{1,0:T(8,128)}, f32[1024,2048]{1,0:T(8,128)}, u32[]{:S(2)}, u32[]{:S(2)}) collective-permute-start(f32[1024,2048]{1,0:T(8,128)} %refs_6_.5), channel_id=1, source_target_pairs={{0,8},{1,9},{2,10},{3,11},{4,12},{5,13},{6,14},{7,15},{8,0},{9,1},... | collective-permute-start | bytes 25165832 | tf_op jit(solution)/shard_map/ppermute | solution.py:50
  2.9 16.8 %all-to-all-start = ((f32[16,16,256]{2,1,0:T(8,128)}), f32[16,16,256]{2,1,0:T(8,128)S(1)}, u32[]{:S(2)}, u32[]{:S(2)}) async-start(f32[16,16,256]{2,1,0:T(8,128)} %payload.1), calls=%async_computation | async-start | bytes 524288 | tf_op jit(solution)/shard_map/all_to_all | solution.py:251
  10.1 12.7 %collective-permute-start.1 = (f32[3,2048]{1,0:T(4,128)}, f32[3,2048]{1,0:T(4,128)S(1)}, u32[]{:S(2)}, u32[]{:S(2)}) collective-permute-start(f32[3,2048]{1,0:T(4,128)} %refs_5_.1), channel_id=1, source_target_pairs={{0,0},{1,16},{2,32},{3,48},{4,64},{5,80},{6,96},{7,112},{8,8},{9,2... | collective-permute-start | bytes 73736 | tf_op jit(solution)/shard_map/ppermute | solution.py:50
  19.7 3.2 %copy-start.2 = (f32[16,16,256]{2,1,0:T(8,128)}, f32[16,16,256]{2,1,0:T(8,128)S(1)}, u32[]{:S(2)}) copy-start(f32[16,16,256]{2,1,0:T(8,128)S(1)} %all-to-all-done.refs_4_) | copy-start | bytes 786436
  20.0 2.1 %collective-permute-start = (s32[16,9]{0,1:T(8,128)S(1)}, s32[16,9]{0,1:T(8,128)S(1)}, u32[]{:S(2)}, u32[]{:S(2)}) collective-permute-start(s32[16,9]{0,1:T(8,128)S(1)} %convert_element_type.14), channel_id=1, source_target_pairs={{0,0},{1,16},{2,32},{3,48},{4,64},{5,80},{6,96},{7,112},{8,8},{9,2... | collective-permute-start | bytes 1736 | tf_op jit(solution)/shard_map/ppermute | solution.py:50
  22.8 0.6 copy-start.4
  31.3 23.3 %collective-permute-start.3 = (f32[3,128,256]{2,1,0:T(8,128)}, f32[3,128,256]{2,1,0:T(8,128)S(1)}, u32[]{:S(2)}, u32[]{:S(2)}) collective-permute-start(f32[3,128,256]{2,1,0:T(8,128)} %get-tuple-element.59), channel_id=1, source_target_pairs={{0,16},{1,17},{2,18},{3,19},{4,20},{5,21},{6,22},{7,23},{8,24},{9,... | collective-permute-start | bytes 1179656 | tf_op jit(solution)/shard_map/ppermute | solution.py:50
  33.1 21.5 %collective-permute-start.9 = (f32[3,128,256]{2,1,0:T(8,128)}, f32[3,128,256]{2,1,0:T(8,128)S(1)}, u32[]{:S(2)}, u32[]{:S(2)}) collective-permute-start(f32[3,128,256]{2,1,0:T(8,128)} %get-tuple-element.60), channel_id=1, source_target_pairs={{0,48},{1,49},{2,50},{3,51},{4,52},{5,53},{6,54},{7,55},{8,56},{9,... | collective-permute-start | bytes 1179656 | tf_op jit(solution)/shard_map/ppermute | solution.py:50
  40.1 14.6 %collective-permute-start.7 = (f32[3,128,256]{2,1,0:T(8,128)}, f32[3,128,256]{2,1,0:T(8,128)}, u32[]{:S(2)}, u32[]{:S(2)}) collective-permute-start(f32[3,128,256]{2,1,0:T(8,128)} %get-tuple-element.61), channel_id=1, source_target_pairs={{0,16},{1,17},{2,18},{3,19},{4,20},{5,21},{6,22},{7,23},{8,24},{9,... | collective-permute-start | bytes 1179656 | tf_op jit(solution)/shard_map/ppermute | solution.py:50
  40.2 15.6 %collective-permute-start.5 = (f32[3,128,256]{2,1,0:T(8,128)S(1)}, f32[3,128,256]{2,1,0:T(8,128)}, u32[]{:S(2)}, u32[]{:S(2)}) collective-permute-start(f32[3,128,256]{2,1,0:T(8,128)S(1)} %get-tuple-element.62), channel_id=1, source_target_pairs={{0,48},{1,49},{2,50},{3,51},{4,52},{5,53},{6,54},{7,55},{8,56},{9,... | collective-permute-start | bytes 1179656 | tf_op jit(solution)/shard_map/ppermute | solution.py:50
  51.4 4.4 %copy-start = (f32[12,256,256]{2,1,0:T(8,128)S(1)}, f32[12,256,256]{2,1,0:T(8,128)}, u32[]{:S(2)}) copy-start(f32[12,256,256]{2,1,0:T(8,128)} %products.4.refs_7_) | copy-start | bytes 9437188
  57.9 2.0 %copy-start.3 = (f32[3,256,256]{2,1,0:T(8,128)}, f32[3,256,256]{2,1,0:T(8,128)S(1)}, u32[]{:S(2)}) copy-start(f32[3,256,256]{2,1,0:T(8,128)S(1)} %get-tuple-element.54) | copy-start | bytes 2359300
  57.9 36.3 %collective-permute-start.10 = (f32[3,256,256]{2,1,0:T(8,128)S(1)}, f32[3,256,256]{2,1,0:T(8,128)}, u32[]{:S(2)}, u32[]{:S(2)}) collective-permute-start(f32[3,256,256]{2,1,0:T(8,128)S(1)} %get-tuple-element.52), channel_id=1, source_target_pairs={{0,48},{1,49},{2,50},{3,51},{4,52},{5,53},{6,54},{7,55},{8,56},{9,... | collective-permute-start | bytes 2359304 | tf_op jit(solution)/shard_map/ppermute | solution.py:50
  59.8 34.4 %collective-permute-start.8 = (f32[3,256,256]{2,1,0:T(8,128)}, f32[3,256,256]{2,1,0:T(8,128)}, u32[]{:S(2)}, u32[]{:S(2)}) collective-permute-start(f32[3,256,256]{2,1,0:T(8,128)} %get-tuple-element.53), channel_id=1, source_target_pairs={{0,16},{1,17},{2,18},{3,19},{4,20},{5,21},{6,22},{7,23},{8,24},{9,... | collective-permute-start | bytes 2359304 | tf_op jit(solution)/shard_map/ppermute | solution.py:50
  66.1 28.1 %copy-start.1 = (f32[6,256,256]{2,1,0:T(8,128)S(1)}, f32[6,256,256]{2,1,0:T(8,128)}, u32[]{:S(2)}) copy-start(f32[6,256,256]{2,1,0:T(8,128)} %products.3.refs_8_) | copy-start | bytes 4718596
  90.8 44.4 %collective-permute-start.4 = (f32[3,256,256]{2,1,0:T(8,128)S(1)}, f32[3,256,256]{2,1,0:T(8,128)}, u32[]{:S(2)}, u32[]{:S(2)}) collective-permute-start(f32[3,256,256]{2,1,0:T(8,128)S(1)} %get-tuple-element.51), channel_id=1, source_target_pairs={{0,16},{1,17},{2,18},{3,19},{4,20},{5,21},{6,22},{7,23},{8,24},{9,... | collective-permute-start | bytes 2359304 | tf_op jit(solution)/shard_map/ppermute | solution.py:50
  91.5 43.7 %collective-permute-start.6 = (f32[3,256,256]{2,1,0:T(8,128)}, f32[3,256,256]{2,1,0:T(8,128)}, u32[]{:S(2)}, u32[]{:S(2)}) collective-permute-start(f32[3,256,256]{2,1,0:T(8,128)} %copy-done.3), channel_id=1, source_target_pairs={{0,48},{1,49},{2,50},{3,51},{4,52},{5,53},{6,54},{7,55},{8,56},{9,... | collective-permute-start | bytes 2359304 | tf_op jit(solution)/shard_map/ppermute | solution.py:50
  96.6 38.7 %collective-permute-start.11 = (f32[3,256,256]{2,1,0:T(8,128)}, f32[3,256,256]{2,1,0:T(8,128)S(1)}, u32[]{:S(2)}, u32[]{:S(2)}) collective-permute-start(f32[3,256,256]{2,1,0:T(8,128)} %fusion), channel_id=1, source_target_pairs={{0,64},{1,65},{2,66},{3,67},{4,68},{5,69},{6,70},{7,71},{8,72},{9,... | collective-permute-start | bytes 2359304 | tf_op jit(solution)/shard_map/ppermute | solution.py:50
  97.8 23.7 %all-to-all-start.3 = ((f32[8,1,128]{2,1,0:T(1,128)}), f32[8,1,128]{2,1,0:T(1,128)S(1)}, u32[]{:S(2)}, u32[]{:S(2)}) async-start(f32[8,1,128]{2,1,0:T(1,128)} %broadcast_in_dim.34), calls=%async_computation.3 | async-start | bytes 8192 | tf_op jit(solution)/shard_map/all_to_all | solution.py:290
  122.1 12.5 %all-to-all-start.2 = ((f32[16,4,128]{2,1,0:T(4,128)}), f32[16,4,128]{2,1,0:T(4,128)S(1)}, u32[]{:S(2)}, u32[]{:S(2)}) async-start(f32[16,4,128]{2,1,0:T(4,128)} %broadcast_in_dim.33), calls=%async_computation.2 | async-start | bytes 65536 | tf_op jit(solution)/shard_map/all_to_all | solution.py:288

commit v2 on v1

v2 whole, which is shorter than its diff:
```python
import itertools

import jax
import jax.numpy as jnp
from jax import lax
from jax.experimental import pallas as pl
from jax.experimental.pallas import tpu as pltpu
from jax.sharding import Mesh, PartitionSpec as P


BS = 256
SLOTS = 3
AXES = ("xh", "y", "c", "xl", "z")
SIZES = (2, 4, 2, 2, 4)
DP = ("xh", "y", "c")
IND = ("xl", "z")


def pairs(target):
    def flat(place):
        index = 0
        for size, coord in zip(SIZES, place):
            index = index * size + coord
        return index

    places = itertools.product(*(range(size) for size in SIZES))
    return [(flat(place), flat(target(*place))) for place in places]


def shift_y(step):
    return pairs(lambda xh, y, c, xl, z: (xh, (y + step) % 4, c, xl, z))


SWAP_CORE = pairs(lambda xh, y, c, xl, z: (xh, y, 1 - c, xl, z))
SWAP_XH = pairs(lambda xh, y, c, xl, z: (1 - xh, y, c, xl, z))
SWAP_XL = pairs(lambda xh, y, c, xl, z: (xh, y, c, 1 - xl, z))


def flip_y(bits):
    return pairs(lambda xh, y, c, xl, z: (xh, y ^ bits, c, xl, z))


def flip_z(bits):
    return pairs(lambda xh, y, c, xl, z: (xh, y, c, xl, z ^ bits))


Y_UP = shift_y(1)
Y_DOWN = shift_y(3)


def transpose_place(xh, y, c, xl, z):
    row = (xh * 4 + y) * 2 + c
    col = xl * 4 + z
    owner, new_col = 2 * col + row % 2, row // 2
    return (owner // 8, owner // 2 % 4, owner % 2, new_col // 4, new_col % 4)


TRANSPOSE = pairs(transpose_place)


def permute(value, perm):
    return lax.ppermute(value, AXES, perm)


def payload_kernel(rows_ref, cols_ref, count_ref, x_ref, out_ref, pack_ref):
    lane = lax.broadcasted_iota(jnp.int32, (1, BS), 1)
    info = jnp.zeros((1, BS), jnp.int32)
    pack_ref[...] = jnp.zeros_like(pack_ref)
    for slot in range(SLOTS):
        live = jnp.where(count_ref[0, 0] > slot, 1, 0)
        row = rows_ref[0, 0, slot] * live
        col = cols_ref[0, 0, slot] * live
        start = pl.multiple_of(row * BS, BS)
        pack_ref[4 * slot : 4 * slot + 3, :] = x_ref[:, pl.ds(start, BS)]
        for place, value in enumerate((row, col, live)):
            info = jnp.where(lane == 3 * slot + place, value, info)
    pack_ref[12:13, :] = info.astype(jnp.float32)
    packed = pack_ref[...]
    for dest in range(out_ref.shape[0]):
        out_ref[dest] = packed


def slot_of(place, step, own_ref, near_ref, pos_ref):
    own_x = place // SLOTS
    slot = place % SLOTS
    xh = jnp.where(own_x == 1, pos_ref[0], 1 - pos_ref[0])
    group = xh * 8 + lax.rem(pos_ref[1] + step, 4) * 2 + pos_ref[2]
    row = own_ref[group, 3 * slot]
    col = own_ref[group, 3 * slot + 1]
    live = own_ref[group, 3 * slot + 2]
    near = 0
    found = 0
    for other in range(SLOTS):
        match = jnp.where(near_ref[group, 3 * other] == row, near_ref[group, 3 * other + 2], 0)
        near = near + match * near_ref[group, 3 * other + 1]
        found = found + match
    return group, slot, col, near, (live * found) > 0


def scaled_points(pay_ref, group, slot, z_ref, start, scale_ref):
    rolled = pltpu.roll(pay_ref[group], lax.rem(16 - 4 * slot, 16), 0)
    padded = jnp.concatenate([rolled[0:8], jnp.zeros((120, BS), jnp.float32)], axis=0)
    x_cols = jnp.transpose(padded)
    z_rows = z_ref[:, pl.ds(pl.multiple_of(start, BS), BS)]
    inverses = [1.0 / scale_ref[q] for q in range(3)]
    return [x_cols[:, q : q + 1] * inverses[q] for q in range(3)], [z_rows[q : q + 1, :] * inverses[q] for q in range(3)]


def strip_offsets(points, row):
    x_cols, z_rows = points
    return [x_cols[q][row : row + STRIP] - z_rows[q] for q in range(3)]


def radius_of(offsets):
    dist = offsets[0] * offsets[0] + offsets[1] * offsets[1] + offsets[2] * offsets[2]
    return dist * lax.rsqrt(jnp.maximum(dist, 1e-30))


def split(value):
    high = value.astype(jnp.bfloat16)
    return high, (value - high.astype(jnp.float32)).astype(jnp.bfloat16)


STRIP = 32
HALF = BS // 2
COUNT = 2 * SLOTS


def product_kernel(steps, form, own_ref, near_ref, pos_ref, scale_ref, pay_ref, z_ref, mine_ref, mate_ref, *refs):
    *outs, tiles, results, left, right, in_sems, out_sems = refs

    def copy_in(source, row, col, place):
        window = source.at[pl.ds(row * BS, BS), pl.ds(col * BS, BS)]
        return pltpu.make_async_copy(window, tiles.at[place], in_sems.at[place])

    def copy_half(place, half, out, index):
        window = results.at[place, pl.ds(half * HALF, HALF)]
        return pltpu.make_async_copy(window, out.at[index], out_sems.at[place, half])

    def copy_out(number, local, place):
        if form == "whole":
            for half in range(2):
                window = outs[0].at[local, pl.ds(half * HALF, HALF)]
                source = results.at[place, pl.ds(half * HALF, HALF)]
                pltpu.make_async_copy(source, window, out_sems.at[place, half]).start()
        elif form == "halves":
            for half in range(2):
                copy_half(place, half, outs[half], local).start()
        else:
            for own_x in range(2):

                @pl.when(local // SLOTS == own_x)
                def _():
                    for half in range(2):
                        out = outs[4 * number + 2 * own_x + half]
                        copy_half(place, half, out, local % SLOTS).start()

    for number, step in enumerate(steps):
        for local in range(COUNT):
            place = number * COUNT + local
            _, _, col, near, active = slot_of(local, step, own_ref, near_ref, pos_ref)
            mine = (near // 4) == pos_ref[2]
            row = lax.rem(near, 4)

            @pl.when(jnp.logical_and(active, mine))
            def _():
                copy_in(mine_ref, row, col, place).start()

            @pl.when(jnp.logical_and(active, jnp.logical_not(mine)))
            def _():
                copy_in(mate_ref, row, col, place).start()

    for number, step in enumerate(steps):

        def body(local, carry):
            place = number * COUNT + local
            group, slot, _, near, active = slot_of(local, step, own_ref, near_ref, pos_ref)

            @pl.when(active)
            def _():
                points = scaled_points(pay_ref, group, slot, z_ref, near * BS, scale_ref)
                for row in range(0, BS, STRIP):
                    rows = slice(row, row + STRIP)
                    radius = radius_of(strip_offsets(points, row))
                    remain = jnp.maximum(1.0 - radius, 0.0)
                    square = remain * remain
                    high, low = split(square * square * (4.0 * radius + 1.0))
                    left[rows, 0:BS] = high
                    left[rows, BS : 2 * BS] = low
                    left[rows, 2 * BS : 3 * BS] = high
                copy_in(mine_ref, 0, 0, place).wait()
                for row in range(0, BS, STRIP):
                    high, low = split(tiles[place, pl.ds(row, STRIP), :])
                    right[row : row + STRIP, :] = low
                    right[BS + row : BS + row + STRIP, :] = high
                    right[2 * BS + row : 2 * BS + row + STRIP, :] = high
                results[place] = jnp.dot(left[...], right[...], preferred_element_type=jnp.float32)

            @pl.when(jnp.logical_not(active))
            def _():
                results[place] = jnp.zeros((BS, BS), jnp.float32)

            copy_out(number, local, place)
            return carry

        lax.fori_loop(0, COUNT, body, 0)

    for place in range(COUNT * len(steps)):
        for half in range(2):
            window = results.at[place, pl.ds(half * HALF, HALF)]
            other = results.at[place, pl.ds((1 - half) * HALF, HALF)]
            pltpu.make_async_copy(window, other, out_sems.at[place, half]).wait()


SMEM = pl.BlockSpec(memory_space=pltpu.SMEM)
VMEM = pl.BlockSpec(memory_space=pltpu.VMEM)
HBM = pl.BlockSpec(memory_space=pl.ANY)


def products(steps, form, tables, scales, payload, z_near, mine, mate):
    number = COUNT * len(steps)
    shapes = {
        "whole": [(COUNT, BS, BS)],
        "halves": [(COUNT, HALF, BS)] * 2,
        "split": [(SLOTS, HALF, BS)] * (4 * len(steps)),
    }[form]

    def kernel(*refs):
        product_kernel(steps, form, *refs)

    return pl.pallas_call(
        kernel,
        out_shape=[jax.ShapeDtypeStruct(shape, jnp.float32) for shape in shapes],
        in_specs=[SMEM, SMEM, SMEM, SMEM, VMEM, VMEM, HBM, HBM],
        out_specs=[HBM] * len(shapes),
        scratch_shapes=[
            pltpu.VMEM((number, BS, BS), jnp.float32),
            pltpu.VMEM((number, BS, BS), jnp.float32),
            pltpu.VMEM((BS, 3 * BS), jnp.bfloat16),
            pltpu.VMEM((3 * BS, BS), jnp.bfloat16),
            pltpu.SemaphoreType.DMA((number,)),
            pltpu.SemaphoreType.DMA((number, 2)),
        ],
    )(*tables, scales, payload, z_near, mine, mate)


def gradient_kernel(own_ref, near_ref, pos_ref, scale_ref, pay_ref, z_ref, *refs):
    parts, out_ref = refs[:-1], refs[-1]
    out_ref[...] = jnp.zeros_like(out_ref)
    far, sides, here = parts[:2], parts[2:10], parts[10:]

    def accumulate(local, step, pick):
        group, slot, col, _, active = slot_of(local, step, own_ref, near_ref, pos_ref)

        @pl.when(active)
        def _():
            start = pl.multiple_of(col * BS, BS)
            points = scaled_points(pay_ref, group, slot, z_ref, start, scale_ref)
            z_sums = [jnp.zeros((8, BS), jnp.float32) for _ in range(3)]
            scale_sums = list(z_sums)
            for row in range(0, BS, STRIP):
                offsets = strip_offsets(points, row)
                remain = jnp.maximum(1.0 - radius_of(offsets), 0.0)
                grad = pick(row) * (remain * remain * remain)
                for q in range(3):
                    weighted = grad * offsets[q]
                    squared = weighted * offsets[q]
                    for piece in range(0, STRIP, 8):
                        z_sums[q] = z_sums[q] + weighted[piece : piece + 8]
                        scale_sums[q] = scale_sums[q] + squared[piece : piece + 8]
            for q in range(3):
                factor = 20.0 / scale_ref[q]
                out_ref[q : q + 1, pl.ds(start, BS)] += factor * jnp.sum(z_sums[q], axis=0, keepdims=True)
                out_ref[3:4, q * BS : (q + 1) * BS] += factor * jnp.sum(scale_sums[q], axis=0, keepdims=True)

    def both(top, bottom, index):
        def pick(row):
            source = top if row < HALF else bottom
            return source[index, pl.ds(row % HALF, STRIP), :]

        return pick

    def body(local, carry):
        accumulate(local, 2, both(far[0], far[1], local))
        accumulate(local, 0, lambda row: here[0][local, pl.ds(row, STRIP), :])
        return carry

    lax.fori_loop(0, COUNT, body, 0)

    def side_body(slot, carry):
        for number, step in enumerate((1, 3)):
            for own_x in range(2):
                top, bottom = sides[4 * number + 2 * own_x : 4 * number + 2 * own_x + 2]
                accumulate(own_x * SLOTS + slot, step, both(top, bottom, slot))
        return carry

    lax.fori_loop(0, SLOTS, side_body, 0)


def gradients(tables, scales, payload, z_own, parts):
    return pl.pallas_call(
        gradient_kernel,
        out_shape=jax.ShapeDtypeStruct((4, z_own.shape[1]), jnp.float32),
        in_specs=[SMEM, SMEM, SMEM, SMEM, VMEM, VMEM] + [VMEM] * len(parts),
        out_specs=VMEM,
        name="gradients",
    )(*tables, scales, payload, z_own, *parts)


def combine_kernel(base_ref, tops, bottoms, extra, count_ref, out_ref):
    slot = pl.program_id(0)
    keep = count_ref[0, 0] > slot
    for half, pieces in enumerate((tops, bottoms)):
        rows = pl.ds(half * HALF, HALF)
        total = base_ref[0, rows, :]
        for piece in pieces:
            total = total + piece[0]
        if extra is not None:
            total = jnp.where(keep, total + extra[0, rows, :], 0.0)
        out_ref[0, rows, :] = total


def combine(base, first, tops, bottoms, extra, count):
    whole = pl.BlockSpec((1, BS, BS), lambda s: (s, 0, 0))
    half = pl.BlockSpec((1, HALF, BS), lambda s: (s, 0, 0))
    extras = [] if extra is None else [extra]

    def kernel(count_ref, base_ref, *refs):
        extra_ref = refs[4] if extras else None
        combine_kernel(base_ref, refs[0:2], refs[2:4], extra_ref, count_ref, refs[-1])

    return pl.pallas_call(
        kernel,
        grid=(SLOTS,),
        out_shape=jax.ShapeDtypeStruct((SLOTS, BS, BS), jnp.float32),
        in_specs=[SMEM, pl.BlockSpec((1, BS, BS), lambda s: (s + first, 0, 0))] + [half] * 4 + [whole] * len(extras),
        out_specs=whole,
    )(count, base, *tops, *bottoms, *extras)


def on_device(x_points, z_points, length_scales, dpsi_grad, block_rows, block_cols, block_count):
    xh, y, core = (lax.axis_index(name).astype(jnp.int32) for name in DP)
    mate = permute(dpsi_grad, SWAP_CORE)
    z_near = permute(z_points, TRANSPOSE)
    outgoing = pl.pallas_call(
        payload_kernel,
        out_shape=jax.ShapeDtypeStruct((16, 16, BS), jnp.float32),
        in_specs=[SMEM, SMEM, SMEM, VMEM],
        out_specs=VMEM,
        scratch_shapes=[pltpu.VMEM((16, BS), jnp.float32)],
        name="payload",
    )(block_rows, block_cols, block_count, x_points)
    payload = lax.all_to_all(outgoing, DP, 0, 0, tiled=True)
    own_table = payload[:, 12, :9].astype(jnp.int32)
    near_table = permute(own_table, TRANSPOSE)
    tables = (own_table, near_table, jnp.stack([xh, y, core]))

    args = (tables, length_scales, payload, z_near, dpsi_grad, mate)
    far = products((2,), "halves", *args)
    got_up = permute(far[0], Y_UP)
    got_down = permute(far[1], Y_DOWN)
    sides = products((1, 3), "split", *args)
    up_o, up_w, down_o, down_w = (sides[2 * k : 2 * k + 2] for k in range(4))
    direct_up_o = permute(up_o[1], Y_UP)
    direct_down_o = permute(down_o[0], Y_DOWN)
    (here,) = products((0,), "whole", *args)
    local = gradients(tables, length_scales, payload, z_points, (*far, *sides, here))
    sum_up_o = permute(up_o[0] + got_up[:SLOTS], Y_UP)
    sum_down_o = permute(down_o[1] + got_down[:SLOTS], Y_DOWN)
    direct_up_w = permute(up_w[1], Y_UP)
    direct_down_w = permute(down_w[0], Y_DOWN)
    sum_up_w = permute(up_w[0] + got_up[SLOTS:], Y_UP)
    sum_down_w = permute(down_w[1] + got_down[SLOTS:], Y_DOWN)
    sum_o = combine(here, 0, (sum_up_o, direct_down_o), (direct_up_o, sum_down_o), None, block_count)
    got_x = permute(sum_o, SWAP_XH)
    dk_local = combine(here, SLOTS, (sum_up_w, direct_down_w), (direct_up_w, sum_down_w), got_x, block_count)

    total = local + permute(local, SWAP_CORE)
    total = total + permute(total, SWAP_XH)
    total = (total + permute(total, flip_y(1))) + (permute(total, flip_y(2)) + permute(total, flip_y(3)))
    z_grad = total[:3]
    scale = jnp.pad(jnp.sum(total[3, : 3 * BS].reshape(3, BS), axis=1), (0, 125)).reshape(1, 128)
    scale = (scale + permute(scale, flip_z(1))) + (permute(scale, flip_z(2)) + permute(scale, flip_z(3)))
    scale = scale + permute(scale, SWAP_XL)
    scale_grad = scale[0, :3]
    return dk_local.reshape(1, 1, SLOTS, BS, BS), z_grad, scale_grad


def solution(mesh):
    fine = Mesh(mesh.devices.reshape(SIZES), AXES)

    return jax.shard_map(
        on_device,
        mesh=fine,
        in_specs=(
            P(None, DP),
            P(None, IND),
            P(),
            P(DP, IND),
            P(DP, IND, None),
            P(DP, IND, None),
            P(DP, IND),
        ),
        out_specs=(P(DP, IND, None, None, None), P(None, IND), P()),
        check_vma=False,
    )
```

time: 140 us -> 131 us (0.936); the launches traced: 138 us -> 130 us
  blocking collectives: 10.2 us -> 0 us
  waiting for transfers between devices: 31.7 us -> 41.7 us
  local copies, waits for them, and re-layouts: 11.4 us -> 3.55 us
  other arithmetic: 8.36 us -> 2.51 us
  starting transfers between devices: 40.7 us -> 44.1 us
  Pallas kernels: 34 us -> 36.9 us
    ppermute x12 -> x23, waiting for transfers between devices: 1.2 us -> 33.6 us  [permute(): return lax.ppermute(value, AXES, perm)]
    all_to_all x2 -> x0, waiting for transfers between devices: 22.4 us -> none  [the longest x1 15.3 us: on_device(): lax.all_to_all(jnp.broadcast_to(summed[3:4], (8, width)), IND, 0, 0, tile...]
    ppermute x12 -> x23, starting transfers between devices: 20.2 us -> 36.8 us  [permute(): return lax.ppermute(value, AXES, perm)]
    all_to_all x2 -> x0, starting transfers between devices: 13.3 us -> none  [the longest x1 8.33 us: on_device(): lax.all_to_all(jnp.broadcast_to(summed[3:4], (8, width)), IND, 0, 0, tile...]
    all_to_all x1 -> x0, blocking collectives: 10.2 us -> none  [on_device(): summed = jnp.sum(lax.all_to_all(chunks, DP, 0, 0, tiled=True), axis=0)]
    slice x8 -> x1, local copies, waits for them, and re-layouts: 6.58 us -> 0.02 us  [on_device(): total[3, :3 * BS].reshape(3, BS)]
    pallas_call x4 -> x6, Pallas kernels: 32.5 us -> 35.4 us  [the longest x3 17.9 us: products(): pl.pallas_call(kernel, out_shape=[jax.ShapeDtypeStruct(shape, jnp.float32...]
    reshape x1 -> x0, other arithmetic: 2.48 us -> none  [on_device(): return (dk_local.reshape(1, 1, s3, BS, BS), z_grad, scale_grad)]
  transfers between devices with their start and end apart: 15 -> 24, of which waited for: 5 -> 13; matrix products, arithmetic and copies ran while one was open for 9% -> 2% of each run, Pallas kernels for 21% -> 19%
where the time goes in v2:
time: 131 us; the launch traced here: 130 us
  starting transfers between devices  44.1 us (34%)
  waiting for transfers between devices  41.7 us (32%)
  Pallas kernels  36.9 us (28%)
  local copies, waits for them, and re-layouts  3.55 us (3%)
  other arithmetic  2.51 us (2%)
  between operations  1.53 us (1%)
    ppermute x23, starting transfers between devices, permute(): return lax.ppermute(value, AXES, perm)  36.8 us
    ppermute x23, waiting for transfers between devices, permute(): return lax.ppermute(value, AXES, perm)  33.6 us
    pallas_call x3, Pallas kernels, products(): pl.pallas_call(kernel, out_shape=[jax.ShapeDtypeStruct(shape, jnp.float32...  17.9 us
    pallas_call x1, Pallas kernels, gradients(): pl.pallas_call(gradient_kernel, out_shape=jax.ShapeDtypeStruct((4, z_own....  10.7 us
    all_to_all x1, waiting for transfers between devices, on_device(): payload = lax.all_to_all(outgoing, DP, 0, 0, tiled=True)  8.1 us
    all_to_all x1, starting transfers between devices, on_device(): payload = lax.all_to_all(outgoing, DP, 0, 0, tiled=True)  7.25 us
    pallas_call x2, Pallas kernels, combine(): pl.pallas_call(kernel, grid=(SLOTS,), out_shape=jax.ShapeDtypeStruct((SLO...  6.79 us
    unnamed x34, local copies, waits for them, and re-layouts  3 us
  transfers between devices with their start and end apart: 24, of which 13 were waited for; matrix products, arithmetic and copies ran while one was open for 2% of the time, Pallas kernels for 19%

profile of v2, /device:TPU:0, one launch (start us, length us, event | category | flops | bytes accessed | tf_op | source)
XLA Modules:
  0.0 130.3 jit_solution(1850883034681836439)
XLA Ops:
  0.6 0.1 collective-permute-start.2
  1.4 1.5 %payload.1 = f32[16,16,256]{2,1,0:T(8,128)} custom-call(s32[1,1,3]{2,1,0:T(1,128)} %rows_ref.1, s32[1,1,3]{2,1,0:T(1,128)} %cols_ref.1, s32[1,1]{1,0:T(1,128)S(6)} %copy.10.count_ref, f32[3,2048]{1,0:T(4,128)} %x_ref.1), custom_call_target="tpu_custom_call" | custom-call | tf_op jit(solution)/shard_map/payload/pallas_call | solution.py:345
  2.9 7.3 %all-to-all-start = ((f32[16,16,256]{2,1,0:T(8,128)}), f32[16,16,256]{2,1,0:T(8,128)S(1)}, u32[]{:S(2)}, u32[]{:S(2)}) async-start(f32[16,16,256]{2,1,0:T(8,128)} %payload.1), calls=%async_computation | async-start | bytes 524288 | tf_op jit(solution)/shard_map/all_to_all | solution.py:353
  10.1 1.4 %collective-permute-start.1 = (f32[3,2048]{1,0:T(4,128)}, f32[3,2048]{1,0:T(4,128)S(1)}, u32[]{:S(2)}, u32[]{:S(2)}) collective-permute-start(f32[3,2048]{1,0:T(4,128)} %z_ref.1), channel_id=1, source_target_pairs={{0,0},{1,16},{2,32},{3,48},{4,64},{5,80},{6,96},{7,112},{8,8},{9,2... | collective-permute-start | bytes 73736 | tf_op jit(solution)/shard_map/ppermute | solution.py:62
  11.6 8.1 %all-to-all-done.refs_4_.pay_ref = f32[16,16,256]{2,1,0:T(8,128)S(1)} async-done(((f32[16,16,256]{2,1,0:T(8,128)}), f32[16,16,256]{2,1,0:T(8,128)S(1)}, u32[]{:S(2)}, u32[]{:S(2)}) %all-to-all-start) | async-done | bytes 262176 | tf_op jit(solution)/shard_map/all_to_all | solution.py:353
  19.7 0.7 collective-permute-start
  20.4 0.6 pad_add_fusion.refs_2_.pos_ref
  21.0 0.6 copy-done.13
  21.6 5.9 %shard_map.96 = (f32[6,128,256]{2,1,0:T(8,128)}, f32[6,128,256]{2,1,0:T(8,128)}) custom-call(s32[16,9]{1,0:T(8,128)} %bitcast.14, s32[16,9]{1,0:T(8,128)} %copy-done.15, s32[3]{0:T(128)} %pad_add_fusion.refs_2_.pos_ref, f32[3]{0:T(128)} %scale_ref.1, f32[16,16,256]{2,1,0:T(8,128)} %copy-done, f32[3,2048]{1,0:T(4,128)} %copy-done.13, f32[1024,2048]{1,0:T(8,128)} %refs_6_.5, ...), custom_call_target="tpu_custom_call" | custom-call | tf_op jit(solution)/shard_map/pallas_call | solution.py:231
  27.5 6.4 %collective-permute-start.7 = (f32[6,128,256]{2,1,0:T(8,128)}, f32[6,128,256]{2,1,0:T(8,128)S(1)}, u32[]{:S(2)}, u32[]{:S(2)}) collective-permute-start(f32[6,128,256]{2,1,0:T(8,128)} %get-tuple-element.18.refs_1_), channel_id=1, source_target_pairs={{0,48},{1,49},{2,50},{3,51},{4,52},{5,53},{6,54},{7,55},{8,56},{9,... | collective-permute-start | bytes 2359304 | tf_op jit(solution)/shard_map/ppermute | solution.py:62
  33.8 7.8 %shard_map.95 = (f32[3,128,256]{2,1,0:T(8,128)}, f32[3,128,256]{2,1,0:T(8,128)}, f32[3,128,256]{2,1,0:T(8,128)}, f32[3,128,256]{2,1,0:T(8,128)}, f32[3,128,256]{...) custom-call(s32[16,9]{1,0:T(8,128)} %bitcast.15, s32[16,9]{1,0:T(8,128)} %copy-done.15, ...), custom_call_target="tpu_custom_call" | custom-call | tf_op jit(solution)/shard_map/pallas_call | solution.py:231
  41.7 4.2 %shard_map.94.base_ref.refs_10_ = f32[6,256,256]{2,1,0:T(8,128)} custom-call(s32[16,9]{1,0:T(8,128)} %bitcast.16, s32[16,9]{1,0:T(8,128)} %copy-done.15, s32[3]{0:T(128)} %pad_add_fusion.refs_2_.pos_ref, f32[3]{0:T(128)} %scale_ref.1, f32[16,16,256]{2,1,0:T(8,128)} %copy-done, f32[3,2048]{1,0:T(4,128)} %copy-done.13, f32[1024,2048]{1,0:T(8,128)} %refs_6_.5, ...), custom_call_target="tpu_custom_call" | custom-call | tf_op jit(solution)/shard_map/pallas_call | solution.py:231
  45.9 10.7 %gradients.1 = f32[4,2048]{1,0:T(4,128)} custom-call(s32[16,9]{1,0:T(8,128)} %bitcast.17, s32[16,9]{1,0:T(8,128)} %copy-done.15, s32[3]{0:T(128)} %pad_add_fusion.refs_2_.pos_ref, f32[3]{0:T(128)} %scale_ref.1, f32[16,16,256]{2,1,0:T(8,128)} %copy-done, f32[3,2048]{1,0:T(4,128)} %z_ref.1, f32[6,128,256]{2,1,0:T(8,128)} %get-tuple-element.14.refs_0_, ...), custom_call_target="tpu_custom_call" | custom-call | tf_op jit(solution)/shard_map/gradients/pallas_call | solution.py:301
  56.6 0.0 collective-permute-start.14
  56.6 1.4 %collective-permute-done.14 = f32[4,2048]{1,0:T(4,128)S(1)} collective-permute-done((f32[4,2048]{1,0:T(4,128)}, f32[4,2048]{1,0:T(4,128)S(1)}, u32[]{:S(2)}, u32[]{:S(2)}) %collective-permute-start.14) | collective-permute-done | bytes 32800 | tf_op jit(solution)/shard_map/ppermute | solution.py:62
  58.0 0.8 add.45
  58.8 0.1 collective-permute-start.15
  58.9 3.7 %collective-permute-start.10 = (f32[3,128,256]{2,1,0:T(8,128)}, f32[3,128,256]{2,1,0:T(8,128)}, u32[]{:S(2)}, u32[]{:S(2)}) collective-permute-start(f32[3,128,256]{2,1,0:T(8,128)} %get-tuple-element.20.refs_6_), channel_id=1, source_target_pairs={{0,48},{1,49},{2,50},{3,51},{4,52},{5,53},{6,54},{7,55},{8,56},{9,... | collective-permute-start | bytes 1179656 | tf_op jit(solution)/shard_map/ppermute | solution.py:62
  62.6 1.7 %collective-permute-done.15 = f32[4,2048]{1,0:T(4,128)S(1)} collective-permute-done((f32[4,2048]{1,0:T(4,128)S(1)}, f32[4,2048]{1,0:T(4,128)S(1)}, u32[]{:S(2)}, u32[]{:S(2)}) %collective-permute-start.15) | collective-permute-done | bytes 32800 | tf_op jit(solution)/shard_map/ppermute | solution.py:62
  64.3 0.1 collective-permute-start.16
  64.4 3.0 %collective-permute-start.17 = (f32[4,2048]{1,0:T(4,128)S(1)}, f32[4,2048]{1,0:T(4,128)S(1)}, u32[]{:S(2)}, u32[]{:S(2)}) collective-permute-start(f32[4,2048]{1,0:T(4,128)S(1)} %add.46), channel_id=1, source_target_pairs={{0,32},{1,33},{2,34},{3,35},{4,36},{5,37},{6,38},{7,39},{8,40},{9,... | collective-permute-start | bytes 98312 | tf_op jit(solution)/shard_map/ppermute | solution.py:62
  67.4 0.9 slice_add_fusion
  68.3 1.7 %collective-permute-start.18 = (f32[4,2048]{1,0:T(4,128)S(1)}, f32[4,2048]{1,0:T(4,128)S(1)}, u32[]{:S(2)}, u32[]{:S(2)}) collective-permute-start(f32[4,2048]{1,0:T(4,128)S(1)} %add.46), channel_id=1, source_target_pairs={{0,48},{1,49},{2,50},{3,51},{4,52},{5,53},{6,54},{7,55},{8,56},{9,... | collective-permute-start | bytes 98312 | tf_op jit(solution)/shard_map/ppermute | solution.py:62
  70.0 0.1 slice_add_fusion.1
  70.1 2.2 %collective-permute-done.16 = f32[4,2048]{1,0:T(4,128)S(1)} collective-permute-done((f32[4,2048]{1,0:T(4,128)S(1)}, f32[4,2048]{1,0:T(4,128)S(1)}, u32[]{:S(2)}, u32[]{:S(2)}) %collective-permute-start.16) | collective-permute-done | bytes 32800 | tf_op jit(solution)/shard_map/ppermute | solution.py:62
  72.3 2.5 %collective-permute-start.12 = (f32[3,128,256]{2,1,0:T(8,128)S(1)}, f32[3,128,256]{2,1,0:T(8,128)S(1)}, u32[]{:S(2)}, u32[]{:S(2)}) collective-permute-start(f32[3,128,256]{2,1,0:T(8,128)S(1)} %get-tuple-element.23), channel_id=1, source_target_pairs={{0,48},{1,49},{2,50},{3,51},{4,52},{5,53},{6,54},{7,55},{8,56},{9,... | collective-permute-start | bytes 1179656 | tf_op jit(solution)/shard_map/ppermute | solution.py:62
  74.8 1.3 collective-permute-done.18
  76.1 6.7 %collective-permute-done.12.refs_3_ = f32[3,128,256]{2,1,0:T(8,128)S(1)} collective-permute-done((f32[3,128,256]{2,1,0:T(8,128)S(1)}, f32[3,128,256]{2,1,0:T(8,128)S(1)}, u32[]{:S(2)}, u32[]{:S(2)}) %collective-permute-start.12) | collective-permute-done | bytes 393248 | tf_op jit(solution)/shard_map/ppermute | solution.py:62
  82.8 2.7 %collective-permute-done.9.refs_0_ = f32[3,128,256]{2,1,0:T(8,128)S(1)} collective-permute-done((f32[3,128,256]{2,1,0:T(8,128)S(1)}, f32[3,128,256]{2,1,0:T(8,128)S(1)}, u32[]{:S(2)}, u32[]{:S(2)}) %collective-permute-start.9) | collective-permute-done | bytes 393248 | tf_op jit(solution)/shard_map/ppermute | solution.py:62
  85.5 0.8 copy-done.12
  86.3 3.3 %shard_map.97 = f32[3,256,256]{2,1,0:T(8,128)} custom-call(s32[1,1]{1,0:T(1,128)S(6)} %copy.10.count_ref, f32[6,256,256]{2,1,0:T(8,128)} %shard_map.94.base_ref.refs_10_, f32[3,128,256]{2,1,0:T(8,128)} %copy-done.12, f32[3,128,256]{2,1,0:T(8,128)} %collective-permute-done.10.refs_1_, f32[3,128,256]{2,1,0:T(8,128)} %collective-permute-done.11.refs_2_, ...), custom_call_target="tpu_custom_call" | custom-call | tf_op jit(solution)/shard_map/pallas_call | solution.py:332
  89.6 1.2 collective-permute-start.13
  90.8 0.1 reduce_sum.9
  90.9 4.9 %collective-permute-start.19 = (f32[1,128]{1,0:T(1,128)S(1)}, f32[1,128]{1,0:T(1,128)S(1)}, u32[]{:S(2)}, u32[]{:S(2)}) collective-permute-start(f32[1,128]{1,0:T(1,128)S(1)} %pad_bitcast_fusion), channel_id=1, source_target_pairs={{0,1},{1,0},{2,3},{3,2},{4,5},{5,4},{6,7},{7,6},{8,9},{9,8},{10,11... | collective-permute-start | bytes 1544 | tf_op jit(solution)/shard_map/ppermute | solution.py:62
  95.8 6.8 %collective-permute-start.20 = (f32[1,128]{1,0:T(1,128)S(1)}, f32[1,128]{1,0:T(1,128)S(1)}, u32[]{:S(2)}, u32[]{:S(2)}) collective-permute-start(f32[1,128]{1,0:T(1,128)S(1)} %pad_bitcast_fusion), channel_id=1, source_target_pairs={{0,2},{1,3},{2,0},{3,1},{4,6},{5,7},{6,4},{7,5},{8,10},{9,11},{10,... | collective-permute-start | bytes 1544 | tf_op jit(solution)/shard_map/ppermute | solution.py:62
  102.7 1.5 %collective-permute-done.20 = f32[1,128]{1,0:T(1,128)S(1)} collective-permute-done((f32[1,128]{1,0:T(1,128)S(1)}, f32[1,128]{1,0:T(1,128)S(1)}, u32[]{:S(2)}, u32[]{:S(2)}) %collective-permute-start.20) | collective-permute-done | bytes 544 | tf_op jit(solution)/shard_map/ppermute | solution.py:62
  104.2 3.2 %collective-permute-done.21 = f32[1,128]{1,0:T(1,128)S(1)} collective-permute-done((f32[1,128]{1,0:T(1,128)S(1)}, f32[1,128]{1,0:T(1,128)S(1)}, u32[]{:S(2)}, u32[]{:S(2)}) %collective-permute-start.21) | collective-permute-done | bytes 544 | tf_op jit(solution)/shard_map/ppermute | solution.py:62
  107.5 1.1 collective-permute-start.5
  108.5 1.0 collective-permute-start.6
  109.6 2.2 %collective-permute-start.8 = (f32[3,128,256]{2,1,0:T(8,128)}, f32[3,128,256]{2,1,0:T(8,128)S(1)}, u32[]{:S(2)}, u32[]{:S(2)}) collective-permute-start(f32[3,128,256]{2,1,0:T(8,128)} %get-tuple-element.24), channel_id=1, source_target_pairs={{0,48},{1,49},{2,50},{3,51},{4,52},{5,53},{6,54},{7,55},{8,56},{9,... | collective-permute-start | bytes 1179656 | tf_op jit(solution)/shard_map/ppermute | solution.py:62
  111.8 0.5 slice_bitcast_fusion
  112.3 6.6 %collective-permute-done.5.refs_1_ = f32[3,128,256]{2,1,0:T(8,128)S(1)} collective-permute-done((f32[3,128,256]{2,1,0:T(8,128)}, f32[3,128,256]{2,1,0:T(8,128)S(1)}, u32[]{:S(2)}, u32[]{:S(2)}) %collective-permute-start.5) | collective-permute-done | bytes 393248 | tf_op jit(solution)/shard_map/ppermute | solution.py:62
  118.9 2.0 %collective-permute-done.6.refs_2_ = f32[3,128,256]{2,1,0:T(8,128)S(1)} collective-permute-done((f32[3,128,256]{2,1,0:T(8,128)S(1)}, f32[3,128,256]{2,1,0:T(8,128)S(1)}, u32[]{:S(2)}, u32[]{:S(2)}) %collective-permute-start.6) | collective-permute-done | bytes 393248 | tf_op jit(solution)/shard_map/ppermute | solution.py:62
  120.9 2.2 %collective-permute-done.8.refs_3_ = f32[3,128,256]{2,1,0:T(8,128)S(1)} collective-permute-done((f32[3,128,256]{2,1,0:T(8,128)}, f32[3,128,256]{2,1,0:T(8,128)S(1)}, u32[]{:S(2)}, u32[]{:S(2)}) %collective-permute-start.8) | collective-permute-done | bytes 393248 | tf_op jit(solution)/shard_map/ppermute | solution.py:62
  123.1 2.0 %collective-permute-done.4.refs_0_ = f32[3,128,256]{2,1,0:T(8,128)S(1)} collective-permute-done((f32[3,128,256]{2,1,0:T(8,128)S(1)}, f32[3,128,256]{2,1,0:T(8,128)S(1)}, u32[]{:S(2)}, u32[]{:S(2)}) %collective-permute-start.4) | collective-permute-done | bytes 393248 | tf_op jit(solution)/shard_map/ppermute | solution.py:62
  125.2 0.7 copy-done.11
  125.9 0.9 copy-done.5
  126.8 3.5 %shard_map.98 = f32[3,256,256]{2,1,0:T(8,128)} custom-call(s32[1,1]{1,0:T(1,128)S(6)} %copy.10.count_ref, f32[6,256,256]{2,1,0:T(8,128)} %shard_map.94.base_ref.refs_10_, f32[3,128,256]{2,1,0:T(8,128)} %copy-done.11, f32[3,128,256]{2,1,0:T(8,128)} %copy-done.7, f32[3,128,256]{2,1,0:T(8,128)} %copy-done.8, f32[3,128,256]{2,1,0:T(8,128)} %copy-done.9, ...), custom_call_target="tpu_custom_call" | custom-call | tf_op jit(solution)/shard_map/pallas_call | solution.py:332
  (55 shorter events, 0.2 us)
Async XLA Ops:
  0.6 20.3 %collective-permute-start.2 = (f32[1024,2048]{1,0:T(8,128)}, f32[1024,2048]{1,0:T(8,128)}, u32[]{:S(2)}, u32[]{:S(2)}) collective-permute-start(f32[1024,2048]{1,0:T(8,128)} %refs_6_.5), channel_id=1, source_target_pairs={{0,8},{1,9},{2,10},{3,11},{4,12},{5,13},{6,14},{7,15},{8,0},{9,1},... | collective-permute-start | bytes 25165832 | tf_op jit(solution)/shard_map/ppermute | solution.py:62
  2.9 16.8 %all-to-all-start = ((f32[16,16,256]{2,1,0:T(8,128)}), f32[16,16,256]{2,1,0:T(8,128)S(1)}, u32[]{:S(2)}, u32[]{:S(2)}) async-start(f32[16,16,256]{2,1,0:T(8,128)} %payload.1), calls=%async_computation | async-start | bytes 524288 | tf_op jit(solution)/shard_map/all_to_all | solution.py:353
  10.1 10.8 %collective-permute-start.1 = (f32[3,2048]{1,0:T(4,128)}, f32[3,2048]{1,0:T(4,128)S(1)}, u32[]{:S(2)}, u32[]{:S(2)}) collective-permute-start(f32[3,2048]{1,0:T(4,128)} %z_ref.1), channel_id=1, source_target_pairs={{0,0},{1,16},{2,32},{3,48},{4,64},{5,80},{6,96},{7,112},{8,8},{9,2... | collective-permute-start | bytes 73736 | tf_op jit(solution)/shard_map/ppermute | solution.py:62
  19.7 1.3 %copy-start = (f32[16,16,256]{2,1,0:T(8,128)}, f32[16,16,256]{2,1,0:T(8,128)S(1)}, u32[]{:S(2)}) copy-start(f32[16,16,256]{2,1,0:T(8,128)S(1)} %all-to-all-done.refs_4_.pay_ref) | copy-start | bytes 786436
  19.7 1.3 %copy-start.14 = (s32[16,1,9]{2,1,0:T(1,128)}, s32[16,1,9]{2,1,0:T(1,128)S(1)}, u32[]{:S(2)}) copy-start(s32[16,1,9]{2,1,0:T(1,128)S(1)} %slice_convert_fusion) | copy-start | bytes 1732
  19.7 1.3 collective-permute-start
  21.0 0.6 copy-start.13
  21.0 0.6 copy-start.15
  27.5 36.9 %collective-permute-start.7 = (f32[6,128,256]{2,1,0:T(8,128)}, f32[6,128,256]{2,1,0:T(8,128)S(1)}, u32[]{:S(2)}, u32[]{:S(2)}) collective-permute-start(f32[6,128,256]{2,1,0:T(8,128)} %get-tuple-element.18.refs_1_), channel_id=1, source_target_pairs={{0,48},{1,49},{2,50},{3,51},{4,52},{5,53},{6,54},{7,55},{8,56},{9,... | collective-permute-start | bytes 2359304 | tf_op jit(solution)/shard_map/ppermute | solution.py:62
  33.8 34.5 %collective-permute-start.3 = (f32[6,128,256]{2,1,0:T(8,128)}, f32[6,128,256]{2,1,0:T(8,128)S(1)}, u32[]{:S(2)}, u32[]{:S(2)}) collective-permute-start(f32[6,128,256]{2,1,0:T(8,128)} %get-tuple-element.14.refs_0_), channel_id=1, source_target_pairs={{0,16},{1,17},{2,18},{3,19},{4,20},{5,21},{6,22},{7,23},{8,24},{9,... | collective-permute-start | bytes 2359304 | tf_op jit(solution)/shard_map/ppermute | solution.py:62
  41.6 25.8 %copy-start.3 = (f32[3,128,256]{2,1,0:T(8,128)S(1)}, f32[3,128,256]{2,1,0:T(8,128)}, u32[]{:S(2)}) copy-start(f32[3,128,256]{2,1,0:T(8,128)} %get-tuple-element.22.refs_7_) | copy-start | bytes 1179652
  41.7 25.8 %copy-start.4 = (f32[3,128,256]{2,1,0:T(8,128)S(1)}, f32[3,128,256]{2,1,0:T(8,128)}, u32[]{:S(2)}) copy-start(f32[3,128,256]{2,1,0:T(8,128)} %get-tuple-element.17.refs_9_) | copy-start | bytes 1179652
  45.8 24.2 %copy-start.1 = (f32[3,128,256]{2,1,0:T(8,128)S(1)}, f32[3,128,256]{2,1,0:T(8,128)}, u32[]{:S(2)}) copy-start(f32[3,128,256]{2,1,0:T(8,128)} %get-tuple-element.19.refs_2_) | copy-start | bytes 1179652
  45.9 24.1 %copy-start.2 = (f32[3,128,256]{2,1,0:T(8,128)S(1)}, f32[3,128,256]{2,1,0:T(8,128)}, u32[]{:S(2)}) copy-start(f32[3,128,256]{2,1,0:T(8,128)} %get-tuple-element.13.refs_4_) | copy-start | bytes 1179652
  45.9 62.7 %copy-start.6 = (f32[3,128,256]{2,1,0:T(8,128)S(1)}, f32[3,128,256]{2,1,0:T(8,128)}, u32[]{:S(2)}) copy-start(f32[3,128,256]{2,1,0:T(8,128)} %get-tuple-element.16.refs_5_) | copy-start | bytes 1179652
  56.6 1.4 %collective-permute-start.14 = (f32[4,2048]{1,0:T(4,128)}, f32[4,2048]{1,0:T(4,128)S(1)}, u32[]{:S(2)}, u32[]{:S(2)}) collective-permute-start(f32[4,2048]{1,0:T(4,128)} %gradients.1), channel_id=1, source_target_pairs={{0,8},{1,9},{2,10},{3,11},{4,12},{5,13},{6,14},{7,15},{8,0},{9,1},... | collective-permute-start | bytes 98312 | tf_op jit(solution)/shard_map/ppermute | solution.py:62
  58.8 5.5 %collective-permute-start.15 = (f32[4,2048]{1,0:T(4,128)S(1)}, f32[4,2048]{1,0:T(4,128)S(1)}, u32[]{:S(2)}, u32[]{:S(2)}) collective-permute-start(f32[4,2048]{1,0:T(4,128)S(1)} %add.45), channel_id=1, source_target_pairs={{0,64},{1,65},{2,66},{3,67},{4,68},{5,69},{6,70},{7,71},{8,72},{9,... | collective-permute-start | bytes 98312 | tf_op jit(solution)/shard_map/ppermute | solution.py:62
  58.9 17.2 %collective-permute-start.10 = (f32[3,128,256]{2,1,0:T(8,128)}, f32[3,128,256]{2,1,0:T(8,128)}, u32[]{:S(2)}, u32[]{:S(2)}) collective-permute-start(f32[3,128,256]{2,1,0:T(8,128)} %get-tuple-element.20.refs_6_), channel_id=1, source_target_pairs={{0,48},{1,49},{2,50},{3,51},{4,52},{5,53},{6,54},{7,55},{8,56},{9,... | collective-permute-start | bytes 1179656 | tf_op jit(solution)/shard_map/ppermute | solution.py:62
  62.6 13.5 %collective-permute-start.11 = (f32[3,128,256]{2,1,0:T(8,128)}, f32[3,128,256]{2,1,0:T(8,128)}, u32[]{:S(2)}, u32[]{:S(2)}) collective-permute-start(f32[3,128,256]{2,1,0:T(8,128)} %get-tuple-element.21.refs_3_), channel_id=1, source_target_pairs={{0,16},{1,17},{2,18},{3,19},{4,20},{5,21},{6,22},{7,23},{8,24},{9,... | collective-permute-start | bytes 1179656 | tf_op jit(solution)/shard_map/ppermute | solution.py:62
  64.3 8.0 %collective-permute-start.16 = (f32[4,2048]{1,0:T(4,128)S(1)}, f32[4,2048]{1,0:T(4,128)S(1)}, u32[]{:S(2)}, u32[]{:S(2)}) collective-permute-start(f32[4,2048]{1,0:T(4,128)S(1)} %add.46), channel_id=1, source_target_pairs={{0,16},{1,17},{2,18},{3,19},{4,20},{5,21},{6,22},{7,23},{8,24},{9,... | collective-permute-start | bytes 98312 | tf_op jit(solution)/shard_map/ppermute | solution.py:62
  64.4 10.4 %collective-permute-start.17 = (f32[4,2048]{1,0:T(4,128)S(1)}, f32[4,2048]{1,0:T(4,128)S(1)}, u32[]{:S(2)}, u32[]{:S(2)}) collective-permute-start(f32[4,2048]{1,0:T(4,128)S(1)} %add.46), channel_id=1, source_target_pairs={{0,32},{1,33},{2,34},{3,35},{4,36},{5,37},{6,38},{7,39},{8,40},{9,... | collective-permute-start | bytes 98312 | tf_op jit(solution)/shard_map/ppermute | solution.py:62
  68.3 7.8 %collective-permute-start.18 = (f32[4,2048]{1,0:T(4,128)S(1)}, f32[4,2048]{1,0:T(4,128)S(1)}, u32[]{:S(2)}, u32[]{:S(2)}) collective-permute-start(f32[4,2048]{1,0:T(4,128)S(1)} %add.46), channel_id=1, source_target_pairs={{0,48},{1,49},{2,50},{3,51},{4,52},{5,53},{6,54},{7,55},{8,56},{9,... | collective-permute-start | bytes 98312 | tf_op jit(solution)/shard_map/ppermute | solution.py:62
  72.3 10.5 %collective-permute-start.12 = (f32[3,128,256]{2,1,0:T(8,128)S(1)}, f32[3,128,256]{2,1,0:T(8,128)S(1)}, u32[]{:S(2)}, u32[]{:S(2)}) collective-permute-start(f32[3,128,256]{2,1,0:T(8,128)S(1)} %get-tuple-element.23), channel_id=1, source_target_pairs={{0,48},{1,49},{2,50},{3,51},{4,52},{5,53},{6,54},{7,55},{8,56},{9,... | collective-permute-start | bytes 1179656 | tf_op jit(solution)/shard_map/ppermute | solution.py:62
  74.8 10.7 %collective-permute-start.9 = (f32[3,128,256]{2,1,0:T(8,128)S(1)}, f32[3,128,256]{2,1,0:T(8,128)S(1)}, u32[]{:S(2)}, u32[]{:S(2)}) collective-permute-start(f32[3,128,256]{2,1,0:T(8,128)S(1)} %get-tuple-element.25), channel_id=1, source_target_pairs={{0,16},{1,17},{2,18},{3,19},{4,20},{5,21},{6,22},{7,23},{8,24},{9,... | collective-permute-start | bytes 1179656 | tf_op jit(solution)/shard_map/ppermute | solution.py:62
  76.1 54.2 %copy-start.16 = (f32[4,2048]{1,0:T(4,128)}, f32[4,2048]{1,0:T(4,128)S(1)}, u32[]{:S(2)}) copy-start(f32[4,2048]{1,0:T(4,128)S(1)} %add_add_fusion) | copy-start | bytes 98308
  82.8 2.7 %copy-start.10 = (f32[3,128,256]{2,1,0:T(8,128)}, f32[3,128,256]{2,1,0:T(8,128)S(1)}, u32[]{:S(2)}) copy-start(f32[3,128,256]{2,1,0:T(8,128)S(1)} %collective-permute-done.12.refs_3_) | copy-start | bytes 1179652
  85.5 0.8 copy-start.12
  89.6 35.6 %collective-permute-start.13 = (f32[3,256,256]{2,1,0:T(8,128)}, f32[3,256,256]{2,1,0:T(8,128)S(1)}, u32[]{:S(2)}, u32[]{:S(2)}) collective-permute-start(f32[3,256,256]{2,1,0:T(8,128)} %shard_map.97), channel_id=1, source_target_pairs={{0,64},{1,65},{2,66},{3,67},{4,68},{5,69},{6,70},{7,71},{8,72},{9,... | collective-permute-start | bytes 2359304 | tf_op jit(solution)/shard_map/ppermute | solution.py:62
  90.9 11.8 %collective-permute-start.19 = (f32[1,128]{1,0:T(1,128)S(1)}, f32[1,128]{1,0:T(1,128)S(1)}, u32[]{:S(2)}, u32[]{:S(2)}) collective-permute-start(f32[1,128]{1,0:T(1,128)S(1)} %pad_bitcast_fusion), channel_id=1, source_target_pairs={{0,1},{1,0},{2,3},{3,2},{4,5},{5,4},{6,7},{7,6},{8,9},{9,8},{10,11... | collective-permute-start | bytes 1544 | tf_op jit(solution)/shard_map/ppermute | solution.py:62
  95.8 8.4 %collective-permute-start.20 = (f32[1,128]{1,0:T(1,128)S(1)}, f32[1,128]{1,0:T(1,128)S(1)}, u32[]{:S(2)}, u32[]{:S(2)}) collective-permute-start(f32[1,128]{1,0:T(1,128)S(1)} %pad_bitcast_fusion), channel_id=1, source_target_pairs={{0,2},{1,3},{2,0},{3,1},{4,6},{5,7},{6,4},{7,5},{8,10},{9,11},{10,... | collective-permute-start | bytes 1544 | tf_op jit(solution)/shard_map/ppermute | solution.py:62
  102.7 4.8 %collective-permute-start.21 = (f32[1,128]{1,0:T(1,128)S(1)}, f32[1,128]{1,0:T(1,128)S(1)}, u32[]{:S(2)}, u32[]{:S(2)}) collective-permute-start(f32[1,128]{1,0:T(1,128)S(1)} %pad_bitcast_fusion), channel_id=1, source_target_pairs={{0,3},{1,2},{2,1},{3,0},{4,7},{5,6},{6,5},{7,4},{8,11},{9,10},{10,... | collective-permute-start | bytes 1544 | tf_op jit(solution)/shard_map/ppermute | solution.py:62
  107.5 4.3 %collective-permute-start.22 = (f32[1,128]{1,0:T(1,128)S(1)}, f32[1,128]{1,0:T(1,128)S(1)}, u32[]{:S(2)}, u32[]{:S(2)}) collective-permute-start(f32[1,128]{1,0:T(1,128)S(1)} %add_add_fusion.1), channel_id=1, source_target_pairs={{0,4},{1,5},{2,6},{3,7},{4,0},{5,1},{6,2},{7,3},{8,12},{9,13},{10,... | collective-permute-start | bytes 1544 | tf_op jit(solution)/shard_map/ppermute | solution.py:62
  107.5 11.5 %collective-permute-start.5 = (f32[3,128,256]{2,1,0:T(8,128)}, f32[3,128,256]{2,1,0:T(8,128)S(1)}, u32[]{:S(2)}, u32[]{:S(2)}) collective-permute-start(f32[3,128,256]{2,1,0:T(8,128)} %get-tuple-element.15.refs_8_), channel_id=1, source_target_pairs={{0,48},{1,49},{2,50},{3,51},{4,52},{5,53},{6,54},{7,55},{8,56},{9,... | collective-permute-start | bytes 1179656 | tf_op jit(solution)/shard_map/ppermute | solution.py:62
  108.5 12.4 %collective-permute-start.6 = (f32[3,128,256]{2,1,0:T(8,128)S(1)}, f32[3,128,256]{2,1,0:T(8,128)S(1)}, u32[]{:S(2)}, u32[]{:S(2)}) collective-permute-start(f32[3,128,256]{2,1,0:T(8,128)S(1)} %copy-done.6), channel_id=1, source_target_pairs={{0,16},{1,17},{2,18},{3,19},{4,20},{5,21},{6,22},{7,23},{8,24},{9,... | collective-permute-start | bytes 1179656 | tf_op jit(solution)/shard_map/ppermute | solution.py:62
  109.6 13.6 %collective-permute-start.8 = (f32[3,128,256]{2,1,0:T(8,128)}, f32[3,128,256]{2,1,0:T(8,128)S(1)}, u32[]{:S(2)}, u32[]{:S(2)}) collective-permute-start(f32[3,128,256]{2,1,0:T(8,128)} %get-tuple-element.24), channel_id=1, source_target_pairs={{0,48},{1,49},{2,50},{3,51},{4,52},{5,53},{6,54},{7,55},{8,56},{9,... | collective-permute-start | bytes 1179656 | tf_op jit(solution)/shard_map/ppermute | solution.py:62
  111.8 13.4 %collective-permute-start.4 = (f32[3,128,256]{2,1,0:T(8,128)S(1)}, f32[3,128,256]{2,1,0:T(8,128)S(1)}, u32[]{:S(2)}, u32[]{:S(2)}) collective-permute-start(f32[3,128,256]{2,1,0:T(8,128)S(1)} %get-tuple-element.26), channel_id=1, source_target_pairs={{0,16},{1,17},{2,18},{3,19},{4,20},{5,21},{6,22},{7,23},{8,24},{9,... | collective-permute-start | bytes 1179656 | tf_op jit(solution)/shard_map/ppermute | solution.py:62
  118.9 6.2 %copy-start.7 = (f32[3,128,256]{2,1,0:T(8,128)}, f32[3,128,256]{2,1,0:T(8,128)S(1)}, u32[]{:S(2)}) copy-start(f32[3,128,256]{2,1,0:T(8,128)S(1)} %collective-permute-done.5.refs_1_) | copy-start | bytes 1179652
  120.9 4.2 %copy-start.8 = (f32[3,128,256]{2,1,0:T(8,128)}, f32[3,128,256]{2,1,0:T(8,128)S(1)}, u32[]{:S(2)}) copy-start(f32[3,128,256]{2,1,0:T(8,128)S(1)} %collective-permute-done.6.refs_2_) | copy-start | bytes 1179652
  123.1 2.0 %copy-start.9 = (f32[3,128,256]{2,1,0:T(8,128)}, f32[3,128,256]{2,1,0:T(8,128)S(1)}, u32[]{:S(2)}) copy-start(f32[3,128,256]{2,1,0:T(8,128)S(1)} %collective-permute-done.8.refs_3_) | copy-start | bytes 1179652
  125.1 0.8 copy-start.11
  125.9 0.9 copy-start.5

commit v3 on v2

--- a/solution.py
+++ b/solution.py
@@ -97,18 +97,34 @@
     return group, slot, col, near, (live * found) > 0
 
 
-def scaled_points(pay_ref, group, slot, z_ref, start, scale_ref):
-    rolled = pltpu.roll(pay_ref[group], lax.rem(16 - 4 * slot, 16), 0)
-    padded = jnp.concatenate([rolled[0:8], jnp.zeros((120, BS), jnp.float32)], axis=0)
-    x_cols = jnp.transpose(padded)
+def column_kernel(pos_ref, scale_ref, pay_ref, out_ref):
+    lane = lax.broadcasted_iota(jnp.int32, (1, 128), 1)
+    inverse = jnp.zeros((1, 128), jnp.float32)
+    for q in range(3):
+        inverse = jnp.where(lane == q, 1.0 / scale_ref[q], inverse)
+    for chip in range(8):
+        padded = jnp.concatenate([pay_ref[2 * chip + pos_ref[2]], jnp.zeros((112, BS), jnp.float32)], axis=0)
+        turned = jnp.transpose(padded)
+        for slot in range(SLOTS):
+            shifted = turned if slot == 0 else pltpu.roll(turned, 128 - 4 * slot, 1)
+            out_ref[chip, slot] = shifted * inverse
+
+
+def scaled_points(cols_ref, group, slot, z_ref, start, scale_ref):
     z_rows = z_ref[:, pl.ds(pl.multiple_of(start, BS), BS)]
-    inverses = [1.0 / scale_ref[q] for q in range(3)]
-    return [x_cols[:, q : q + 1] * inverses[q] for q in range(3)], [z_rows[q : q + 1, :] * inverses[q] for q in range(3)]
+    z_rows = [z_rows[q : q + 1, :] * (1.0 / scale_ref[q]) for q in range(3)]
+
+    def x_strip(row):
+        block = cols_ref[group // 2, slot, pl.ds(row, STRIP), :]
+        return [block[:, q : q + 1] for q in range(3)]
+
+    return x_strip, z_rows
 
 
 def strip_offsets(points, row):
-    x_cols, z_rows = points
-    return [x_cols[q][row : row + STRIP] - z_rows[q] for q in range(3)]
+    x_strip, z_rows = points
+    x_cols = x_strip(row)
+    return [x_cols[q] - z_rows[q] for q in range(3)]
 
 
 def radius_of(offsets):
@@ -127,33 +143,19 @@
 
 
 def product_kernel(steps, form, own_ref, near_ref, pos_ref, scale_ref, pay_ref, z_ref, mine_ref, mate_ref, *refs):
-    *outs, tiles, results, left, right, in_sems, out_sems = refs
+    *outs, tiles, left, right, in_sems = refs
 
     def copy_in(source, row, col, place):
         window = source.at[pl.ds(row * BS, BS), pl.ds(col * BS, BS)]
         return pltpu.make_async_copy(window, tiles.at[place], in_sems.at[place])
 
-    def copy_half(place, half, out, index):
-        window = results.at[place, pl.ds(half * HALF, HALF)]
-        return pltpu.make_async_copy(window, out.at[index], out_sems.at[place, half])
-
-    def copy_out(number, local, place):
+    def store(number, own_x, slot, half, value):
         if form == "whole":
-            for half in range(2):
-                window = outs[0].at[local, pl.ds(half * HALF, HALF)]
-                source = results.at[place, pl.ds(half * HALF, HALF)]
-                pltpu.make_async_copy(source, window, out_sems.at[place, half]).start()
+            outs[0][own_x * SLOTS + slot, pl.ds(half * HALF, HALF), :] = value
         elif form == "halves":
-            for half in range(2):
-                copy_half(place, half, outs[half], local).start()
+            outs[half][own_x * SLOTS + slot] = value
         else:
-            for own_x in range(2):
-
-                @pl.when(local // SLOTS == own_x)
-                def _():
-                    for half in range(2):
-                        out = outs[4 * number + 2 * own_x + half]
-                        copy_half(place, half, out, local % SLOTS).start()
+            outs[4 * number + 2 * own_x + half][slot] = value
 
     for number, step in enumerate(steps):
         for local in range(COUNT):
@@ -170,51 +172,57 @@
             def _():
                 copy_in(mate_ref, row, col, place).start()
 
-    for number, step in enumerate(steps):
-
-        def body(local, carry):
+    def block(number, step, own_x):
+        def body(slot, carry):
+            local = own_x * SLOTS + slot
             place = number * COUNT + local
-            group, slot, _, near, active = slot_of(local, step, own_ref, near_ref, pos_ref)
+            group, _, _, near, active = slot_of(local, step, own_ref, near_ref, pos_ref)
 
             @pl.when(active)
             def _():
                 points = scaled_points(pay_ref, group, slot, z_ref, near * BS, scale_ref)
-                for row in range(0, BS, STRIP):
-                    rows = slice(row, row + STRIP)
-                    radius = radius_of(strip_offsets(points, row))
-                    remain = jnp.maximum(1.0 - radius, 0.0)
-                    square = remain * remain
-                    high, low = split(square * square * (4.0 * radius + 1.0))
-                    left[rows, 0:BS] = high
-                    left[rows, BS : 2 * BS] = low
-                    left[rows, 2 * BS : 3 * BS] = high
                 copy_in(mine_ref, 0, 0, place).wait()
                 for row in range(0, BS, STRIP):
                     high, low = split(tiles[place, pl.ds(row, STRIP), :])
                     right[row : row + STRIP, :] = low
                     right[BS + row : BS + row + STRIP, :] = high
                     right[2 * BS + row : 2 * BS + row + STRIP, :] = high
-                results[place] = jnp.dot(left[...], right[...], preferred_element_type=jnp.float32)
+                for half in range(2):
+                    for row in range(half * HALF, (half + 1) * HALF, STRIP):
+                        rows = slice(row, row + STRIP)
+                        radius = radius_of(strip_offsets(points, row))
+                        remain = jnp.maximum(1.0 - radius, 0.0)
+                        square = remain * remain
+                        high, low = split(square * square * (4.0 * radius + 1.0))
+                        left[rows, 0:BS] = high
+                        left[rows, BS : 2 * BS] = low
+                        left[rows, 2 * BS : 3 * BS] = high
+                    rows = pl.ds(half * HALF, HALF)
+                    value = jnp.dot(left[rows, :], right[...], preferred_element_type=jnp.float32)
+                    store(number, own_x, slot, half, value)
 
             @pl.when(jnp.logical_not(active))
             def _():
-                results[place] = jnp.zeros((BS, BS), jnp.float32)
-
-            copy_out(number, local, place)
+                for half in range(2):
+                    store(number, own_x, slot, half, jnp.zeros((HALF, BS), jnp.float32))
+
             return carry
 
-        lax.fori_loop(0, COUNT, body, 0)
-
-    for place in range(COUNT * len(steps)):
-        for half in range(2):
-            window = results.at[place, pl.ds(half * HALF, HALF)]
-            other = results.at[place, pl.ds((1 - half) * HALF, HALF)]
-            pltpu.make_async_copy(window, other, out_sems.at[place, half]).wait()
+        lax.fori_loop(0, SLOTS, body, 0)
+
+    for number, step in enumerate(steps):
+        for own_x in range(2):
+            block(number, step, own_x)
+
+
+def grant(mebibytes):
+    return pltpu.CompilerParams(vmem_limit_bytes=mebibytes << 20)
 
 
 SMEM = pl.BlockSpec(memory_space=pltpu.SMEM)
 VMEM = pl.BlockSpec(memory_space=pltpu.VMEM)
 HBM = pl.BlockSpec(memory_space=pl.ANY)
+FAR_MEMORY = pl.BlockSpec(memory_space=pltpu.HBM)
 
 
 def products(steps, form, tables, scales, payload, z_near, mine, mate):
@@ -230,17 +238,16 @@
 
     return pl.pallas_call(
         kernel,
-        out_shape=[jax.ShapeDtypeStruct(shape, jnp.float32) for shape in shapes],
-        in_specs=[SMEM, SMEM, SMEM, SMEM, VMEM, VMEM, HBM, HBM],
-        out_specs=[HBM] * len(shapes),
+        out_shape=[pltpu.VMEM(shape, jnp.float32) for shape in shapes],
+        in_specs=[SMEM, SMEM, SMEM, SMEM, VMEM, VMEM, FAR_MEMORY, FAR_MEMORY],
+        out_specs=[VMEM] * len(shapes),
         scratch_shapes=[
-            pltpu.VMEM((number, BS, BS), jnp.float32),
             pltpu.VMEM((number, BS, BS), jnp.float32),
             pltpu.VMEM((BS, 3 * BS), jnp.bfloat16),
             pltpu.VMEM((3 * BS, BS), jnp.bfloat16),
             pltpu.SemaphoreType.DMA((number,)),
-            pltpu.SemaphoreType.DMA((number, 2)),
         ],
+        compiler_params=grant(4 + number),
     )(*tables, scales, payload, z_near, mine, mate)
 
 
@@ -304,42 +311,64 @@
         in_specs=[SMEM, SMEM, SMEM, SMEM, VMEM, VMEM] + [VMEM] * len(parts),
         out_specs=VMEM,
         name="gradients",
+        compiler_params=grant(16),
     )(*tables, scales, payload, z_own, *parts)
 
 
-def combine_kernel(base_ref, tops, bottoms, extra, count_ref, out_ref):
-    slot = pl.program_id(0)
-    keep = count_ref[0, 0] > slot
-    for half, pieces in enumerate((tops, bottoms)):
-        rows = pl.ds(half * HALF, HALF)
-        total = base_ref[0, rows, :]
-        for piece in pieces:
-            total = total + piece[0]
+def combine_kernel(first, count_ref, base_ref, *refs):
+    *pieces, out_ref, base, halves, total, in_sems, out_sems = refs
+    extra = pieces[4] if len(pieces) == 5 else None
+
+    def copies(slot):
+        made = [pltpu.make_async_copy(base_ref.at[first + slot], base.at[0, slot], in_sems.at[slot, 0])]
+        for number in range(4):
+            made.append(pltpu.make_async_copy(pieces[number].at[slot], halves.at[number, slot], in_sems.at[slot, 1 + number]))
         if extra is not None:
-            total = jnp.where(keep, total + extra[0, rows, :], 0.0)
-        out_ref[0, rows, :] = total
+            made.append(pltpu.make_async_copy(extra.at[slot], base.at[1, slot], in_sems.at[slot, 5]))
+        return made
+
+    for slot in range(SLOTS):
+        for copy in copies(slot):
+            copy.start()
+    for slot in range(SLOTS):
+        for copy in copies(slot):
+            copy.wait()
+        for half in range(2):
+            rows = pl.ds(half * HALF, HALF)
+            value = base[0, slot, rows, :] + halves[2 * half, slot] + halves[2 * half + 1, slot]
+            if extra is not None:
+                value = jnp.where(count_ref[0, 0] > slot, value + base[1, slot, rows, :], 0.0)
+            total[slot, rows, :] = value
+        pltpu.make_async_copy(total.at[slot], out_ref.at[slot], out_sems.at[slot]).start()
+    for slot in range(SLOTS):
+        pltpu.make_async_copy(total.at[slot], out_ref.at[slot], out_sems.at[slot]).wait()
 
 
 def combine(base, first, tops, bottoms, extra, count):
-    whole = pl.BlockSpec((1, BS, BS), lambda s: (s, 0, 0))
-    half = pl.BlockSpec((1, HALF, BS), lambda s: (s, 0, 0))
     extras = [] if extra is None else [extra]
 
-    def kernel(count_ref, base_ref, *refs):
-        extra_ref = refs[4] if extras else None
-        combine_kernel(base_ref, refs[0:2], refs[2:4], extra_ref, count_ref, refs[-1])
+    def kernel(*refs):
+        combine_kernel(first, *refs)
 
     return pl.pallas_call(
         kernel,
-        grid=(SLOTS,),
         out_shape=jax.ShapeDtypeStruct((SLOTS, BS, BS), jnp.float32),
-        in_specs=[SMEM, pl.BlockSpec((1, BS, BS), lambda s: (s + first, 0, 0))] + [half] * 4 + [whole] * len(extras),
-        out_specs=whole,
+        in_specs=[SMEM] + [HBM] * (5 + len(extras)),
+        out_specs=HBM,
+        scratch_shapes=[
+            pltpu.VMEM((1 + len(extras), SLOTS, BS, BS), jnp.float32),
+            pltpu.VMEM((4, SLOTS, HALF, BS), jnp.float32),
+            pltpu.VMEM((SLOTS, BS, BS), jnp.float32),
+            pltpu.SemaphoreType.DMA((SLOTS, 6)),
+            pltpu.SemaphoreType.DMA((SLOTS,)),
+        ],
+        compiler_params=grant(8),
     )(count, base, *tops, *bottoms, *extras)
 
 
 def on_device(x_points, z_points, length_scales, dpsi_grad, block_rows, block_cols, block_count):
     xh, y, core = (lax.axis_index(name).astype(jnp.int32) for name in DP)
+    length_scales = pltpu.with_memory_space_constraint(length_scales, pltpu.HBM)
     mate = permute(dpsi_grad, SWAP_CORE)
     z_near = permute(z_points, TRANSPOSE)
     outgoing = pl.pallas_call(
@@ -349,13 +378,23 @@
         out_specs=VMEM,
         scratch_shapes=[pltpu.VMEM((16, BS), jnp.float32)],
         name="payload",
+        compiler_params=grant(58),
     )(block_rows, block_cols, block_count, x_points)
     payload = lax.all_to_all(outgoing, DP, 0, 0, tiled=True)
     own_table = payload[:, 12, :9].astype(jnp.int32)
     near_table = permute(own_table, TRANSPOSE)
     tables = (own_table, near_table, jnp.stack([xh, y, core]))
 
-    args = (tables, length_scales, payload, z_near, dpsi_grad, mate)
+    columns = pl.pallas_call(
+        column_kernel,
+        out_shape=pltpu.VMEM((8, SLOTS, BS, 128), jnp.float32),
+        in_specs=[SMEM, SMEM, VMEM],
+        out_specs=VMEM,
+        name="columns",
+        compiler_params=grant(8),
+    )(tables[2], length_scales, payload)
+    mine = pltpu.with_memory_space_constraint(dpsi_grad, pltpu.HBM)
+    args = (tables, length_scales, columns, z_near, mine, mate)
     far = products((2,), "halves", *args)
     got_up = permute(far[0], Y_UP)
     got_down = permute(far[1], Y_DOWN)
@@ -364,7 +403,7 @@
     direct_up_o = permute(up_o[1], Y_UP)
     direct_down_o = permute(down_o[0], Y_DOWN)
     (here,) = products((0,), "whole", *args)
-    local = gradients(tables, length_scales, payload, z_points, (*far, *sides, here))
+    local = gradients(tables, length_scales, columns, z_points, (*far, *sides, here))
     sum_up_o = permute(up_o[0] + got_up[:SLOTS], Y_UP)
     sum_down_o = permute(down_o[1] + got_down[:SLOTS], Y_DOWN)
     direct_up_w = permute(up_w[1], Y_UP)

time: 131 us -> 118 us (0.901)
  Pallas kernels: 36.9 us -> 29.9 us
  local copies, waits for them, and re-layouts: 3.55 us -> 0.58 us
  starting transfers between devices: 44.1 us -> 42.1 us
    pallas_call x1, Pallas kernels: 10.7 us -> 6.66 us  [gradients(): pl.pallas_call(gradient_kernel, out_shape=jax.ShapeDtypeStruct((4, z_own....]
    unnamed x34 -> x6, local copies, waits for them, and re-layouts: 3 us -> 0.02 us
    pallas_call x5 -> x6, Pallas kernels: 24.7 us -> 21.7 us  [the longest x3 14.4 us: products(): pl.pallas_call(kernel, out_shape=[pltpu.VMEM(shape, jnp.float32) for shap...]
    ppermute x23, starting transfers between devices: 36.8 us -> 34.8 us  [permute(): return lax.ppermute(value, AXES, perm)]
  transfers between devices with their start and end apart: 24 -> 24, of which waited for: 13 -> 14; matrix products, arithmetic and copies ran while one was open for 2% -> 2% of each run, Pallas kernels for 19% -> 17%
where the time goes in v3:
time: 118 us; the launch traced here: 117 us
  starting transfers between devices  42.1 us (36%)
  waiting for transfers between devices  41.1 us (35%)
  Pallas kernels  29.9 us (25%)
  other arithmetic  1.95 us (2%)
  between operations  1.65 us (1%)
    ppermute x23, starting transfers between devices, permute(): return lax.ppermute(value, AXES, perm)  34.8 us
    ppermute x23, waiting for transfers between devices, permute(): return lax.ppermute(value, AXES, perm)  33 us
    pallas_call x3, Pallas kernels, products(): pl.pallas_call(kernel, out_shape=[pltpu.VMEM(shape, jnp.float32) for shap...  14.4 us
    all_to_all x1, waiting for transfers between devices, on_device(): payload = lax.all_to_all(outgoing, DP, 0, 0, tiled=True)  8.1 us
    all_to_all x1, starting transfers between devices, on_device(): payload = lax.all_to_all(outgoing, DP, 0, 0, tiled=True)  7.25 us
    pallas_call x1, Pallas kernels, gradients(): pl.pallas_call(gradient_kernel, out_shape=jax.ShapeDtypeStruct((4, z_own....  6.66 us
    pallas_call x2, Pallas kernels, combine(): pl.pallas_call(kernel, out_shape=jax.ShapeDtypeStruct((SLOTS, BS, BS), jn...  5.72 us
  transfers between devices with their start and end apart: 24, of which 14 were waited for; matrix products, arithmetic and copies ran while one was open for 2% of the time, Pallas kernels for 17%

profile of v3, /device:TPU:0, one launch (start us, length us, event | category | flops | bytes accessed | tf_op | source)
XLA Modules:
  0.0 117.3 jit_solution(4095526876068563388)
XLA Ops:
  0.6 0.1 collective-permute-start.2
  1.4 1.5 %payload.1 = f32[16,16,256]{2,1,0:T(8,128)} custom-call(s32[1,1,3]{2,1,0:T(1,128)} %rows_ref.1, s32[1,1,3]{2,1,0:T(1,128)} %cols_ref.1, s32[1,1]{1,0:T(1,128)S(6)} %copy.14.count_ref.refs_0_, f32[3,2048]{1,0:T(4,128)} %x_ref.1), custom_call_target="tpu_custom_call" | custom-call | tf_op jit(solution)/shard_map/payload/pallas_call | solution.py:374
  2.9 7.3 %all-to-all-start = ((f32[16,16,256]{2,1,0:T(8,128)}), f32[16,16,256]{2,1,0:T(8,128)S(1)}, u32[]{:S(2)}, u32[]{:S(2)}) async-start(f32[16,16,256]{2,1,0:T(8,128)} %payload.1), calls=%async_computation | async-start | bytes 524288 | tf_op jit(solution)/shard_map/all_to_all | solution.py:383
  10.1 1.4 %collective-permute-start.1 = (f32[3,2048]{1,0:T(4,128)}, f32[3,2048]{1,0:T(4,128)S(1)}, u32[]{:S(2)}, u32[]{:S(2)}) collective-permute-start(f32[3,2048]{1,0:T(4,128)} %z_ref.1), channel_id=1, source_target_pairs={{0,0},{1,16},{2,32},{3,48},{4,64},{5,80},{6,96},{7,112},{8,8},{9,2... | collective-permute-start | bytes 73736 | tf_op jit(solution)/shard_map/ppermute | solution.py:62
  11.6 8.1 %all-to-all-done.pay_ref = f32[16,16,256]{2,1,0:T(8,128)S(1)} async-done(((f32[16,16,256]{2,1,0:T(8,128)}), f32[16,16,256]{2,1,0:T(8,128)S(1)}, u32[]{:S(2)}, u32[]{:S(2)}) %all-to-all-start) | async-done | bytes 262176 | tf_op jit(solution)/shard_map/all_to_all | solution.py:383
  19.7 0.7 collective-permute-start
  20.4 0.1 pad_add_fusion.pos_ref.refs_2_
  20.4 1.6 %columns.1.refs_4_.pay_ref = f32[8,3,256,128]{3,2,1,0:T(8,128)S(1)} custom-call(s32[3]{0:T(128)S(1)} %pad_add_fusion.pos_ref.refs_2_, f32[3]{0:T(128)} %scale_ref.3, f32[16,16,256]{2,1,0:T(8,128)S(1)} %all-to-all-done.pay_ref), custom_call_target="tpu_custom_call" | custom-call | tf_op jit(solution)/shard_map/columns/pallas_call | solution.py:388
  22.1 4.8 %shard_map.96 = (f32[6,128,256]{2,1,0:T(8,128)S(1)}, f32[6,128,256]{2,1,0:T(8,128)S(1)}) custom-call(s32[16,9]{1,0:T(8,128)S(1)} %convert_bitcast_fusion.refs_0_.own_ref, s32[16,9]{1,0:T(8,128)S(1)} %collective-permute-done.refs_1_.near_ref, s32[3]{0:T(128)S(1)} %pad_add_fusion.pos_ref.refs_2_, f32[3]{0:T(128)} %scale_ref.3, ...), custom_call_target="tpu_custom_call" | custom-call | tf_op jit(solution)/shard_map/pallas_call | solution.py:239
  26.9 5.8 %collective-permute-start.7 = (f32[6,128,256]{2,1,0:T(8,128)S(1)}, f32[6,128,256]{2,1,0:T(8,128)S(1)}, u32[]{:S(2)}, u32[]{:S(2)}) collective-permute-start(f32[6,128,256]{2,1,0:T(8,128)S(1)} %get-tuple-element.18.refs_1_), channel_id=1, source_target_pairs={{0,48},{1,49},{2,50},{3,51},{4,52},{5,53},{6,54},{7,55},{8,56},{9,... | collective-permute-start | bytes 2359304 | tf_op jit(solution)/shard_map/ppermute | solution.py:62
  32.7 6.2 %shard_map.95 = (f32[3,128,256]{2,1,0:T(8,128)S(1)}, f32[3,128,256]{2,1,0:T(8,128)S(1)}, f32[3,128,256]{2,1,0:T(8,128)S(1)}, f32[3,128,256]{2,1,0:T(8,128)S(1)},...) custom-call(s32[16,9]{1,0:T(8,128)S(1)} %convert_bitcast_fusion.refs, ...), custom_call_target="tpu_custom_call" | custom-call | tf_op jit(solution)/shard_map/pallas_call | solution.py:239
  38.9 0.0 copy-start.1
  39.0 3.4 %shard_map.94.refs_1_.refs_10_ = f32[6,256,256]{2,1,0:T(8,128)S(1)} custom-call(s32[16,9]{1,0:T(8,128)S(1)} %convert_bitcast_fusion.refs_0_.own_ref, s32[16,9]{1,0:T(8,128)S(1)} %collective-permute-done.refs_1_.near_ref, s32[3]{0:T(128)S(1)} %pad_add_fusion.pos_ref.refs_2_, f32[3]{0:T(128)} %scale_ref.3, f32[8,3,256,128]{3,2,1,0:T(8,128)S(1)} %columns.1.refs_4_.pay_ref, ...), custom_call_target="tpu_custom_call" | custom-call | tf_op jit(solution)/shard_map/pallas_call | solution.py:239
  42.4 6.7 %gradients.1 = f32[4,2048]{1,0:T(4,128)S(1)} custom-call(s32[16,9]{1,0:T(8,128)S(1)} %convert_bitcast_fusion.refs_0_.own_ref, s32[16,9]{1,0:T(8,128)S(1)} %collective-permute-done.refs_1_.near_ref, s32[3]{0:T(128)S(1)} %pad_add_fusion.pos_ref.refs_2_, f32[3]{0:T(128)} %scale_ref.3, f32[8,3,256,128]{3,2,1,0:T(8,128)S(1)} %columns.1.refs_4_.pay_ref, ...), custom_call_target="tpu_custom_call" | custom-call | tf_op jit(solution)/shard_map/gradients/pallas_call | solution.py:308
  49.1 0.4 collective-permute-start.14
  49.5 0.9 collective-permute-done.14
  50.4 0.5 collective-permute-start.15
  50.8 3.7 %collective-permute-start.10 = (f32[3,128,256]{2,1,0:T(8,128)S(1)}, f32[3,128,256]{2,1,0:T(8,128)S(1)}, u32[]{:S(2)}, u32[]{:S(2)}) collective-permute-start(f32[3,128,256]{2,1,0:T(8,128)S(1)} %get-tuple-element.20.refs_6_), channel_id=1, source_target_pairs={{0,48},{1,49},{2,50},{3,51},{4,52},{5,53},{6,54},{7,55},{8,56},{9,... | collective-permute-start | bytes 1179656 | tf_op jit(solution)/shard_map/ppermute | solution.py:62
  54.6 1.3 %collective-permute-done.15 = f32[4,2048]{1,0:T(4,128)S(1)} collective-permute-done((f32[4,2048]{1,0:T(4,128)S(1)}, f32[4,2048]{1,0:T(4,128)S(1)}, u32[]{:S(2)}, u32[]{:S(2)}) %collective-permute-start.15) | collective-permute-done | bytes 32800 | tf_op jit(solution)/shard_map/ppermute | solution.py:62
  55.9 0.1 collective-permute-start.16
  56.0 3.4 %collective-permute-start.17 = (f32[4,2048]{1,0:T(4,128)S(1)}, f32[4,2048]{1,0:T(4,128)S(1)}, u32[]{:S(2)}, u32[]{:S(2)}) collective-permute-start(f32[4,2048]{1,0:T(4,128)S(1)} %add.46), channel_id=1, source_target_pairs={{0,32},{1,33},{2,34},{3,35},{4,36},{5,37},{6,38},{7,39},{8,40},{9,... | collective-permute-start | bytes 98312 | tf_op jit(solution)/shard_map/ppermute | solution.py:62
  59.4 0.9 slice_add_fusion
  60.2 1.3 %collective-permute-start.18 = (f32[4,2048]{1,0:T(4,128)S(1)}, f32[4,2048]{1,0:T(4,128)S(1)}, u32[]{:S(2)}, u32[]{:S(2)}) collective-permute-start(f32[4,2048]{1,0:T(4,128)S(1)} %add.46), channel_id=1, source_target_pairs={{0,48},{1,49},{2,50},{3,51},{4,52},{5,53},{6,54},{7,55},{8,56},{9,... | collective-permute-start | bytes 98312 | tf_op jit(solution)/shard_map/ppermute | solution.py:62
  61.5 0.8 slice_add_fusion.1
  62.4 1.7 %collective-permute-done.16 = f32[4,2048]{1,0:T(4,128)S(1)} collective-permute-done((f32[4,2048]{1,0:T(4,128)S(1)}, f32[4,2048]{1,0:T(4,128)S(1)}, u32[]{:S(2)}, u32[]{:S(2)}) %collective-permute-start.16) | collective-permute-done | bytes 32800 | tf_op jit(solution)/shard_map/ppermute | solution.py:62
  64.0 2.5 %collective-permute-start.12 = (f32[3,128,256]{2,1,0:T(8,128)S(1)}, f32[3,128,256]{2,1,0:T(8,128)S(1)}, u32[]{:S(2)}, u32[]{:S(2)}) collective-permute-start(f32[3,128,256]{2,1,0:T(8,128)S(1)} %get-tuple-element.23), channel_id=1, source_target_pairs={{0,48},{1,49},{2,50},{3,51},{4,52},{5,53},{6,54},{7,55},{8,56},{9,... | collective-permute-start | bytes 1179656 | tf_op jit(solution)/shard_map/ppermute | solution.py:62
  66.5 0.0 collective-permute-start.9
  66.5 1.3 %collective-permute-done.18 = f32[4,2048]{1,0:T(4,128)S(1)} collective-permute-done((f32[4,2048]{1,0:T(4,128)S(1)}, f32[4,2048]{1,0:T(4,128)S(1)}, u32[]{:S(2)}, u32[]{:S(2)}) %collective-permute-start.18) | collective-permute-done | bytes 32800 | tf_op jit(solution)/shard_map/ppermute | solution.py:62
  67.8 0.0 copy-start.2
  67.8 6.6 %collective-permute-done.12.refs_5_ = f32[3,128,256]{2,1,0:T(8,128)S(1)} collective-permute-done((f32[3,128,256]{2,1,0:T(8,128)S(1)}, f32[3,128,256]{2,1,0:T(8,128)S(1)}, u32[]{:S(2)}, u32[]{:S(2)}) %collective-permute-start.12) | collective-permute-done | bytes 393248 | tf_op jit(solution)/shard_map/ppermute | solution.py:62
  74.5 2.8 %collective-permute-done.9.refs_2_ = f32[3,128,256]{2,1,0:T(8,128)S(1)} collective-permute-done((f32[3,128,256]{2,1,0:T(8,128)S(1)}, f32[3,128,256]{2,1,0:T(8,128)S(1)}, u32[]{:S(2)}, u32[]{:S(2)}) %collective-permute-start.9) | collective-permute-done | bytes 393248 | tf_op jit(solution)/shard_map/ppermute | solution.py:62
  77.3 2.5 %shard_map.97 = f32[3,256,256]{2,1,0:T(8,128)S(1)} custom-call(s32[1,1]{1,0:T(1,128)S(6)} %copy.14.count_ref.refs_0_, f32[6,256,256]{2,1,0:T(8,128)S(1)} %shard_map.94.refs_1_.refs_10_, f32[3,128,256]{2,1,0:T(8,128)S(1)} %collective-permute-done.9.refs_2_, f32[3,128,256]{2,1,0:T(8,128)S(1)} %collective-permute-done.10.refs_3_, ...), custom_call_target="tpu_custom_call" | custom-call | tf_op jit(solution)/shard_map/pallas_call | solution.py:353
  79.7 1.2 %collective-permute-start.13 = (f32[3,256,256]{2,1,0:T(8,128)S(1)}, f32[3,256,256]{2,1,0:T(8,128)S(1)}, u32[]{:S(2)}, u32[]{:S(2)}) collective-permute-start(f32[3,256,256]{2,1,0:T(8,128)S(1)} %shard_map.97), channel_id=1, source_target_pairs={{0,64},{1,65},{2,66},{3,67},{4,68},{5,69},{6,70},{7,71},{8,72},{9,... | collective-permute-start | bytes 2359304 | tf_op jit(solution)/shard_map/ppermute | solution.py:62
  81.0 0.1 reduce_sum.9
  81.1 3.5 %collective-permute-start.19 = (f32[1,128]{1,0:T(1,128)S(1)}, f32[1,128]{1,0:T(1,128)S(1)}, u32[]{:S(2)}, u32[]{:S(2)}) collective-permute-start(f32[1,128]{1,0:T(1,128)S(1)} %pad_bitcast_fusion), channel_id=1, source_target_pairs={{0,1},{1,0},{2,3},{3,2},{4,5},{5,4},{6,7},{7,6},{8,9},{9,8},{10,11... | collective-permute-start | bytes 1544 | tf_op jit(solution)/shard_map/ppermute | solution.py:62
  84.6 6.8 %collective-permute-start.20 = (f32[1,128]{1,0:T(1,128)S(1)}, f32[1,128]{1,0:T(1,128)S(1)}, u32[]{:S(2)}, u32[]{:S(2)}) collective-permute-start(f32[1,128]{1,0:T(1,128)S(1)} %pad_bitcast_fusion), channel_id=1, source_target_pairs={{0,2},{1,3},{2,0},{3,1},{4,6},{5,7},{6,4},{7,5},{8,10},{9,11},{10,... | collective-permute-start | bytes 1544 | tf_op jit(solution)/shard_map/ppermute | solution.py:62
  91.4 1.5 %collective-permute-done.20 = f32[1,128]{1,0:T(1,128)S(1)} collective-permute-done((f32[1,128]{1,0:T(1,128)S(1)}, f32[1,128]{1,0:T(1,128)S(1)}, u32[]{:S(2)}, u32[]{:S(2)}) %collective-permute-start.20) | collective-permute-done | bytes 544 | tf_op jit(solution)/shard_map/ppermute | solution.py:62
  93.0 3.2 %collective-permute-done.21 = f32[1,128]{1,0:T(1,128)S(1)} collective-permute-done((f32[1,128]{1,0:T(1,128)S(1)}, f32[1,128]{1,0:T(1,128)S(1)}, u32[]{:S(2)}, u32[]{:S(2)}) %collective-permute-start.21) | collective-permute-done | bytes 544 | tf_op jit(solution)/shard_map/ppermute | solution.py:62
  96.2 0.2 collective-permute-start.5
  96.5 1.9 %collective-permute-start.6 = (f32[3,128,256]{2,1,0:T(8,128)S(1)}, f32[3,128,256]{2,1,0:T(8,128)S(1)}, u32[]{:S(2)}, u32[]{:S(2)}) collective-permute-start(f32[3,128,256]{2,1,0:T(8,128)S(1)} %get-tuple-element.16.refs_5_), channel_id=1, source_target_pairs={{0,16},{1,17},{2,18},{3,19},{4,20},{5,21},{6,22},{7,23},{8,24},{9,... | collective-permute-start | bytes 1179656 | tf_op jit(solution)/shard_map/ppermute | solution.py:62
  98.3 1.4 %collective-permute-start.8 = (f32[3,128,256]{2,1,0:T(8,128)}, f32[3,128,256]{2,1,0:T(8,128)S(1)}, u32[]{:S(2)}, u32[]{:S(2)}) collective-permute-start(f32[3,128,256]{2,1,0:T(8,128)} %get-tuple-element.24), channel_id=1, source_target_pairs={{0,48},{1,49},{2,50},{3,51},{4,52},{5,53},{6,54},{7,55},{8,56},{9,... | collective-permute-start | bytes 1179656 | tf_op jit(solution)/shard_map/ppermute | solution.py:62
  99.7 0.8 collective-permute-done.22
  100.5 0.5 slice_bitcast_fusion
  101.0 6.7 %collective-permute-done.5.refs_3_ = f32[3,128,256]{2,1,0:T(8,128)S(1)} collective-permute-done((f32[3,128,256]{2,1,0:T(8,128)}, f32[3,128,256]{2,1,0:T(8,128)S(1)}, u32[]{:S(2)}, u32[]{:S(2)}) %collective-permute-start.5) | collective-permute-done | bytes 393248 | tf_op jit(solution)/shard_map/ppermute | solution.py:62
  107.7 1.7 %collective-permute-done.6.refs_4_ = f32[3,128,256]{2,1,0:T(8,128)S(1)} collective-permute-done((f32[3,128,256]{2,1,0:T(8,128)S(1)}, f32[3,128,256]{2,1,0:T(8,128)S(1)}, u32[]{:S(2)}, u32[]{:S(2)}) %collective-permute-start.6) | collective-permute-done | bytes 393248 | tf_op jit(solution)/shard_map/ppermute | solution.py:62
  109.4 2.5 %collective-permute-done.8.refs_5_ = f32[3,128,256]{2,1,0:T(8,128)S(1)} collective-permute-done((f32[3,128,256]{2,1,0:T(8,128)}, f32[3,128,256]{2,1,0:T(8,128)S(1)}, u32[]{:S(2)}, u32[]{:S(2)}) %collective-permute-start.8) | collective-permute-done | bytes 393248 | tf_op jit(solution)/shard_map/ppermute | solution.py:62
  111.9 1.9 %collective-permute-done.4.refs_2_ = f32[3,128,256]{2,1,0:T(8,128)S(1)} collective-permute-done((f32[3,128,256]{2,1,0:T(8,128)}, f32[3,128,256]{2,1,0:T(8,128)S(1)}, u32[]{:S(2)}, u32[]{:S(2)}) %collective-permute-start.4) | collective-permute-done | bytes 393248 | tf_op jit(solution)/shard_map/ppermute | solution.py:62
  113.9 3.3 %shard_map.98 = f32[3,256,256]{2,1,0:T(8,128)} custom-call(s32[1,1]{1,0:T(1,128)S(6)} %copy.14.count_ref.refs_0_, f32[6,256,256]{2,1,0:T(8,128)S(1)} %shard_map.94.refs_1_.refs_10_, f32[3,128,256]{2,1,0:T(8,128)S(1)} %collective-permute-done.4.refs_2_, f32[3,128,256]{2,1,0:T(8,128)S(1)} %collective-permute-done.5.refs_3_, ...), custom_call_target="tpu_custom_call" | custom-call | tf_op jit(solution)/shard_map/pallas_call | solution.py:353
  (29 shorter events, 0.1 us)
Async XLA Ops:
  0.6 21.4 %collective-permute-start.2 = (f32[1024,2048]{1,0:T(8,128)}, f32[1024,2048]{1,0:T(8,128)}, u32[]{:S(2)}, u32[]{:S(2)}) collective-permute-start(f32[1024,2048]{1,0:T(8,128)} %refs_6_.5), channel_id=1, source_target_pairs={{0,8},{1,9},{2,10},{3,11},{4,12},{5,13},{6,14},{7,15},{8,0},{9,1},... | collective-permute-start | bytes 25165832 | tf_op jit(solution)/shard_map/ppermute | solution.py:62
  2.9 16.8 %all-to-all-start = ((f32[16,16,256]{2,1,0:T(8,128)}), f32[16,16,256]{2,1,0:T(8,128)S(1)}, u32[]{:S(2)}, u32[]{:S(2)}) async-start(f32[16,16,256]{2,1,0:T(8,128)} %payload.1), calls=%async_computation | async-start | bytes 524288 | tf_op jit(solution)/shard_map/all_to_all | solution.py:383
  10.1 11.9 %collective-permute-start.1 = (f32[3,2048]{1,0:T(4,128)}, f32[3,2048]{1,0:T(4,128)S(1)}, u32[]{:S(2)}, u32[]{:S(2)}) collective-permute-start(f32[3,2048]{1,0:T(4,128)} %z_ref.1), channel_id=1, source_target_pairs={{0,0},{1,16},{2,32},{3,48},{4,64},{5,80},{6,96},{7,112},{8,8},{9,2... | collective-permute-start | bytes 73736 | tf_op jit(solution)/shard_map/ppermute | solution.py:62
  19.7 2.3 %collective-permute-start = (s32[16,9]{1,0:T(8,128)S(1)}, s32[16,9]{1,0:T(8,128)S(1)}, u32[]{:S(2)}, u32[]{:S(2)}) collective-permute-start(s32[16,9]{1,0:T(8,128)S(1)} %convert_bitcast_fusion.refs_0_.own_ref), channel_id=1, source_target_pairs={{0,0},{1,16},{2,32},{3,48},{4,64},{5,80},{6,96},{7,112},{8,8},{9,2... | collective-permute-start | bytes 1736 | tf_op jit(solution)/shard_map/ppermute | solution.py:62
  26.9 29.1 %collective-permute-start.7 = (f32[6,128,256]{2,1,0:T(8,128)S(1)}, f32[6,128,256]{2,1,0:T(8,128)S(1)}, u32[]{:S(2)}, u32[]{:S(2)}) collective-permute-start(f32[6,128,256]{2,1,0:T(8,128)S(1)} %get-tuple-element.18.refs_1_), channel_id=1, source_target_pairs={{0,48},{1,49},{2,50},{3,51},{4,52},{5,53},{6,54},{7,55},{8,56},{9,... | collective-permute-start | bytes 2359304 | tf_op jit(solution)/shard_map/ppermute | solution.py:62
  32.7 27.5 %collective-permute-start.3 = (f32[6,128,256]{2,1,0:T(8,128)S(1)}, f32[6,128,256]{2,1,0:T(8,128)S(1)}, u32[]{:S(2)}, u32[]{:S(2)}) collective-permute-start(f32[6,128,256]{2,1,0:T(8,128)S(1)} %get-tuple-element.14.refs_0_), channel_id=1, source_target_pairs={{0,16},{1,17},{2,18},{3,19},{4,20},{5,21},{6,22},{7,23},{8,24},{9,... | collective-permute-start | bytes 2359304 | tf_op jit(solution)/shard_map/ppermute | solution.py:62
  38.9 3.4 %copy-start = (f32[3,128,256]{2,1,0:T(8,128)}, f32[3,128,256]{2,1,0:T(8,128)S(1)}, u32[]{:S(2)}) copy-start(f32[3,128,256]{2,1,0:T(8,128)S(1)} %get-tuple-element.15.refs_8_) | copy-start | bytes 1179652
  38.9 3.4 %copy-start.1 = (f32[3,2048]{1,0:T(4,128)S(1)}, f32[3,2048]{1,0:T(4,128)}, u32[]{:S(2)}) copy-start(f32[3,2048]{1,0:T(4,128)} %z_ref.1) | copy-start | bytes 73732
  49.1 1.3 %collective-permute-start.14 = (f32[4,2048]{1,0:T(4,128)S(1)}, f32[4,2048]{1,0:T(4,128)S(1)}, u32[]{:S(2)}, u32[]{:S(2)}) collective-permute-start(f32[4,2048]{1,0:T(4,128)S(1)} %gradients.1), channel_id=1, source_target_pairs={{0,8},{1,9},{2,10},{3,11},{4,12},{5,13},{6,14},{7,15},{8,0},{9,1},... | collective-permute-start | bytes 98312 | tf_op jit(solution)/shard_map/ppermute | solution.py:62
  50.4 5.5 %collective-permute-start.15 = (f32[4,2048]{1,0:T(4,128)S(1)}, f32[4,2048]{1,0:T(4,128)S(1)}, u32[]{:S(2)}, u32[]{:S(2)}) collective-permute-start(f32[4,2048]{1,0:T(4,128)S(1)} %add.45), channel_id=1, source_target_pairs={{0,64},{1,65},{2,66},{3,67},{4,68},{5,69},{6,70},{7,71},{8,72},{9,... | collective-permute-start | bytes 98312 | tf_op jit(solution)/shard_map/ppermute | solution.py:62
  50.8 17.0 %collective-permute-start.10 = (f32[3,128,256]{2,1,0:T(8,128)S(1)}, f32[3,128,256]{2,1,0:T(8,128)S(1)}, u32[]{:S(2)}, u32[]{:S(2)}) collective-permute-start(f32[3,128,256]{2,1,0:T(8,128)S(1)} %get-tuple-element.20.refs_6_), channel_id=1, source_target_pairs={{0,48},{1,49},{2,50},{3,51},{4,52},{5,53},{6,54},{7,55},{8,56},{9,... | collective-permute-start | bytes 1179656 | tf_op jit(solution)/shard_map/ppermute | solution.py:62
  54.6 13.3 %collective-permute-start.11 = (f32[3,128,256]{2,1,0:T(8,128)S(1)}, f32[3,128,256]{2,1,0:T(8,128)S(1)}, u32[]{:S(2)}, u32[]{:S(2)}) collective-permute-start(f32[3,128,256]{2,1,0:T(8,128)S(1)} %get-tuple-element.21.refs_3_), channel_id=1, source_target_pairs={{0,16},{1,17},{2,18},{3,19},{4,20},{5,21},{6,22},{7,23},{8,24},{9,... | collective-permute-start | bytes 1179656 | tf_op jit(solution)/shard_map/ppermute | solution.py:62
  55.9 8.2 %collective-permute-start.16 = (f32[4,2048]{1,0:T(4,128)S(1)}, f32[4,2048]{1,0:T(4,128)S(1)}, u32[]{:S(2)}, u32[]{:S(2)}) collective-permute-start(f32[4,2048]{1,0:T(4,128)S(1)} %add.46), channel_id=1, source_target_pairs={{0,16},{1,17},{2,18},{3,19},{4,20},{5,21},{6,22},{7,23},{8,24},{9,... | collective-permute-start | bytes 98312 | tf_op jit(solution)/shard_map/ppermute | solution.py:62
  56.0 10.5 %collective-permute-start.17 = (f32[4,2048]{1,0:T(4,128)S(1)}, f32[4,2048]{1,0:T(4,128)S(1)}, u32[]{:S(2)}, u32[]{:S(2)}) collective-permute-start(f32[4,2048]{1,0:T(4,128)S(1)} %add.46), channel_id=1, source_target_pairs={{0,32},{1,33},{2,34},{3,35},{4,36},{5,37},{6,38},{7,39},{8,40},{9,... | collective-permute-start | bytes 98312 | tf_op jit(solution)/shard_map/ppermute | solution.py:62
  60.2 7.6 %collective-permute-start.18 = (f32[4,2048]{1,0:T(4,128)S(1)}, f32[4,2048]{1,0:T(4,128)S(1)}, u32[]{:S(2)}, u32[]{:S(2)}) collective-permute-start(f32[4,2048]{1,0:T(4,128)S(1)} %add.46), channel_id=1, source_target_pairs={{0,48},{1,49},{2,50},{3,51},{4,52},{5,53},{6,54},{7,55},{8,56},{9,... | collective-permute-start | bytes 98312 | tf_op jit(solution)/shard_map/ppermute | solution.py:62
  64.0 10.4 %collective-permute-start.12 = (f32[3,128,256]{2,1,0:T(8,128)S(1)}, f32[3,128,256]{2,1,0:T(8,128)S(1)}, u32[]{:S(2)}, u32[]{:S(2)}) collective-permute-start(f32[3,128,256]{2,1,0:T(8,128)S(1)} %get-tuple-element.23), channel_id=1, source_target_pairs={{0,48},{1,49},{2,50},{3,51},{4,52},{5,53},{6,54},{7,55},{8,56},{9,... | collective-permute-start | bytes 1179656 | tf_op jit(solution)/shard_map/ppermute | solution.py:62
  66.5 10.7 %collective-permute-start.9 = (f32[3,128,256]{2,1,0:T(8,128)S(1)}, f32[3,128,256]{2,1,0:T(8,128)S(1)}, u32[]{:S(2)}, u32[]{:S(2)}) collective-permute-start(f32[3,128,256]{2,1,0:T(8,128)S(1)} %get-tuple-element.25), channel_id=1, source_target_pairs={{0,16},{1,17},{2,18},{3,19},{4,20},{5,21},{6,22},{7,23},{8,24},{9,... | collective-permute-start | bytes 1179656 | tf_op jit(solution)/shard_map/ppermute | solution.py:62
  67.8 13.2 %copy-start.2 = (f32[4,2048]{1,0:T(4,128)}, f32[4,2048]{1,0:T(4,128)S(1)}, u32[]{:S(2)}) copy-start(f32[4,2048]{1,0:T(4,128)S(1)} %add_add_fusion) | copy-start | bytes 98308
  79.7 34.1 %collective-permute-start.13 = (f32[3,256,256]{2,1,0:T(8,128)S(1)}, f32[3,256,256]{2,1,0:T(8,128)S(1)}, u32[]{:S(2)}, u32[]{:S(2)}) collective-permute-start(f32[3,256,256]{2,1,0:T(8,128)S(1)} %shard_map.97), channel_id=1, source_target_pairs={{0,64},{1,65},{2,66},{3,67},{4,68},{5,69},{6,70},{7,71},{8,72},{9,... | collective-permute-start | bytes 2359304 | tf_op jit(solution)/shard_map/ppermute | solution.py:62
  81.1 10.3 %collective-permute-start.19 = (f32[1,128]{1,0:T(1,128)S(1)}, f32[1,128]{1,0:T(1,128)S(1)}, u32[]{:S(2)}, u32[]{:S(2)}) collective-permute-start(f32[1,128]{1,0:T(1,128)S(1)} %pad_bitcast_fusion), channel_id=1, source_target_pairs={{0,1},{1,0},{2,3},{3,2},{4,5},{5,4},{6,7},{7,6},{8,9},{9,8},{10,11... | collective-permute-start | bytes 1544 | tf_op jit(solution)/shard_map/ppermute | solution.py:62
  84.6 8.4 %collective-permute-start.20 = (f32[1,128]{1,0:T(1,128)S(1)}, f32[1,128]{1,0:T(1,128)S(1)}, u32[]{:S(2)}, u32[]{:S(2)}) collective-permute-start(f32[1,128]{1,0:T(1,128)S(1)} %pad_bitcast_fusion), channel_id=1, source_target_pairs={{0,2},{1,3},{2,0},{3,1},{4,6},{5,7},{6,4},{7,5},{8,10},{9,11},{10,... | collective-permute-start | bytes 1544 | tf_op jit(solution)/shard_map/ppermute | solution.py:62
  91.4 4.8 %collective-permute-start.21 = (f32[1,128]{1,0:T(1,128)S(1)}, f32[1,128]{1,0:T(1,128)S(1)}, u32[]{:S(2)}, u32[]{:S(2)}) collective-permute-start(f32[1,128]{1,0:T(1,128)S(1)} %pad_bitcast_fusion), channel_id=1, source_target_pairs={{0,3},{1,2},{2,1},{3,0},{4,7},{5,6},{6,5},{7,4},{8,11},{9,10},{10,... | collective-permute-start | bytes 1544 | tf_op jit(solution)/shard_map/ppermute | solution.py:62
  96.2 4.3 %collective-permute-start.22 = (f32[1,128]{1,0:T(1,128)S(1)}, f32[1,128]{1,0:T(1,128)S(1)}, u32[]{:S(2)}, u32[]{:S(2)}) collective-permute-start(f32[1,128]{1,0:T(1,128)S(1)} %add_add_fusion.1), channel_id=1, source_target_pairs={{0,4},{1,5},{2,6},{3,7},{4,0},{5,1},{6,2},{7,3},{8,12},{9,13},{10,... | collective-permute-start | bytes 1544 | tf_op jit(solution)/shard_map/ppermute | solution.py:62
  96.2 11.5 %collective-permute-start.5 = (f32[3,128,256]{2,1,0:T(8,128)}, f32[3,128,256]{2,1,0:T(8,128)S(1)}, u32[]{:S(2)}, u32[]{:S(2)}) collective-permute-start(f32[3,128,256]{2,1,0:T(8,128)} %copy-done), channel_id=1, source_target_pairs={{0,48},{1,49},{2,50},{3,51},{4,52},{5,53},{6,54},{7,55},{8,56},{9,... | collective-permute-start | bytes 1179656 | tf_op jit(solution)/shard_map/ppermute | solution.py:62
  96.5 12.9 %collective-permute-start.6 = (f32[3,128,256]{2,1,0:T(8,128)S(1)}, f32[3,128,256]{2,1,0:T(8,128)S(1)}, u32[]{:S(2)}, u32[]{:S(2)}) collective-permute-start(f32[3,128,256]{2,1,0:T(8,128)S(1)} %get-tuple-element.16.refs_5_), channel_id=1, source_target_pairs={{0,16},{1,17},{2,18},{3,19},{4,20},{5,21},{6,22},{7,23},{8,24},{9,... | collective-permute-start | bytes 1179656 | tf_op jit(solution)/shard_map/ppermute | solution.py:62
  98.3 13.6 %collective-permute-start.8 = (f32[3,128,256]{2,1,0:T(8,128)}, f32[3,128,256]{2,1,0:T(8,128)S(1)}, u32[]{:S(2)}, u32[]{:S(2)}) collective-permute-start(f32[3,128,256]{2,1,0:T(8,128)} %get-tuple-element.24), channel_id=1, source_target_pairs={{0,48},{1,49},{2,50},{3,51},{4,52},{5,53},{6,54},{7,55},{8,56},{9,... | collective-permute-start | bytes 1179656 | tf_op jit(solution)/shard_map/ppermute | solution.py:62
  100.5 13.4 %collective-permute-start.4 = (f32[3,128,256]{2,1,0:T(8,128)}, f32[3,128,256]{2,1,0:T(8,128)S(1)}, u32[]{:S(2)}, u32[]{:S(2)}) collective-permute-start(f32[3,128,256]{2,1,0:T(8,128)} %get-tuple-element.26), channel_id=1, source_target_pairs={{0,16},{1,17},{2,18},{3,19},{4,20},{5,21},{6,22},{7,23},{8,24},{9,... | collective-permute-start | bytes 1179656 | tf_op jit(solution)/shard_map/ppermute | solution.py:62

commit v4 on v3

--- a/solution.py
+++ b/solution.py
@@ -181,12 +181,6 @@
             @pl.when(active)
             def _():
                 points = scaled_points(pay_ref, group, slot, z_ref, near * BS, scale_ref)
-                copy_in(mine_ref, 0, 0, place).wait()
-                for row in range(0, BS, STRIP):
-                    high, low = split(tiles[place, pl.ds(row, STRIP), :])
-                    right[row : row + STRIP, :] = low
-                    right[BS + row : BS + row + STRIP, :] = high
-                    right[2 * BS + row : 2 * BS + row + STRIP, :] = high
                 for half in range(2):
                     for row in range(half * HALF, (half + 1) * HALF, STRIP):
                         rows = slice(row, row + STRIP)
@@ -197,6 +191,13 @@
                         left[rows, 0:BS] = high
                         left[rows, BS : 2 * BS] = low
                         left[rows, 2 * BS : 3 * BS] = high
+                copy_in(mine_ref, 0, 0, place).wait()
+                for row in range(0, BS, STRIP):
+                    high, low = split(tiles[place, pl.ds(row, STRIP), :])
+                    right[row : row + STRIP, :] = low
+                    right[BS + row : BS + row + STRIP, :] = high
+                    right[2 * BS + row : 2 * BS + row + STRIP, :] = high
+                for half in range(2):
                     rows = pl.ds(half * HALF, HALF)
                     value = jnp.dot(left[rows, :], right[...], preferred_element_type=jnp.float32)
                     store(number, own_x, slot, half, value)
@@ -315,55 +316,38 @@
     )(*tables, scales, payload, z_own, *parts)
 
 
-def combine_kernel(first, count_ref, base_ref, *refs):
-    *pieces, out_ref, base, halves, total, in_sems, out_sems = refs
-    extra = pieces[4] if len(pieces) == 5 else None
-
-    def copies(slot):
-        made = [pltpu.make_async_copy(base_ref.at[first + slot], base.at[0, slot], in_sems.at[slot, 0])]
+def combine_kernel(first, base_ref, *refs):
+    *pieces, out_ref, halves, in_sems = refs
+
+    def copy(slot, number):
+        return pltpu.make_async_copy(pieces[number].at[slot], halves.at[number, slot], in_sems.at[slot, number])
+
+    for slot in range(SLOTS):
         for number in range(4):
-            made.append(pltpu.make_async_copy(pieces[number].at[slot], halves.at[number, slot], in_sems.at[slot, 1 + number]))
-        if extra is not None:
-            made.append(pltpu.make_async_copy(extra.at[slot], base.at[1, slot], in_sems.at[slot, 5]))
-        return made
-
+            copy(slot, number).start()
     for slot in range(SLOTS):
-        for copy in copies(slot):
-            copy.start()
-    for slot in range(SLOTS):
-        for copy in copies(slot):
-            copy.wait()
+        for number in range(4):
+            copy(slot, number).wait()
         for half in range(2):
             rows = pl.ds(half * HALF, HALF)
-            value = base[0, slot, rows, :] + halves[2 * half, slot] + halves[2 * half + 1, slot]
-            if extra is not None:
-                value = jnp.where(count_ref[0, 0] > slot, value + base[1, slot, rows, :], 0.0)
-            total[slot, rows, :] = value
-        pltpu.make_async_copy(total.at[slot], out_ref.at[slot], out_sems.at[slot]).start()
-    for slot in range(SLOTS):
-        pltpu.make_async_copy(total.at[slot], out_ref.at[slot], out_sems.at[slot]).wait()
-
-
-def combine(base, first, tops, bottoms, extra, count):
-    extras = [] if extra is None else [extra]
-
+            out_ref[slot, rows, :] = base_ref[first + slot, rows, :] + halves[2 * half, slot] + halves[2 * half + 1, slot]
+
+
+def combine(base, first, tops, bottoms):
     def kernel(*refs):
         combine_kernel(first, *refs)
 
     return pl.pallas_call(
         kernel,
-        out_shape=jax.ShapeDtypeStruct((SLOTS, BS, BS), jnp.float32),
-        in_specs=[SMEM] + [HBM] * (5 + len(extras)),
-        out_specs=HBM,
+        out_shape=pltpu.VMEM((SLOTS, BS, BS), jnp.float32),
+        in_specs=[VMEM] + [HBM] * 4,
+        out_specs=VMEM,
         scratch_shapes=[
-            pltpu.VMEM((1 + len(extras), SLOTS, BS, BS), jnp.float32),
             pltpu.VMEM((4, SLOTS, HALF, BS), jnp.float32),
-            pltpu.VMEM((SLOTS, BS, BS), jnp.float32),
-            pltpu.SemaphoreType.DMA((SLOTS, 6)),
-            pltpu.SemaphoreType.DMA((SLOTS,)),
+            pltpu.SemaphoreType.DMA((SLOTS, 4)),
         ],
         compiler_params=grant(8),
-    )(count, base, *tops, *bottoms, *extras)
+    )(base, *tops, *bottoms)
 
 
 def on_device(x_points, z_points, length_scales, dpsi_grad, block_rows, block_cols, block_count):
@@ -410,9 +394,11 @@
     direct_down_w = permute(down_w[0], Y_DOWN)
     sum_up_w = permute(up_w[0] + got_up[SLOTS:], Y_UP)
     sum_down_w = permute(down_w[1] + got_down[SLOTS:], Y_DOWN)
-    sum_o = combine(here, 0, (sum_up_o, direct_down_o), (direct_up_o, sum_down_o), None, block_count)
+    sum_o = combine(here, 0, (sum_up_o, direct_down_o), (direct_up_o, sum_down_o))
     got_x = permute(sum_o, SWAP_XH)
-    dk_local = combine(here, SLOTS, (sum_up_w, direct_down_w), (direct_up_w, sum_down_w), got_x, block_count)
+    sum_w = combine(here, SLOTS, (sum_up_w, direct_down_w), (direct_up_w, sum_down_w))
+    live = jnp.arange(SLOTS, dtype=jnp.int32)[:, None, None] < block_count
+    dk_local = jnp.where(live, sum_w + got_x, 0.0)
 
     total = local + permute(local, SWAP_CORE)
     total = total + permute(total, SWAP_XH)

time: 118 us -> 118 us (level)
  Pallas kernels: 29.9 us -> 28.2 us
  other arithmetic: 1.95 us -> 3.38 us
    reshape x0 -> x1, other arithmetic: none -> 2.17 us  [on_device(): return (dk_local.reshape(1, 1, SLOTS, BS, BS), z_grad, scale_grad)]
    pallas_call x2, Pallas kernels: 5.72 us -> 4.48 us  [combine(): pl.pallas_call(kernel, out_shape=pltpu.VMEM((SLOTS, BS, BS), jnp.float32)...]
  transfers between devices with their start and end apart: 24 -> 24, of which waited for: 14 -> 14; matrix products, arithmetic and copies ran while one was open for 2% -> 2% of each run, Pallas kernels for 17% -> 18%
where the time goes in v4:
time: 118 us
  starting transfers between devices  42.3 us (36%)
  waiting for transfers between devices  41.7 us (35%)
  Pallas kernels  28.2 us (24%)
  other arithmetic  3.38 us (3%)
  between operations  1.51 us (1%)
    ppermute x23, starting transfers between devices, permute(): return lax.ppermute(value, AXES, perm)  35.1 us
    ppermute x23, waiting for transfers between devices, permute(): return lax.ppermute(value, AXES, perm)  33.6 us
    pallas_call x3, Pallas kernels, products(): pl.pallas_call(kernel, out_shape=[pltpu.VMEM(shape, jnp.float32) for shap...  14 us
    all_to_all x1, waiting for transfers between devices, on_device(): payload = lax.all_to_all(outgoing, DP, 0, 0, tiled=True)  8.1 us
    all_to_all x1, starting transfers between devices, on_device(): payload = lax.all_to_all(outgoing, DP, 0, 0, tiled=True)  7.25 us
    pallas_call x1, Pallas kernels, gradients(): pl.pallas_call(gradient_kernel, out_shape=jax.ShapeDtypeStruct((4, z_own....  6.66 us
    pallas_call x2, Pallas kernels, combine(): pl.pallas_call(kernel, out_shape=pltpu.VMEM((SLOTS, BS, BS), jnp.float32)...  4.48 us
  transfers between devices with their start and end apart: 24, of which 14 were waited for; matrix products, arithmetic and copies ran while one was open for 2% of the time, Pallas kernels for 18%

profile of v4, /device:TPU:0, one launch (start us, length us, event | category | flops | bytes accessed | tf_op | source)
XLA Modules:
  0.0 117.7 jit_solution(16929103448898478884)
XLA Ops:
  0.6 0.1 collective-permute-start.2
  1.4 1.5 %payload.1 = f32[16,16,256]{2,1,0:T(8,128)} custom-call(s32[1,1,3]{2,1,0:T(1,128)} %rows_ref.1, s32[1,1,3]{2,1,0:T(1,128)} %cols_ref.1, s32[1,1]{1,0:T(1,128)} %copy.14.count_ref, f32[3,2048]{1,0:T(4,128)} %x_ref.1), custom_call_target="tpu_custom_call" | custom-call | tf_op jit(solution)/shard_map/payload/pallas_call | solution.py:358
  2.9 7.3 %all-to-all-start = ((f32[16,16,256]{2,1,0:T(8,128)}), f32[16,16,256]{2,1,0:T(8,128)S(1)}, u32[]{:S(2)}, u32[]{:S(2)}) async-start(f32[16,16,256]{2,1,0:T(8,128)} %payload.1), calls=%async_computation | async-start | bytes 524288 | tf_op jit(solution)/shard_map/all_to_all | solution.py:367
  10.1 1.4 %collective-permute-start.1 = (f32[3,2048]{1,0:T(4,128)}, f32[3,2048]{1,0:T(4,128)S(1)}, u32[]{:S(2)}, u32[]{:S(2)}) collective-permute-start(f32[3,2048]{1,0:T(4,128)} %z_ref.1), channel_id=1, source_target_pairs={{0,0},{1,16},{2,32},{3,48},{4,64},{5,80},{6,96},{7,112},{8,8},{9,2... | collective-permute-start | bytes 73736 | tf_op jit(solution)/shard_map/ppermute | solution.py:62
  11.6 8.1 %all-to-all-done.pay_ref = f32[16,16,256]{2,1,0:T(8,128)S(1)} async-done(((f32[16,16,256]{2,1,0:T(8,128)}), f32[16,16,256]{2,1,0:T(8,128)S(1)}, u32[]{:S(2)}, u32[]{:S(2)}) %all-to-all-start) | async-done | bytes 262176 | tf_op jit(solution)/shard_map/all_to_all | solution.py:367
  19.7 0.7 collective-permute-start
  20.4 0.1 pad_add_fusion.pos_ref.refs_2_
  20.4 1.6 %columns.1.refs_4_.pay_ref = f32[8,3,256,128]{3,2,1,0:T(8,128)S(1)} custom-call(s32[3]{0:T(128)S(1)} %pad_add_fusion.pos_ref.refs_2_, f32[3]{0:T(128)} %scale_ref.3, f32[16,16,256]{2,1,0:T(8,128)S(1)} %all-to-all-done.pay_ref), custom_call_target="tpu_custom_call" | custom-call | tf_op jit(solution)/shard_map/columns/pallas_call | solution.py:372
  22.1 4.7 %shard_map.96 = (f32[6,128,256]{2,1,0:T(8,128)S(1)}, f32[6,128,256]{2,1,0:T(8,128)S(1)}) custom-call(s32[16,9]{1,0:T(8,128)S(1)} %convert_bitcast_fusion.refs_0_.own_ref, s32[16,9]{1,0:T(8,128)S(1)} %collective-permute-done.refs_1_.near_ref, s32[3]{0:T(128)S(1)} %pad_add_fusion.pos_ref.refs_2_, f32[3]{0:T(128)} %scale_ref.3, ...), custom_call_target="tpu_custom_call" | custom-call | tf_op jit(solution)/shard_map/pallas_call | solution.py:240
  26.8 5.7 %collective-permute-start.7 = (f32[6,128,256]{2,1,0:T(8,128)S(1)}, f32[6,128,256]{2,1,0:T(8,128)S(1)}, u32[]{:S(2)}, u32[]{:S(2)}) collective-permute-start(f32[6,128,256]{2,1,0:T(8,128)S(1)} %get-tuple-element.18.refs_1_), channel_id=1, source_target_pairs={{0,48},{1,49},{2,50},{3,51},{4,52},{5,53},{6,54},{7,55},{8,56},{9,... | collective-permute-start | bytes 2359304 | tf_op jit(solution)/shard_map/ppermute | solution.py:62
  32.5 6.2 %shard_map.95 = (f32[3,128,256]{2,1,0:T(8,128)S(1)}, f32[3,128,256]{2,1,0:T(8,128)S(1)}, f32[3,128,256]{2,1,0:T(8,128)S(1)}, f32[3,128,256]{2,1,0:T(8,128)S(1)},...) custom-call(s32[16,9]{1,0:T(8,128)S(1)} %convert_bitcast_fusion.refs, ...), custom_call_target="tpu_custom_call" | custom-call | tf_op jit(solution)/shard_map/pallas_call | solution.py:240
  38.7 3.1 %shard_map.94.refs_0_.refs_10_ = f32[6,256,256]{2,1,0:T(8,128)S(1)} custom-call(s32[16,9]{1,0:T(8,128)S(1)} %convert_bitcast_fusion.refs_0_.own_ref, s32[16,9]{1,0:T(8,128)S(1)} %collective-permute-done.refs_1_.near_ref, s32[3]{0:T(128)S(1)} %pad_add_fusion.pos_ref.refs_2_, f32[3]{0:T(128)} %scale_ref.3, f32[8,3,256,128]{3,2,1,0:T(8,128)S(1)} %columns.1.refs_4_.pay_ref, ...), custom_call_target="tpu_custom_call" | custom-call | tf_op jit(solution)/shard_map/pallas_call | solution.py:240
  41.8 6.7 %gradients.1 = f32[4,2048]{1,0:T(4,128)S(1)} custom-call(s32[16,9]{1,0:T(8,128)S(1)} %convert_bitcast_fusion.refs_0_.own_ref, s32[16,9]{1,0:T(8,128)S(1)} %collective-permute-done.refs_1_.near_ref, s32[3]{0:T(128)S(1)} %pad_add_fusion.pos_ref.refs_2_, f32[3]{0:T(128)} %scale_ref.3, f32[8,3,256,128]{3,2,1,0:T(8,128)S(1)} %columns.1.refs_4_.pay_ref, ...), custom_call_target="tpu_custom_call" | custom-call | tf_op jit(solution)/shard_map/gradients/pallas_call | solution.py:309
  48.5 0.5 collective-permute-start.14
  48.9 0.9 collective-permute-done.14
  49.8 0.5 collective-permute-start.15
  50.3 3.7 %collective-permute-start.10 = (f32[3,128,256]{2,1,0:T(8,128)S(1)}, f32[3,128,256]{2,1,0:T(8,128)S(1)}, u32[]{:S(2)}, u32[]{:S(2)}) collective-permute-start(f32[3,128,256]{2,1,0:T(8,128)S(1)} %get-tuple-element.20.refs_6_), channel_id=1, source_target_pairs={{0,48},{1,49},{2,50},{3,51},{4,52},{5,53},{6,54},{7,55},{8,56},{9,... | collective-permute-start | bytes 1179656 | tf_op jit(solution)/shard_map/ppermute | solution.py:62
  54.0 1.3 %collective-permute-done.15 = f32[4,2048]{1,0:T(4,128)S(1)} collective-permute-done((f32[4,2048]{1,0:T(4,128)S(1)}, f32[4,2048]{1,0:T(4,128)S(1)}, u32[]{:S(2)}, u32[]{:S(2)}) %collective-permute-start.15) | collective-permute-done | bytes 32800 | tf_op jit(solution)/shard_map/ppermute | solution.py:62
  55.3 0.1 collective-permute-start.16
  55.4 3.3 %collective-permute-start.17 = (f32[4,2048]{1,0:T(4,128)S(1)}, f32[4,2048]{1,0:T(4,128)S(1)}, u32[]{:S(2)}, u32[]{:S(2)}) collective-permute-start(f32[4,2048]{1,0:T(4,128)S(1)} %add.50), channel_id=1, source_target_pairs={{0,32},{1,33},{2,34},{3,35},{4,36},{5,37},{6,38},{7,39},{8,40},{9,... | collective-permute-start | bytes 98312 | tf_op jit(solution)/shard_map/ppermute | solution.py:62
  58.8 0.1 slice_add_fusion
  58.9 1.4 %collective-permute-start.18 = (f32[4,2048]{1,0:T(4,128)S(1)}, f32[4,2048]{1,0:T(4,128)S(1)}, u32[]{:S(2)}, u32[]{:S(2)}) collective-permute-start(f32[4,2048]{1,0:T(4,128)S(1)} %add.50), channel_id=1, source_target_pairs={{0,48},{1,49},{2,50},{3,51},{4,52},{5,53},{6,54},{7,55},{8,56},{9,... | collective-permute-start | bytes 98312 | tf_op jit(solution)/shard_map/ppermute | solution.py:62
  60.3 0.8 slice_add_fusion.1
  61.1 2.3 %collective-permute-done.16 = f32[4,2048]{1,0:T(4,128)S(1)} collective-permute-done((f32[4,2048]{1,0:T(4,128)S(1)}, f32[4,2048]{1,0:T(4,128)S(1)}, u32[]{:S(2)}, u32[]{:S(2)}) %collective-permute-start.16) | collective-permute-done | bytes 32800 | tf_op jit(solution)/shard_map/ppermute | solution.py:62
  63.4 2.5 %collective-permute-start.12 = (f32[3,128,256]{2,1,0:T(8,128)S(1)}, f32[3,128,256]{2,1,0:T(8,128)S(1)}, u32[]{:S(2)}, u32[]{:S(2)}) collective-permute-start(f32[3,128,256]{2,1,0:T(8,128)S(1)} %get-tuple-element.23), channel_id=1, source_target_pairs={{0,48},{1,49},{2,50},{3,51},{4,52},{5,53},{6,54},{7,55},{8,56},{9,... | collective-permute-start | bytes 1179656 | tf_op jit(solution)/shard_map/ppermute | solution.py:62
  65.9 0.0 collective-permute-start.9
  65.9 1.3 %collective-permute-done.18 = f32[4,2048]{1,0:T(4,128)S(1)} collective-permute-done((f32[4,2048]{1,0:T(4,128)S(1)}, f32[4,2048]{1,0:T(4,128)S(1)}, u32[]{:S(2)}, u32[]{:S(2)}) %collective-permute-start.18) | collective-permute-done | bytes 32800 | tf_op jit(solution)/shard_map/ppermute | solution.py:62
  67.2 0.0 copy-start.1
  67.2 6.6 %collective-permute-done.12.refs_4_ = f32[3,128,256]{2,1,0:T(8,128)S(1)} collective-permute-done((f32[3,128,256]{2,1,0:T(8,128)S(1)}, f32[3,128,256]{2,1,0:T(8,128)S(1)}, u32[]{:S(2)}, u32[]{:S(2)}) %collective-permute-start.12) | collective-permute-done | bytes 393248 | tf_op jit(solution)/shard_map/ppermute | solution.py:62
  73.9 2.8 %collective-permute-done.9.refs_1_ = f32[3,128,256]{2,1,0:T(8,128)S(1)} collective-permute-done((f32[3,128,256]{2,1,0:T(8,128)S(1)}, f32[3,128,256]{2,1,0:T(8,128)S(1)}, u32[]{:S(2)}, u32[]{:S(2)}) %collective-permute-start.9) | collective-permute-done | bytes 393248 | tf_op jit(solution)/shard_map/ppermute | solution.py:62
  76.7 2.2 %shard_map.98 = f32[3,256,256]{2,1,0:T(8,128)S(1)} custom-call(f32[6,256,256]{2,1,0:T(8,128)S(1)} %shard_map.94.refs_0_.refs_10_, f32[3,128,256]{2,1,0:T(8,128)S(1)} %collective-permute-done.9.refs_1_, f32[3,128,256]{2,1,0:T(8,128)S(1)} %collective-permute-done.10.refs_2_, f32[3,128,256]{2,1,0:T(8,128)S(1)} %collective-permute-done.11.refs_3_, ...), custom_call_target="tpu_custom_call" | custom-call | tf_op jit(solution)/shard_map/pallas_call | solution.py:340
  78.9 1.2 %collective-permute-start.13 = (f32[3,256,256]{2,1,0:T(8,128)S(1)}, f32[3,256,256]{2,1,0:T(8,128)}, u32[]{:S(2)}, u32[]{:S(2)}) collective-permute-start(f32[3,256,256]{2,1,0:T(8,128)S(1)} %shard_map.98), channel_id=1, source_target_pairs={{0,64},{1,65},{2,66},{3,67},{4,68},{5,69},{6,70},{7,71},{8,72},{9,... | collective-permute-start | bytes 2359304 | tf_op jit(solution)/shard_map/ppermute | solution.py:62
  80.2 0.1 reduce_sum.9
  80.3 3.7 %collective-permute-start.19 = (f32[1,128]{1,0:T(1,128)S(1)}, f32[1,128]{1,0:T(1,128)S(1)}, u32[]{:S(2)}, u32[]{:S(2)}) collective-permute-start(f32[1,128]{1,0:T(1,128)S(1)} %pad_bitcast_fusion), channel_id=1, source_target_pairs={{0,1},{1,0},{2,3},{3,2},{4,5},{5,4},{6,7},{7,6},{8,9},{9,8},{10,11... | collective-permute-start | bytes 1544 | tf_op jit(solution)/shard_map/ppermute | solution.py:62
  84.0 6.9 %collective-permute-start.20 = (f32[1,128]{1,0:T(1,128)S(1)}, f32[1,128]{1,0:T(1,128)S(1)}, u32[]{:S(2)}, u32[]{:S(2)}) collective-permute-start(f32[1,128]{1,0:T(1,128)S(1)} %pad_bitcast_fusion), channel_id=1, source_target_pairs={{0,2},{1,3},{2,0},{3,1},{4,6},{5,7},{6,4},{7,5},{8,10},{9,11},{10,... | collective-permute-start | bytes 1544 | tf_op jit(solution)/shard_map/ppermute | solution.py:62
  90.8 1.5 %collective-permute-done.20 = f32[1,128]{1,0:T(1,128)S(1)} collective-permute-done((f32[1,128]{1,0:T(1,128)S(1)}, f32[1,128]{1,0:T(1,128)S(1)}, u32[]{:S(2)}, u32[]{:S(2)}) %collective-permute-start.20) | collective-permute-done | bytes 544 | tf_op jit(solution)/shard_map/ppermute | solution.py:62
  92.4 3.2 %collective-permute-done.21 = f32[1,128]{1,0:T(1,128)S(1)} collective-permute-done((f32[1,128]{1,0:T(1,128)S(1)}, f32[1,128]{1,0:T(1,128)S(1)}, u32[]{:S(2)}, u32[]{:S(2)}) %collective-permute-start.21) | collective-permute-done | bytes 544 | tf_op jit(solution)/shard_map/ppermute | solution.py:62
  95.6 0.2 collective-permute-start.5
  95.8 1.9 %collective-permute-start.6 = (f32[3,128,256]{2,1,0:T(8,128)S(1)}, f32[3,128,256]{2,1,0:T(8,128)S(1)}, u32[]{:S(2)}, u32[]{:S(2)}) collective-permute-start(f32[3,128,256]{2,1,0:T(8,128)S(1)} %get-tuple-element.16.refs_5_), channel_id=1, source_target_pairs={{0,16},{1,17},{2,18},{3,19},{4,20},{5,21},{6,22},{7,23},{8,24},{9,... | collective-permute-start | bytes 1179656 | tf_op jit(solution)/shard_map/ppermute | solution.py:62
  97.7 1.4 %collective-permute-start.8 = (f32[3,128,256]{2,1,0:T(8,128)S(1)}, f32[3,128,256]{2,1,0:T(8,128)S(1)}, u32[]{:S(2)}, u32[]{:S(2)}) collective-permute-start(f32[3,128,256]{2,1,0:T(8,128)S(1)} %get-tuple-element.24), channel_id=1, source_target_pairs={{0,48},{1,49},{2,50},{3,51},{4,52},{5,53},{6,54},{7,55},{8,56},{9,... | collective-permute-start | bytes 1179656 | tf_op jit(solution)/shard_map/ppermute | solution.py:62
  99.1 0.7 collective-permute-done.22
  99.8 0.5 slice_bitcast_fusion
  100.3 6.6 %collective-permute-done.5.refs_2_ = f32[3,128,256]{2,1,0:T(8,128)S(1)} collective-permute-done((f32[3,128,256]{2,1,0:T(8,128)S(1)}, f32[3,128,256]{2,1,0:T(8,128)S(1)}, u32[]{:S(2)}, u32[]{:S(2)}) %collective-permute-start.5) | collective-permute-done | bytes 393248 | tf_op jit(solution)/shard_map/ppermute | solution.py:62
  107.0 1.8 %collective-permute-done.6.refs_3_ = f32[3,128,256]{2,1,0:T(8,128)S(1)} collective-permute-done((f32[3,128,256]{2,1,0:T(8,128)S(1)}, f32[3,128,256]{2,1,0:T(8,128)S(1)}, u32[]{:S(2)}, u32[]{:S(2)}) %collective-permute-start.6) | collective-permute-done | bytes 393248 | tf_op jit(solution)/shard_map/ppermute | solution.py:62
  108.8 2.4 %collective-permute-done.8.refs_4_ = f32[3,128,256]{2,1,0:T(8,128)S(1)} collective-permute-done((f32[3,128,256]{2,1,0:T(8,128)S(1)}, f32[3,128,256]{2,1,0:T(8,128)S(1)}, u32[]{:S(2)}, u32[]{:S(2)}) %collective-permute-start.8) | collective-permute-done | bytes 393248 | tf_op jit(solution)/shard_map/ppermute | solution.py:62
  111.2 2.1 %collective-permute-done.4.refs_1_ = f32[3,128,256]{2,1,0:T(8,128)S(1)} collective-permute-done((f32[3,128,256]{2,1,0:T(8,128)}, f32[3,128,256]{2,1,0:T(8,128)S(1)}, u32[]{:S(2)}, u32[]{:S(2)}) %collective-permute-start.4) | collective-permute-done | bytes 393248 | tf_op jit(solution)/shard_map/ppermute | solution.py:62
  113.3 2.2 %shard_map.97 = f32[3,256,256]{2,1,0:T(8,128)S(1)} custom-call(f32[6,256,256]{2,1,0:T(8,128)S(1)} %shard_map.94.refs_0_.refs_10_, f32[3,128,256]{2,1,0:T(8,128)S(1)} %collective-permute-done.4.refs_1_, f32[3,128,256]{2,1,0:T(8,128)S(1)} %collective-permute-done.5.refs_2_, f32[3,128,256]{2,1,0:T(8,128)S(1)} %collective-permute-done.6.refs_3_, ...), custom_call_target="tpu_custom_call" | custom-call | tf_op jit(solution)/shard_map/pallas_call | solution.py:340
  115.5 2.2 %select_bitcast_fusion = f32[1,1,3,256,256]{4,3,2,1,0:T(8,128)} fusion(f32[3,256,256]{2,1,0:T(8,128)S(1)} %shard_map.97, f32[3,256,256]{2,1,0:T(8,128)} %collective-permute-done.13, pred[3]{0:T(512)(128)(4,1)S(1)} %iota_compare_fusion), kind=kLoop, calls=%fused_computation | loop fusion | flops 393216 | bytes 2359299 | tf_op jit(solution)/shard_map/reshape | solution.py:411
  (29 shorter events, 0.2 us)
Async XLA Ops:
  0.6 21.4 %collective-permute-start.2 = (f32[1024,2048]{1,0:T(8,128)}, f32[1024,2048]{1,0:T(8,128)}, u32[]{:S(2)}, u32[]{:S(2)}) collective-permute-start(f32[1024,2048]{1,0:T(8,128)} %refs_6_.5), channel_id=1, source_target_pairs={{0,8},{1,9},{2,10},{3,11},{4,12},{5,13},{6,14},{7,15},{8,0},{9,1},... | collective-permute-start | bytes 25165832 | tf_op jit(solution)/shard_map/ppermute | solution.py:62
  2.9 16.8 %all-to-all-start = ((f32[16,16,256]{2,1,0:T(8,128)}), f32[16,16,256]{2,1,0:T(8,128)S(1)}, u32[]{:S(2)}, u32[]{:S(2)}) async-start(f32[16,16,256]{2,1,0:T(8,128)} %payload.1), calls=%async_computation | async-start | bytes 524288 | tf_op jit(solution)/shard_map/all_to_all | solution.py:367
  10.1 11.9 %collective-permute-start.1 = (f32[3,2048]{1,0:T(4,128)}, f32[3,2048]{1,0:T(4,128)S(1)}, u32[]{:S(2)}, u32[]{:S(2)}) collective-permute-start(f32[3,2048]{1,0:T(4,128)} %z_ref.1), channel_id=1, source_target_pairs={{0,0},{1,16},{2,32},{3,48},{4,64},{5,80},{6,96},{7,112},{8,8},{9,2... | collective-permute-start | bytes 73736 | tf_op jit(solution)/shard_map/ppermute | solution.py:62
  19.7 2.3 %collective-permute-start = (s32[16,9]{1,0:T(8,128)S(1)}, s32[16,9]{1,0:T(8,128)S(1)}, u32[]{:S(2)}, u32[]{:S(2)}) collective-permute-start(s32[16,9]{1,0:T(8,128)S(1)} %convert_bitcast_fusion.refs_0_.own_ref), channel_id=1, source_target_pairs={{0,0},{1,16},{2,32},{3,48},{4,64},{5,80},{6,96},{7,112},{8,8},{9,2... | collective-permute-start | bytes 1736 | tf_op jit(solution)/shard_map/ppermute | solution.py:62
  26.8 28.6 %collective-permute-start.7 = (f32[6,128,256]{2,1,0:T(8,128)S(1)}, f32[6,128,256]{2,1,0:T(8,128)S(1)}, u32[]{:S(2)}, u32[]{:S(2)}) collective-permute-start(f32[6,128,256]{2,1,0:T(8,128)S(1)} %get-tuple-element.18.refs_1_), channel_id=1, source_target_pairs={{0,48},{1,49},{2,50},{3,51},{4,52},{5,53},{6,54},{7,55},{8,56},{9,... | collective-permute-start | bytes 2359304 | tf_op jit(solution)/shard_map/ppermute | solution.py:62
  32.5 26.4 %collective-permute-start.3 = (f32[6,128,256]{2,1,0:T(8,128)S(1)}, f32[6,128,256]{2,1,0:T(8,128)S(1)}, u32[]{:S(2)}, u32[]{:S(2)}) collective-permute-start(f32[6,128,256]{2,1,0:T(8,128)S(1)} %get-tuple-element.14.refs_0_), channel_id=1, source_target_pairs={{0,16},{1,17},{2,18},{3,19},{4,20},{5,21},{6,22},{7,23},{8,24},{9,... | collective-permute-start | bytes 2359304 | tf_op jit(solution)/shard_map/ppermute | solution.py:62
  38.7 3.1 %copy-start = (f32[3,2048]{1,0:T(4,128)S(1)}, f32[3,2048]{1,0:T(4,128)}, u32[]{:S(2)}) copy-start(f32[3,2048]{1,0:T(4,128)} %z_ref.1) | copy-start | bytes 73732
  48.5 1.3 %collective-permute-start.14 = (f32[4,2048]{1,0:T(4,128)S(1)}, f32[4,2048]{1,0:T(4,128)S(1)}, u32[]{:S(2)}, u32[]{:S(2)}) collective-permute-start(f32[4,2048]{1,0:T(4,128)S(1)} %gradients.1), channel_id=1, source_target_pairs={{0,8},{1,9},{2,10},{3,11},{4,12},{5,13},{6,14},{7,15},{8,0},{9,1},... | collective-permute-start | bytes 98312 | tf_op jit(solution)/shard_map/ppermute | solution.py:62
  49.8 5.5 %collective-permute-start.15 = (f32[4,2048]{1,0:T(4,128)S(1)}, f32[4,2048]{1,0:T(4,128)S(1)}, u32[]{:S(2)}, u32[]{:S(2)}) collective-permute-start(f32[4,2048]{1,0:T(4,128)S(1)} %add.49), channel_id=1, source_target_pairs={{0,64},{1,65},{2,66},{3,67},{4,68},{5,69},{6,70},{7,71},{8,72},{9,... | collective-permute-start | bytes 98312 | tf_op jit(solution)/shard_map/ppermute | solution.py:62
  50.3 17.0 %collective-permute-start.10 = (f32[3,128,256]{2,1,0:T(8,128)S(1)}, f32[3,128,256]{2,1,0:T(8,128)S(1)}, u32[]{:S(2)}, u32[]{:S(2)}) collective-permute-start(f32[3,128,256]{2,1,0:T(8,128)S(1)} %get-tuple-element.20.refs_6_), channel_id=1, source_target_pairs={{0,48},{1,49},{2,50},{3,51},{4,52},{5,53},{6,54},{7,55},{8,56},{9,... | collective-permute-start | bytes 1179656 | tf_op jit(solution)/shard_map/ppermute | solution.py:62
  54.0 13.3 %collective-permute-start.11 = (f32[3,128,256]{2,1,0:T(8,128)S(1)}, f32[3,128,256]{2,1,0:T(8,128)S(1)}, u32[]{:S(2)}, u32[]{:S(2)}) collective-permute-start(f32[3,128,256]{2,1,0:T(8,128)S(1)} %get-tuple-element.21.refs_3_), channel_id=1, source_target_pairs={{0,16},{1,17},{2,18},{3,19},{4,20},{5,21},{6,22},{7,23},{8,24},{9,... | collective-permute-start | bytes 1179656 | tf_op jit(solution)/shard_map/ppermute | solution.py:62
  55.3 8.1 %collective-permute-start.16 = (f32[4,2048]{1,0:T(4,128)S(1)}, f32[4,2048]{1,0:T(4,128)S(1)}, u32[]{:S(2)}, u32[]{:S(2)}) collective-permute-start(f32[4,2048]{1,0:T(4,128)S(1)} %add.50), channel_id=1, source_target_pairs={{0,16},{1,17},{2,18},{3,19},{4,20},{5,21},{6,22},{7,23},{8,24},{9,... | collective-permute-start | bytes 98312 | tf_op jit(solution)/shard_map/ppermute | solution.py:62
  55.4 10.5 %collective-permute-start.17 = (f32[4,2048]{1,0:T(4,128)S(1)}, f32[4,2048]{1,0:T(4,128)S(1)}, u32[]{:S(2)}, u32[]{:S(2)}) collective-permute-start(f32[4,2048]{1,0:T(4,128)S(1)} %add.50), channel_id=1, source_target_pairs={{0,32},{1,33},{2,34},{3,35},{4,36},{5,37},{6,38},{7,39},{8,40},{9,... | collective-permute-start | bytes 98312 | tf_op jit(solution)/shard_map/ppermute | solution.py:62
  58.9 8.3 %collective-permute-start.18 = (f32[4,2048]{1,0:T(4,128)S(1)}, f32[4,2048]{1,0:T(4,128)S(1)}, u32[]{:S(2)}, u32[]{:S(2)}) collective-permute-start(f32[4,2048]{1,0:T(4,128)S(1)} %add.50), channel_id=1, source_target_pairs={{0,48},{1,49},{2,50},{3,51},{4,52},{5,53},{6,54},{7,55},{8,56},{9,... | collective-permute-start | bytes 98312 | tf_op jit(solution)/shard_map/ppermute | solution.py:62
  63.4 10.4 %collective-permute-start.12 = (f32[3,128,256]{2,1,0:T(8,128)S(1)}, f32[3,128,256]{2,1,0:T(8,128)S(1)}, u32[]{:S(2)}, u32[]{:S(2)}) collective-permute-start(f32[3,128,256]{2,1,0:T(8,128)S(1)} %get-tuple-element.23), channel_id=1, source_target_pairs={{0,48},{1,49},{2,50},{3,51},{4,52},{5,53},{6,54},{7,55},{8,56},{9,... | collective-permute-start | bytes 1179656 | tf_op jit(solution)/shard_map/ppermute | solution.py:62
  65.9 10.7 %collective-permute-start.9 = (f32[3,128,256]{2,1,0:T(8,128)S(1)}, f32[3,128,256]{2,1,0:T(8,128)S(1)}, u32[]{:S(2)}, u32[]{:S(2)}) collective-permute-start(f32[3,128,256]{2,1,0:T(8,128)S(1)} %get-tuple-element.25), channel_id=1, source_target_pairs={{0,16},{1,17},{2,18},{3,19},{4,20},{5,21},{6,22},{7,23},{8,24},{9,... | collective-permute-start | bytes 1179656 | tf_op jit(solution)/shard_map/ppermute | solution.py:62
  67.2 12.9 %copy-start.1 = (f32[4,2048]{1,0:T(4,128)}, f32[4,2048]{1,0:T(4,128)S(1)}, u32[]{:S(2)}) copy-start(f32[4,2048]{1,0:T(4,128)S(1)} %add_add_fusion) | copy-start | bytes 98308
  78.9 36.6 %collective-permute-start.13 = (f32[3,256,256]{2,1,0:T(8,128)S(1)}, f32[3,256,256]{2,1,0:T(8,128)}, u32[]{:S(2)}, u32[]{:S(2)}) collective-permute-start(f32[3,256,256]{2,1,0:T(8,128)S(1)} %shard_map.98), channel_id=1, source_target_pairs={{0,64},{1,65},{2,66},{3,67},{4,68},{5,69},{6,70},{7,71},{8,72},{9,... | collective-permute-start | bytes 2359304 | tf_op jit(solution)/shard_map/ppermute | solution.py:62
  80.3 10.5 %collective-permute-start.19 = (f32[1,128]{1,0:T(1,128)S(1)}, f32[1,128]{1,0:T(1,128)S(1)}, u32[]{:S(2)}, u32[]{:S(2)}) collective-permute-start(f32[1,128]{1,0:T(1,128)S(1)} %pad_bitcast_fusion), channel_id=1, source_target_pairs={{0,1},{1,0},{2,3},{3,2},{4,5},{5,4},{6,7},{7,6},{8,9},{9,8},{10,11... | collective-permute-start | bytes 1544 | tf_op jit(solution)/shard_map/ppermute | solution.py:62
  84.0 8.4 %collective-permute-start.20 = (f32[1,128]{1,0:T(1,128)S(1)}, f32[1,128]{1,0:T(1,128)S(1)}, u32[]{:S(2)}, u32[]{:S(2)}) collective-permute-start(f32[1,128]{1,0:T(1,128)S(1)} %pad_bitcast_fusion), channel_id=1, source_target_pairs={{0,2},{1,3},{2,0},{3,1},{4,6},{5,7},{6,4},{7,5},{8,10},{9,11},{10,... | collective-permute-start | bytes 1544 | tf_op jit(solution)/shard_map/ppermute | solution.py:62
  90.8 4.8 %collective-permute-start.21 = (f32[1,128]{1,0:T(1,128)S(1)}, f32[1,128]{1,0:T(1,128)S(1)}, u32[]{:S(2)}, u32[]{:S(2)}) collective-permute-start(f32[1,128]{1,0:T(1,128)S(1)} %pad_bitcast_fusion), channel_id=1, source_target_pairs={{0,3},{1,2},{2,1},{3,0},{4,7},{5,6},{6,5},{7,4},{8,11},{9,10},{10,... | collective-permute-start | bytes 1544 | tf_op jit(solution)/shard_map/ppermute | solution.py:62
  95.6 4.2 %collective-permute-start.22 = (f32[1,128]{1,0:T(1,128)S(1)}, f32[1,128]{1,0:T(1,128)S(1)}, u32[]{:S(2)}, u32[]{:S(2)}) collective-permute-start(f32[1,128]{1,0:T(1,128)S(1)} %add_add_fusion.1), channel_id=1, source_target_pairs={{0,4},{1,5},{2,6},{3,7},{4,0},{5,1},{6,2},{7,3},{8,12},{9,13},{10,... | collective-permute-start | bytes 1544 | tf_op jit(solution)/shard_map/ppermute | solution.py:62
  95.6 11.4 %collective-permute-start.5 = (f32[3,128,256]{2,1,0:T(8,128)S(1)}, f32[3,128,256]{2,1,0:T(8,128)S(1)}, u32[]{:S(2)}, u32[]{:S(2)}) collective-permute-start(f32[3,128,256]{2,1,0:T(8,128)S(1)} %get-tuple-element.15.refs_8_), channel_id=1, source_target_pairs={{0,48},{1,49},{2,50},{3,51},{4,52},{5,53},{6,54},{7,55},{8,56},{9,... | collective-permute-start | bytes 1179656 | tf_op jit(solution)/shard_map/ppermute | solution.py:62
  95.8 12.9 %collective-permute-start.6 = (f32[3,128,256]{2,1,0:T(8,128)S(1)}, f32[3,128,256]{2,1,0:T(8,128)S(1)}, u32[]{:S(2)}, u32[]{:S(2)}) collective-permute-start(f32[3,128,256]{2,1,0:T(8,128)S(1)} %get-tuple-element.16.refs_5_), channel_id=1, source_target_pairs={{0,16},{1,17},{2,18},{3,19},{4,20},{5,21},{6,22},{7,23},{8,24},{9,... | collective-permute-start | bytes 1179656 | tf_op jit(solution)/shard_map/ppermute | solution.py:62
  97.7 13.5 %collective-permute-start.8 = (f32[3,128,256]{2,1,0:T(8,128)S(1)}, f32[3,128,256]{2,1,0:T(8,128)S(1)}, u32[]{:S(2)}, u32[]{:S(2)}) collective-permute-start(f32[3,128,256]{2,1,0:T(8,128)S(1)} %get-tuple-element.24), channel_id=1, source_target_pairs={{0,48},{1,49},{2,50},{3,51},{4,52},{5,53},{6,54},{7,55},{8,56},{9,... | collective-permute-start | bytes 1179656 | tf_op jit(solution)/shard_map/ppermute | solution.py:62
  99.8 13.5 %collective-permute-start.4 = (f32[3,128,256]{2,1,0:T(8,128)}, f32[3,128,256]{2,1,0:T(8,128)S(1)}, u32[]{:S(2)}, u32[]{:S(2)}) collective-permute-start(f32[3,128,256]{2,1,0:T(8,128)} %get-tuple-element.26), channel_id=1, source_target_pairs={{0,16},{1,17},{2,18},{3,19},{4,20},{5,21},{6,22},{7,23},{8,24},{9,... | collective-permute-start | bytes 1179656 | tf_op jit(solution)/shard_map/ppermute | solution.py:62

commit v5 on v4

--- a/solution.py
+++ b/solution.py
@@ -348,6 +348,36 @@
         ],
         compiler_params=grant(8),
     )(base, *tops, *bottoms)
+
+
+def finish_kernel(count_ref, base_ref, extra_ref, out_ref, extra, total, in_sems, out_sems):
+    def fetch(slot):
+        return pltpu.make_async_copy(extra_ref.at[slot], extra.at[slot], in_sems.at[slot])
+
+    def put(slot):
+        return pltpu.make_async_copy(total.at[slot], out_ref.at[slot], out_sems.at[slot])
+
+    for slot in range(SLOTS):
+        fetch(slot).start()
+    for slot in range(SLOTS):
+        fetch(slot).wait()
+        total[slot] = jnp.where(count_ref[0, 0] > slot, base_ref[slot] + extra[slot], 0.0)
+        put(slot).start()
+    for slot in range(SLOTS):
+        put(slot).wait()
+
+
+def finish(base, extra, count):
+    block = pltpu.VMEM((SLOTS, BS, BS), jnp.float32)
+    return pl.pallas_call(
+        finish_kernel,
+        out_shape=jax.ShapeDtypeStruct((SLOTS, BS, BS), jnp.float32),
+        in_specs=[SMEM, VMEM, HBM],
+        out_specs=HBM,
+        scratch_shapes=[block, block, pltpu.SemaphoreType.DMA((SLOTS,)), pltpu.SemaphoreType.DMA((SLOTS,))],
+        name="finish",
+        compiler_params=grant(8),
+    )(count, base, extra)
 
 
 def on_device(x_points, z_points, length_scales, dpsi_grad, block_rows, block_cols, block_count):
@@ -397,8 +427,7 @@
     sum_o = combine(here, 0, (sum_up_o, direct_down_o), (direct_up_o, sum_down_o))
     got_x = permute(sum_o, SWAP_XH)
     sum_w = combine(here, SLOTS, (sum_up_w, direct_down_w), (direct_up_w, sum_down_w))
-    live = jnp.arange(SLOTS, dtype=jnp.int32)[:, None, None] < block_count
-    dk_local = jnp.where(live, sum_w + got_x, 0.0)
+    dk_local = finish(sum_w, got_x, block_count)
 
     total = local + permute(local, SWAP_CORE)
     total = total + permute(total, SWAP_XH)

time: 118 us -> 117 us (level)
  other arithmetic: 3.38 us -> 1.95 us
    reshape x1 -> x0, other arithmetic: 2.17 us -> none  [on_device(): return (dk_local.reshape(1, 1, SLOTS, BS, BS), z_grad, scale_grad)]
where the time goes in v5:
time: 117 us
  starting transfers between devices  42.3 us (36%)
  waiting for transfers between devices  41.1 us (35%)
  Pallas kernels  29.3 us (25%)
  other arithmetic  1.95 us (2%)
  between operations  1.67 us (1%)
    ppermute x23, starting transfers between devices, permute(): return lax.ppermute(value, AXES, perm)  35 us
    ppermute x23, waiting for transfers between devices, permute(): return lax.ppermute(value, AXES, perm)  33 us
    pallas_call x3, Pallas kernels, products(): pl.pallas_call(kernel, out_shape=[pltpu.VMEM(shape, jnp.float32) for shap...  14.1 us
    all_to_all x1, waiting for transfers between devices, on_device(): payload = lax.all_to_all(outgoing, DP, 0, 0, tiled=True)  8.1 us
    all_to_all x1, starting transfers between devices, on_device(): payload = lax.all_to_all(outgoing, DP, 0, 0, tiled=True)  7.25 us
    pallas_call x1, Pallas kernels, gradients(): pl.pallas_call(gradient_kernel, out_shape=jax.ShapeDtypeStruct((4, z_own....  6.66 us
    pallas_call x2, Pallas kernels, combine(): pl.pallas_call(kernel, out_shape=pltpu.VMEM((SLOTS, BS, BS), jnp.float32)...  4.48 us
  transfers between devices with their start and end apart: 24, of which 14 were waited for; matrix products, arithmetic and copies ran while one was open for 2% of the time, Pallas kernels for 18%

profile of v5, /device:TPU:0, one launch (start us, length us, event | category | flops | bytes accessed | tf_op | source)
XLA Modules:
  0.0 116.9 jit_solution(5672781575279084409)
XLA Ops:
  0.6 0.1 collective-permute-start.2
  1.4 1.5 %payload.1 = f32[16,16,256]{2,1,0:T(8,128)} custom-call(s32[1,1,3]{2,1,0:T(1,128)} %rows_ref.1, s32[1,1,3]{2,1,0:T(1,128)} %cols_ref.1, s32[1,1]{1,0:T(1,128)S(6)} %copy.14.count_ref, f32[3,2048]{1,0:T(4,128)} %x_ref.1), custom_call_target="tpu_custom_call" | custom-call | tf_op jit(solution)/shard_map/payload/pallas_call | solution.py:388
  2.9 7.3 %all-to-all-start = ((f32[16,16,256]{2,1,0:T(8,128)}), f32[16,16,256]{2,1,0:T(8,128)S(1)}, u32[]{:S(2)}, u32[]{:S(2)}) async-start(f32[16,16,256]{2,1,0:T(8,128)} %payload.1), calls=%async_computation | async-start | bytes 524288 | tf_op jit(solution)/shard_map/all_to_all | solution.py:397
  10.1 1.4 %collective-permute-start.1 = (f32[3,2048]{1,0:T(4,128)}, f32[3,2048]{1,0:T(4,128)S(1)}, u32[]{:S(2)}, u32[]{:S(2)}) collective-permute-start(f32[3,2048]{1,0:T(4,128)} %z_ref.1), channel_id=1, source_target_pairs={{0,0},{1,16},{2,32},{3,48},{4,64},{5,80},{6,96},{7,112},{8,8},{9,2... | collective-permute-start | bytes 73736 | tf_op jit(solution)/shard_map/ppermute | solution.py:62
  11.6 8.1 %all-to-all-done.pay_ref = f32[16,16,256]{2,1,0:T(8,128)S(1)} async-done(((f32[16,16,256]{2,1,0:T(8,128)}), f32[16,16,256]{2,1,0:T(8,128)S(1)}, u32[]{:S(2)}, u32[]{:S(2)}) %all-to-all-start) | async-done | bytes 262176 | tf_op jit(solution)/shard_map/all_to_all | solution.py:397
  19.7 0.7 collective-permute-start
  20.4 0.1 pad_add_fusion.pos_ref.refs_2_
  20.4 1.6 %columns.1.refs_4_.pay_ref = f32[8,3,256,128]{3,2,1,0:T(8,128)S(1)} custom-call(s32[3]{0:T(128)S(1)} %pad_add_fusion.pos_ref.refs_2_, f32[3]{0:T(128)} %scale_ref.3, f32[16,16,256]{2,1,0:T(8,128)S(1)} %all-to-all-done.pay_ref), custom_call_target="tpu_custom_call" | custom-call | tf_op jit(solution)/shard_map/columns/pallas_call | solution.py:402
  22.1 4.7 %shard_map.96 = (f32[6,128,256]{2,1,0:T(8,128)S(1)}, f32[6,128,256]{2,1,0:T(8,128)S(1)}) custom-call(s32[16,9]{1,0:T(8,128)S(1)} %convert_bitcast_fusion.refs_0_.own_ref, s32[16,9]{1,0:T(8,128)S(1)} %collective-permute-done.refs_1_.near_ref, s32[3]{0:T(128)S(1)} %pad_add_fusion.pos_ref.refs_2_, f32[3]{0:T(128)} %scale_ref.3, ...), custom_call_target="tpu_custom_call" | custom-call | tf_op jit(solution)/shard_map/pallas_call | solution.py:240
  26.8 5.7 %collective-permute-start.7 = (f32[6,128,256]{2,1,0:T(8,128)S(1)}, f32[6,128,256]{2,1,0:T(8,128)S(1)}, u32[]{:S(2)}, u32[]{:S(2)}) collective-permute-start(f32[6,128,256]{2,1,0:T(8,128)S(1)} %get-tuple-element.18.refs_1_), channel_id=1, source_target_pairs={{0,48},{1,49},{2,50},{3,51},{4,52},{5,53},{6,54},{7,55},{8,56},{9,... | collective-permute-start | bytes 2359304 | tf_op jit(solution)/shard_map/ppermute | solution.py:62
  32.5 6.2 %shard_map.95 = (f32[3,128,256]{2,1,0:T(8,128)S(1)}, f32[3,128,256]{2,1,0:T(8,128)S(1)}, f32[3,128,256]{2,1,0:T(8,128)S(1)}, f32[3,128,256]{2,1,0:T(8,128)S(1)},...) custom-call(s32[16,9]{1,0:T(8,128)S(1)} %convert_bitcast_fusion.refs, ...), custom_call_target="tpu_custom_call" | custom-call | tf_op jit(solution)/shard_map/pallas_call | solution.py:240
  38.7 3.2 %shard_map.94.refs_0_.refs_10_ = f32[6,256,256]{2,1,0:T(8,128)S(1)} custom-call(s32[16,9]{1,0:T(8,128)S(1)} %convert_bitcast_fusion.refs_0_.own_ref, s32[16,9]{1,0:T(8,128)S(1)} %collective-permute-done.refs_1_.near_ref, s32[3]{0:T(128)S(1)} %pad_add_fusion.pos_ref.refs_2_, f32[3]{0:T(128)} %scale_ref.3, f32[8,3,256,128]{3,2,1,0:T(8,128)S(1)} %columns.1.refs_4_.pay_ref, ...), custom_call_target="tpu_custom_call" | custom-call | tf_op jit(solution)/shard_map/pallas_call | solution.py:240
  41.9 6.7 %gradients.1 = f32[4,2048]{1,0:T(4,128)S(1)} custom-call(s32[16,9]{1,0:T(8,128)S(1)} %convert_bitcast_fusion.refs_0_.own_ref, s32[16,9]{1,0:T(8,128)S(1)} %collective-permute-done.refs_1_.near_ref, s32[3]{0:T(128)S(1)} %pad_add_fusion.pos_ref.refs_2_, f32[3]{0:T(128)} %scale_ref.3, f32[8,3,256,128]{3,2,1,0:T(8,128)S(1)} %columns.1.refs_4_.pay_ref, ...), custom_call_target="tpu_custom_call" | custom-call | tf_op jit(solution)/shard_map/gradients/pallas_call | solution.py:309
  48.6 0.5 collective-permute-start.14
  49.1 0.9 collective-permute-done.14
  50.0 0.5 collective-permute-start.15
  50.4 3.7 %collective-permute-start.10 = (f32[3,128,256]{2,1,0:T(8,128)S(1)}, f32[3,128,256]{2,1,0:T(8,128)S(1)}, u32[]{:S(2)}, u32[]{:S(2)}) collective-permute-start(f32[3,128,256]{2,1,0:T(8,128)S(1)} %get-tuple-element.20.refs_6_), channel_id=1, source_target_pairs={{0,48},{1,49},{2,50},{3,51},{4,52},{5,53},{6,54},{7,55},{8,56},{9,... | collective-permute-start | bytes 1179656 | tf_op jit(solution)/shard_map/ppermute | solution.py:62
  54.1 1.3 %collective-permute-done.15 = f32[4,2048]{1,0:T(4,128)S(1)} collective-permute-done((f32[4,2048]{1,0:T(4,128)S(1)}, f32[4,2048]{1,0:T(4,128)S(1)}, u32[]{:S(2)}, u32[]{:S(2)}) %collective-permute-start.15) | collective-permute-done | bytes 32800 | tf_op jit(solution)/shard_map/ppermute | solution.py:62
  55.5 0.1 collective-permute-start.16
  55.6 3.3 %collective-permute-start.17 = (f32[4,2048]{1,0:T(4,128)S(1)}, f32[4,2048]{1,0:T(4,128)S(1)}, u32[]{:S(2)}, u32[]{:S(2)}) collective-permute-start(f32[4,2048]{1,0:T(4,128)S(1)} %add.46), channel_id=1, source_target_pairs={{0,32},{1,33},{2,34},{3,35},{4,36},{5,37},{6,38},{7,39},{8,40},{9,... | collective-permute-start | bytes 98312 | tf_op jit(solution)/shard_map/ppermute | solution.py:62
  58.9 0.9 slice_add_fusion
  59.8 1.3 %collective-permute-start.18 = (f32[4,2048]{1,0:T(4,128)S(1)}, f32[4,2048]{1,0:T(4,128)S(1)}, u32[]{:S(2)}, u32[]{:S(2)}) collective-permute-start(f32[4,2048]{1,0:T(4,128)S(1)} %add.46), channel_id=1, source_target_pairs={{0,48},{1,49},{2,50},{3,51},{4,52},{5,53},{6,54},{7,55},{8,56},{9,... | collective-permute-start | bytes 98312 | tf_op jit(solution)/shard_map/ppermute | solution.py:62
  61.1 0.8 slice_add_fusion.1
  62.0 1.6 %collective-permute-done.16 = f32[4,2048]{1,0:T(4,128)S(1)} collective-permute-done((f32[4,2048]{1,0:T(4,128)S(1)}, f32[4,2048]{1,0:T(4,128)S(1)}, u32[]{:S(2)}, u32[]{:S(2)}) %collective-permute-start.16) | collective-permute-done | bytes 32800 | tf_op jit(solution)/shard_map/ppermute | solution.py:62
  63.6 2.5 %collective-permute-start.12 = (f32[3,128,256]{2,1,0:T(8,128)S(1)}, f32[3,128,256]{2,1,0:T(8,128)S(1)}, u32[]{:S(2)}, u32[]{:S(2)}) collective-permute-start(f32[3,128,256]{2,1,0:T(8,128)S(1)} %get-tuple-element.23), channel_id=1, source_target_pairs={{0,48},{1,49},{2,50},{3,51},{4,52},{5,53},{6,54},{7,55},{8,56},{9,... | collective-permute-start | bytes 1179656 | tf_op jit(solution)/shard_map/ppermute | solution.py:62
  66.1 0.0 collective-permute-start.9
  66.1 1.3 %collective-permute-done.18 = f32[4,2048]{1,0:T(4,128)S(1)} collective-permute-done((f32[4,2048]{1,0:T(4,128)S(1)}, f32[4,2048]{1,0:T(4,128)S(1)}, u32[]{:S(2)}, u32[]{:S(2)}) %collective-permute-start.18) | collective-permute-done | bytes 32800 | tf_op jit(solution)/shard_map/ppermute | solution.py:62
  67.4 0.0 copy-start.2
  67.4 6.6 %collective-permute-done.12.refs_4_ = f32[3,128,256]{2,1,0:T(8,128)S(1)} collective-permute-done((f32[3,128,256]{2,1,0:T(8,128)S(1)}, f32[3,128,256]{2,1,0:T(8,128)S(1)}, u32[]{:S(2)}, u32[]{:S(2)}) %collective-permute-start.12) | collective-permute-done | bytes 393248 | tf_op jit(solution)/shard_map/ppermute | solution.py:62
  74.0 2.8 %collective-permute-done.9.refs_1_ = f32[3,128,256]{2,1,0:T(8,128)S(1)} collective-permute-done((f32[3,128,256]{2,1,0:T(8,128)S(1)}, f32[3,128,256]{2,1,0:T(8,128)S(1)}, u32[]{:S(2)}, u32[]{:S(2)}) %collective-permute-start.9) | collective-permute-done | bytes 393248 | tf_op jit(solution)/shard_map/ppermute | solution.py:62
  76.8 2.2 %shard_map.98 = f32[3,256,256]{2,1,0:T(8,128)S(1)} custom-call(f32[6,256,256]{2,1,0:T(8,128)S(1)} %shard_map.94.refs_0_.refs_10_, f32[3,128,256]{2,1,0:T(8,128)S(1)} %collective-permute-done.9.refs_1_, f32[3,128,256]{2,1,0:T(8,128)S(1)} %collective-permute-done.10.refs_2_, f32[3,128,256]{2,1,0:T(8,128)S(1)} %collective-permute-done.11.refs_3_, ...), custom_call_target="tpu_custom_call" | custom-call | tf_op jit(solution)/shard_map/pallas_call | solution.py:340
  79.1 1.2 %collective-permute-start.13 = (f32[3,256,256]{2,1,0:T(8,128)S(1)}, f32[3,256,256]{2,1,0:T(8,128)S(1)}, u32[]{:S(2)}, u32[]{:S(2)}) collective-permute-start(f32[3,256,256]{2,1,0:T(8,128)S(1)} %shard_map.98), channel_id=1, source_target_pairs={{0,64},{1,65},{2,66},{3,67},{4,68},{5,69},{6,70},{7,71},{8,72},{9,... | collective-permute-start | bytes 2359304 | tf_op jit(solution)/shard_map/ppermute | solution.py:62
  80.3 0.1 reduce_sum.9
  80.5 3.7 %collective-permute-start.19 = (f32[1,128]{1,0:T(1,128)S(1)}, f32[1,128]{1,0:T(1,128)S(1)}, u32[]{:S(2)}, u32[]{:S(2)}) collective-permute-start(f32[1,128]{1,0:T(1,128)S(1)} %pad_bitcast_fusion), channel_id=1, source_target_pairs={{0,1},{1,0},{2,3},{3,2},{4,5},{5,4},{6,7},{7,6},{8,9},{9,8},{10,11... | collective-permute-start | bytes 1544 | tf_op jit(solution)/shard_map/ppermute | solution.py:62
  84.1 6.9 %collective-permute-start.20 = (f32[1,128]{1,0:T(1,128)S(1)}, f32[1,128]{1,0:T(1,128)S(1)}, u32[]{:S(2)}, u32[]{:S(2)}) collective-permute-start(f32[1,128]{1,0:T(1,128)S(1)} %pad_bitcast_fusion), channel_id=1, source_target_pairs={{0,2},{1,3},{2,0},{3,1},{4,6},{5,7},{6,4},{7,5},{8,10},{9,11},{10,... | collective-permute-start | bytes 1544 | tf_op jit(solution)/shard_map/ppermute | solution.py:62
  91.0 1.5 %collective-permute-done.20 = f32[1,128]{1,0:T(1,128)S(1)} collective-permute-done((f32[1,128]{1,0:T(1,128)S(1)}, f32[1,128]{1,0:T(1,128)S(1)}, u32[]{:S(2)}, u32[]{:S(2)}) %collective-permute-start.20) | collective-permute-done | bytes 544 | tf_op jit(solution)/shard_map/ppermute | solution.py:62
  92.5 3.2 %collective-permute-done.21 = f32[1,128]{1,0:T(1,128)S(1)} collective-permute-done((f32[1,128]{1,0:T(1,128)S(1)}, f32[1,128]{1,0:T(1,128)S(1)}, u32[]{:S(2)}, u32[]{:S(2)}) %collective-permute-start.21) | collective-permute-done | bytes 544 | tf_op jit(solution)/shard_map/ppermute | solution.py:62
  95.8 0.2 collective-permute-start.5
  96.0 1.9 %collective-permute-start.6 = (f32[3,128,256]{2,1,0:T(8,128)S(1)}, f32[3,128,256]{2,1,0:T(8,128)S(1)}, u32[]{:S(2)}, u32[]{:S(2)}) collective-permute-start(f32[3,128,256]{2,1,0:T(8,128)S(1)} %get-tuple-element.16.refs_5_), channel_id=1, source_target_pairs={{0,16},{1,17},{2,18},{3,19},{4,20},{5,21},{6,22},{7,23},{8,24},{9,... | collective-permute-start | bytes 1179656 | tf_op jit(solution)/shard_map/ppermute | solution.py:62
  97.9 1.4 %collective-permute-start.8 = (f32[3,128,256]{2,1,0:T(8,128)}, f32[3,128,256]{2,1,0:T(8,128)S(1)}, u32[]{:S(2)}, u32[]{:S(2)}) collective-permute-start(f32[3,128,256]{2,1,0:T(8,128)} %get-tuple-element.24), channel_id=1, source_target_pairs={{0,48},{1,49},{2,50},{3,51},{4,52},{5,53},{6,54},{7,55},{8,56},{9,... | collective-permute-start | bytes 1179656 | tf_op jit(solution)/shard_map/ppermute | solution.py:62
  99.2 0.7 collective-permute-done.22
  100.0 0.5 slice_bitcast_fusion
  100.5 6.8 %collective-permute-done.5.refs_2_ = f32[3,128,256]{2,1,0:T(8,128)S(1)} collective-permute-done((f32[3,128,256]{2,1,0:T(8,128)}, f32[3,128,256]{2,1,0:T(8,128)S(1)}, u32[]{:S(2)}, u32[]{:S(2)}) %collective-permute-start.5) | collective-permute-done | bytes 393248 | tf_op jit(solution)/shard_map/ppermute | solution.py:62
  107.2 1.8 %collective-permute-done.6.refs_3_ = f32[3,128,256]{2,1,0:T(8,128)S(1)} collective-permute-done((f32[3,128,256]{2,1,0:T(8,128)S(1)}, f32[3,128,256]{2,1,0:T(8,128)S(1)}, u32[]{:S(2)}, u32[]{:S(2)}) %collective-permute-start.6) | collective-permute-done | bytes 393248 | tf_op jit(solution)/shard_map/ppermute | solution.py:62
  109.0 2.4 %collective-permute-done.8.refs_4_ = f32[3,128,256]{2,1,0:T(8,128)S(1)} collective-permute-done((f32[3,128,256]{2,1,0:T(8,128)}, f32[3,128,256]{2,1,0:T(8,128)S(1)}, u32[]{:S(2)}, u32[]{:S(2)}) %collective-permute-start.8) | collective-permute-done | bytes 393248 | tf_op jit(solution)/shard_map/ppermute | solution.py:62
  111.5 2.0 %collective-permute-done.4.refs_1_ = f32[3,128,256]{2,1,0:T(8,128)S(1)} collective-permute-done((f32[3,128,256]{2,1,0:T(8,128)}, f32[3,128,256]{2,1,0:T(8,128)S(1)}, u32[]{:S(2)}, u32[]{:S(2)}) %collective-permute-start.4) | collective-permute-done | bytes 393248 | tf_op jit(solution)/shard_map/ppermute | solution.py:62
  113.4 2.2 %shard_map.97.base_ref = f32[3,256,256]{2,1,0:T(8,128)S(1)} custom-call(f32[6,256,256]{2,1,0:T(8,128)S(1)} %shard_map.94.refs_0_.refs_10_, f32[3,128,256]{2,1,0:T(8,128)S(1)} %collective-permute-done.4.refs_1_, f32[3,128,256]{2,1,0:T(8,128)S(1)} %collective-permute-done.5.refs_2_, f32[3,128,256]{2,1,0:T(8,128)S(1)} %collective-permute-done.6.refs_3_, ...), custom_call_target="tpu_custom_call" | custom-call | tf_op jit(solution)/shard_map/pallas_call | solution.py:340
  115.7 1.0 finish.1
  (30 shorter events, 0.1 us)
Async XLA Ops:
  0.6 21.4 %collective-permute-start.2 = (f32[1024,2048]{1,0:T(8,128)}, f32[1024,2048]{1,0:T(8,128)}, u32[]{:S(2)}, u32[]{:S(2)}) collective-permute-start(f32[1024,2048]{1,0:T(8,128)} %refs_6_.5), channel_id=1, source_target_pairs={{0,8},{1,9},{2,10},{3,11},{4,12},{5,13},{6,14},{7,15},{8,0},{9,1},... | collective-permute-start | bytes 25165832 | tf_op jit(solution)/shard_map/ppermute | solution.py:62
  2.9 16.8 %all-to-all-start = ((f32[16,16,256]{2,1,0:T(8,128)}), f32[16,16,256]{2,1,0:T(8,128)S(1)}, u32[]{:S(2)}, u32[]{:S(2)}) async-start(f32[16,16,256]{2,1,0:T(8,128)} %payload.1), calls=%async_computation | async-start | bytes 524288 | tf_op jit(solution)/shard_map/all_to_all | solution.py:397
  10.1 11.9 %collective-permute-start.1 = (f32[3,2048]{1,0:T(4,128)}, f32[3,2048]{1,0:T(4,128)S(1)}, u32[]{:S(2)}, u32[]{:S(2)}) collective-permute-start(f32[3,2048]{1,0:T(4,128)} %z_ref.1), channel_id=1, source_target_pairs={{0,0},{1,16},{2,32},{3,48},{4,64},{5,80},{6,96},{7,112},{8,8},{9,2... | collective-permute-start | bytes 73736 | tf_op jit(solution)/shard_map/ppermute | solution.py:62
  19.7 2.3 %collective-permute-start = (s32[16,9]{1,0:T(8,128)S(1)}, s32[16,9]{1,0:T(8,128)S(1)}, u32[]{:S(2)}, u32[]{:S(2)}) collective-permute-start(s32[16,9]{1,0:T(8,128)S(1)} %convert_bitcast_fusion.refs_0_.own_ref), channel_id=1, source_target_pairs={{0,0},{1,16},{2,32},{3,48},{4,64},{5,80},{6,96},{7,112},{8,8},{9,2... | collective-permute-start | bytes 1736 | tf_op jit(solution)/shard_map/ppermute | solution.py:62
  26.8 28.8 %collective-permute-start.7 = (f32[6,128,256]{2,1,0:T(8,128)S(1)}, f32[6,128,256]{2,1,0:T(8,128)S(1)}, u32[]{:S(2)}, u32[]{:S(2)}) collective-permute-start(f32[6,128,256]{2,1,0:T(8,128)S(1)} %get-tuple-element.18.refs_1_), channel_id=1, source_target_pairs={{0,48},{1,49},{2,50},{3,51},{4,52},{5,53},{6,54},{7,55},{8,56},{9,... | collective-permute-start | bytes 2359304 | tf_op jit(solution)/shard_map/ppermute | solution.py:62
  32.5 27.3 %collective-permute-start.3 = (f32[6,128,256]{2,1,0:T(8,128)S(1)}, f32[6,128,256]{2,1,0:T(8,128)S(1)}, u32[]{:S(2)}, u32[]{:S(2)}) collective-permute-start(f32[6,128,256]{2,1,0:T(8,128)S(1)} %get-tuple-element.14.refs_0_), channel_id=1, source_target_pairs={{0,16},{1,17},{2,18},{3,19},{4,20},{5,21},{6,22},{7,23},{8,24},{9,... | collective-permute-start | bytes 2359304 | tf_op jit(solution)/shard_map/ppermute | solution.py:62
  38.7 3.2 %copy-start = (f32[3,128,256]{2,1,0:T(8,128)}, f32[3,128,256]{2,1,0:T(8,128)S(1)}, u32[]{:S(2)}) copy-start(f32[3,128,256]{2,1,0:T(8,128)S(1)} %get-tuple-element.15.refs_8_) | copy-start | bytes 1179652
  38.7 3.2 %copy-start.1 = (f32[3,2048]{1,0:T(4,128)S(1)}, f32[3,2048]{1,0:T(4,128)}, u32[]{:S(2)}) copy-start(f32[3,2048]{1,0:T(4,128)} %z_ref.1) | copy-start | bytes 73732
  48.6 1.3 %collective-permute-start.14 = (f32[4,2048]{1,0:T(4,128)S(1)}, f32[4,2048]{1,0:T(4,128)S(1)}, u32[]{:S(2)}, u32[]{:S(2)}) collective-permute-start(f32[4,2048]{1,0:T(4,128)S(1)} %gradients.1), channel_id=1, source_target_pairs={{0,8},{1,9},{2,10},{3,11},{4,12},{5,13},{6,14},{7,15},{8,0},{9,1},... | collective-permute-start | bytes 98312 | tf_op jit(solution)/shard_map/ppermute | solution.py:62
  50.0 5.5 %collective-permute-start.15 = (f32[4,2048]{1,0:T(4,128)S(1)}, f32[4,2048]{1,0:T(4,128)S(1)}, u32[]{:S(2)}, u32[]{:S(2)}) collective-permute-start(f32[4,2048]{1,0:T(4,128)S(1)} %add.45), channel_id=1, source_target_pairs={{0,64},{1,65},{2,66},{3,67},{4,68},{5,69},{6,70},{7,71},{8,72},{9,... | collective-permute-start | bytes 98312 | tf_op jit(solution)/shard_map/ppermute | solution.py:62
  50.4 17.0 %collective-permute-start.10 = (f32[3,128,256]{2,1,0:T(8,128)S(1)}, f32[3,128,256]{2,1,0:T(8,128)S(1)}, u32[]{:S(2)}, u32[]{:S(2)}) collective-permute-start(f32[3,128,256]{2,1,0:T(8,128)S(1)} %get-tuple-element.20.refs_6_), channel_id=1, source_target_pairs={{0,48},{1,49},{2,50},{3,51},{4,52},{5,53},{6,54},{7,55},{8,56},{9,... | collective-permute-start | bytes 1179656 | tf_op jit(solution)/shard_map/ppermute | solution.py:62
  54.1 13.3 %collective-permute-start.11 = (f32[3,128,256]{2,1,0:T(8,128)S(1)}, f32[3,128,256]{2,1,0:T(8,128)S(1)}, u32[]{:S(2)}, u32[]{:S(2)}) collective-permute-start(f32[3,128,256]{2,1,0:T(8,128)S(1)} %get-tuple-element.21.refs_3_), channel_id=1, source_target_pairs={{0,16},{1,17},{2,18},{3,19},{4,20},{5,21},{6,22},{7,23},{8,24},{9,... | collective-permute-start | bytes 1179656 | tf_op jit(solution)/shard_map/ppermute | solution.py:62
  55.5 8.1 %collective-permute-start.16 = (f32[4,2048]{1,0:T(4,128)S(1)}, f32[4,2048]{1,0:T(4,128)S(1)}, u32[]{:S(2)}, u32[]{:S(2)}) collective-permute-start(f32[4,2048]{1,0:T(4,128)S(1)} %add.46), channel_id=1, source_target_pairs={{0,16},{1,17},{2,18},{3,19},{4,20},{5,21},{6,22},{7,23},{8,24},{9,... | collective-permute-start | bytes 98312 | tf_op jit(solution)/shard_map/ppermute | solution.py:62
  55.6 10.5 %collective-permute-start.17 = (f32[4,2048]{1,0:T(4,128)S(1)}, f32[4,2048]{1,0:T(4,128)S(1)}, u32[]{:S(2)}, u32[]{:S(2)}) collective-permute-start(f32[4,2048]{1,0:T(4,128)S(1)} %add.46), channel_id=1, source_target_pairs={{0,32},{1,33},{2,34},{3,35},{4,36},{5,37},{6,38},{7,39},{8,40},{9,... | collective-permute-start | bytes 98312 | tf_op jit(solution)/shard_map/ppermute | solution.py:62
  59.8 7.6 %collective-permute-start.18 = (f32[4,2048]{1,0:T(4,128)S(1)}, f32[4,2048]{1,0:T(4,128)S(1)}, u32[]{:S(2)}, u32[]{:S(2)}) collective-permute-start(f32[4,2048]{1,0:T(4,128)S(1)} %add.46), channel_id=1, source_target_pairs={{0,48},{1,49},{2,50},{3,51},{4,52},{5,53},{6,54},{7,55},{8,56},{9,... | collective-permute-start | bytes 98312 | tf_op jit(solution)/shard_map/ppermute | solution.py:62
  63.6 10.4 %collective-permute-start.12 = (f32[3,128,256]{2,1,0:T(8,128)S(1)}, f32[3,128,256]{2,1,0:T(8,128)S(1)}, u32[]{:S(2)}, u32[]{:S(2)}) collective-permute-start(f32[3,128,256]{2,1,0:T(8,128)S(1)} %get-tuple-element.23), channel_id=1, source_target_pairs={{0,48},{1,49},{2,50},{3,51},{4,52},{5,53},{6,54},{7,55},{8,56},{9,... | collective-permute-start | bytes 1179656 | tf_op jit(solution)/shard_map/ppermute | solution.py:62
  66.1 10.7 %collective-permute-start.9 = (f32[3,128,256]{2,1,0:T(8,128)S(1)}, f32[3,128,256]{2,1,0:T(8,128)S(1)}, u32[]{:S(2)}, u32[]{:S(2)}) collective-permute-start(f32[3,128,256]{2,1,0:T(8,128)S(1)} %get-tuple-element.25), channel_id=1, source_target_pairs={{0,16},{1,17},{2,18},{3,19},{4,20},{5,21},{6,22},{7,23},{8,24},{9,... | collective-permute-start | bytes 1179656 | tf_op jit(solution)/shard_map/ppermute | solution.py:62
  67.4 12.9 %copy-start.2 = (f32[4,2048]{1,0:T(4,128)}, f32[4,2048]{1,0:T(4,128)S(1)}, u32[]{:S(2)}) copy-start(f32[4,2048]{1,0:T(4,128)S(1)} %add_add_fusion) | copy-start | bytes 98308
  79.1 36.6 %collective-permute-start.13 = (f32[3,256,256]{2,1,0:T(8,128)S(1)}, f32[3,256,256]{2,1,0:T(8,128)S(1)}, u32[]{:S(2)}, u32[]{:S(2)}) collective-permute-start(f32[3,256,256]{2,1,0:T(8,128)S(1)} %shard_map.98), channel_id=1, source_target_pairs={{0,64},{1,65},{2,66},{3,67},{4,68},{5,69},{6,70},{7,71},{8,72},{9,... | collective-permute-start | bytes 2359304 | tf_op jit(solution)/shard_map/ppermute | solution.py:62
  80.5 10.5 %collective-permute-start.19 = (f32[1,128]{1,0:T(1,128)S(1)}, f32[1,128]{1,0:T(1,128)S(1)}, u32[]{:S(2)}, u32[]{:S(2)}) collective-permute-start(f32[1,128]{1,0:T(1,128)S(1)} %pad_bitcast_fusion), channel_id=1, source_target_pairs={{0,1},{1,0},{2,3},{3,2},{4,5},{5,4},{6,7},{7,6},{8,9},{9,8},{10,11... | collective-permute-start | bytes 1544 | tf_op jit(solution)/shard_map/ppermute | solution.py:62
  84.1 8.4 %collective-permute-start.20 = (f32[1,128]{1,0:T(1,128)S(1)}, f32[1,128]{1,0:T(1,128)S(1)}, u32[]{:S(2)}, u32[]{:S(2)}) collective-permute-start(f32[1,128]{1,0:T(1,128)S(1)} %pad_bitcast_fusion), channel_id=1, source_target_pairs={{0,2},{1,3},{2,0},{3,1},{4,6},{5,7},{6,4},{7,5},{8,10},{9,11},{10,... | collective-permute-start | bytes 1544 | tf_op jit(solution)/shard_map/ppermute | solution.py:62
  91.0 4.8 %collective-permute-start.21 = (f32[1,128]{1,0:T(1,128)S(1)}, f32[1,128]{1,0:T(1,128)S(1)}, u32[]{:S(2)}, u32[]{:S(2)}) collective-permute-start(f32[1,128]{1,0:T(1,128)S(1)} %pad_bitcast_fusion), channel_id=1, source_target_pairs={{0,3},{1,2},{2,1},{3,0},{4,7},{5,6},{6,5},{7,4},{8,11},{9,10},{10,... | collective-permute-start | bytes 1544 | tf_op jit(solution)/shard_map/ppermute | solution.py:62
  95.8 4.2 %collective-permute-start.22 = (f32[1,128]{1,0:T(1,128)S(1)}, f32[1,128]{1,0:T(1,128)S(1)}, u32[]{:S(2)}, u32[]{:S(2)}) collective-permute-start(f32[1,128]{1,0:T(1,128)S(1)} %add_add_fusion.1), channel_id=1, source_target_pairs={{0,4},{1,5},{2,6},{3,7},{4,0},{5,1},{6,2},{7,3},{8,12},{9,13},{10,... | collective-permute-start | bytes 1544 | tf_op jit(solution)/shard_map/ppermute | solution.py:62
  95.8 11.5 %collective-permute-start.5 = (f32[3,128,256]{2,1,0:T(8,128)}, f32[3,128,256]{2,1,0:T(8,128)S(1)}, u32[]{:S(2)}, u32[]{:S(2)}) collective-permute-start(f32[3,128,256]{2,1,0:T(8,128)} %copy-done), channel_id=1, source_target_pairs={{0,48},{1,49},{2,50},{3,51},{4,52},{5,53},{6,54},{7,55},{8,56},{9,... | collective-permute-start | bytes 1179656 | tf_op jit(solution)/shard_map/ppermute | solution.py:62
  96.0 13.0 %collective-permute-start.6 = (f32[3,128,256]{2,1,0:T(8,128)S(1)}, f32[3,128,256]{2,1,0:T(8,128)S(1)}, u32[]{:S(2)}, u32[]{:S(2)}) collective-permute-start(f32[3,128,256]{2,1,0:T(8,128)S(1)} %get-tuple-element.16.refs_5_), channel_id=1, source_target_pairs={{0,16},{1,17},{2,18},{3,19},{4,20},{5,21},{6,22},{7,23},{8,24},{9,... | collective-permute-start | bytes 1179656 | tf_op jit(solution)/shard_map/ppermute | solution.py:62
  97.9 13.6 %collective-permute-start.8 = (f32[3,128,256]{2,1,0:T(8,128)}, f32[3,128,256]{2,1,0:T(8,128)S(1)}, u32[]{:S(2)}, u32[]{:S(2)}) collective-permute-start(f32[3,128,256]{2,1,0:T(8,128)} %get-tuple-element.24), channel_id=1, source_target_pairs={{0,48},{1,49},{2,50},{3,51},{4,52},{5,53},{6,54},{7,55},{8,56},{9,... | collective-permute-start | bytes 1179656 | tf_op jit(solution)/shard_map/ppermute | solution.py:62
  100.0 13.5 %collective-permute-start.4 = (f32[3,128,256]{2,1,0:T(8,128)}, f32[3,128,256]{2,1,0:T(8,128)S(1)}, u32[]{:S(2)}, u32[]{:S(2)}) collective-permute-start(f32[3,128,256]{2,1,0:T(8,128)} %get-tuple-element.26), channel_id=1, source_target_pairs={{0,16},{1,17},{2,18},{3,19},{4,20},{5,21},{6,22},{7,23},{8,24},{9,... | collective-permute-start | bytes 1179656 | tf_op jit(solution)/shard_map/ppermute | solution.py:62
